TPU v7x, 32 devices: a whole 2x2x4 slice. The times are simulated.
32 devices in a mesh: dp: 4 (over z), ctx: 8 (over y, x, core).
Axes of the slice: x: 2, y: 2, z: 4, core: 2. Of those that a mesh axis runs over, the one named last changes fastest.
Arguments:
- queries: bfloat16 [4, 1024, 2048], P('dp', 'ctx'), may hold values from -6 to 6
- keys: bfloat16 [4, 1024, 2048], P('dp', 'ctx'), may hold values from -6 to 6
- values: bfloat16 [4, 1024, 2048], P('dp', 'ctx'), may hold values from -6 to 6
- prior_state: float32 [4, 16, 128, 128], P('dp'), may hold values from -96 to 96
- norm_gain: float32 [2048], replicated, may hold values from 0.1 to 1.9
- router_weight: bfloat16 [2048, 32], replicated, may hold values from -0.125 to 0.125
- expert_ids: int32 [4, 1024, 4], P('dp', 'ctx'), may hold values from 0 to 31, all different within a row; in each aligned block of 128 rows (0 to 127, 128 to 255, ..., all dimensions but the last counted through in order) at most 24 rows name the same one
- w_gate: bfloat16 [32, 2048, 768], P(('dp', 'ctx')), may hold values from -0.125 to 0.125
- w_up: bfloat16 [32, 2048, 768], P(('dp', 'ctx')), may hold values from -0.125 to 0.125
- w_down: bfloat16 [32, 768, 2048], P(('dp', 'ctx')), may hold values from -0.21875 to 0.21875
- cotangent: bfloat16 [4, 1024, 2048], P('dp', 'ctx'), may hold values from -6 to 6
Outputs:
- output: bfloat16 [4, 1024, 2048], P('dp', 'ctx')
- grad_queries: bfloat16 [4, 1024, 2048], P('dp', 'ctx')
- grad_keys: bfloat16 [4, 1024, 2048], P('dp', 'ctx')
- grad_values: bfloat16 [4, 1024, 2048], P('dp', 'ctx')
- grad_gate: bfloat16 [32, 2048, 768], P(('dp', 'ctx'))
- grad_up: bfloat16 [32, 2048, 768], P(('dp', 'ctx'))
- grad_down: bfloat16 [32, 768, 2048], P(('dp', 'ctx'))
- grad_router: float32 [2048, 32], replicated
Inputs may be any that keep to these rules, and one draw needn't show every extreme that they name: `expert_ids`: within the rows of one device (aligned blocks of 128 tokens) no expert is named more than 24 times, and in every draw some expert is named exactly 24 times there; the 4 ids of one token differ.
All inputs are finite; a program needn't handle non-finite values.
Results may differ from a plain program's by a relative error of at most 0.012.
Values may be sent and summed in bfloat16 or wider, within the bound.
No kernel may reach another device: no remote copies, remote signals or barrier semaphores. Data moves between devices by JAX's collectives and lax.ppermute only.
A program may use at most 192 MiB of HBM per device.

v0:
```python
import jax
import jax.numpy as jnp
from jax import lax
from jax.sharding import PartitionSpec as P

H = 16
DH = 128
D = 2048
TOPK = 4


epsilon = 1e-05
exact_mode = lax.Precision.HIGHEST


def carried_in(value, axis, join, neutral):
    count, mine = (lax.axis_size(axis), lax.axis_index(axis))
    pieces = lax.all_gather(value, axis)
    total = jnp.full_like(value, 0) + jnp.asarray(neutral, value.dtype)

    def step(position, total):
        longer = join(total, pieces[position])
        return jnp.where(position < mine, longer, total)

    return lax.fori_loop(0, count - 1, step, total)


def entering(value, axis, join, neutral):
    count = lax.axis_size(axis)
    place = lax.axis_index(axis)
    ahead = count - 1 - place
    gathered = lax.all_gather(value.astype(jnp.bfloat16), axis)
    state = jnp.zeros_like(value) + jnp.asarray(neutral, value.dtype)

    def one(step, state):
        source = count - 1 - step
        return join(state, lax.dynamic_index_in_dim(gathered, source, 0, False).astype(value.dtype))

    return lax.fori_loop(0, ahead, one, state)


def add_states(earlier, later):
    return earlier + later


def expert_forward(inputs, gate_mat, up_mat, down_mat):
    gate_pre = jnp.dot(inputs, gate_mat, preferred_element_type=jnp.float32)
    up_pre = jnp.dot(inputs, up_mat, preferred_element_type=jnp.float32)
    gate_sig = jax.nn.sigmoid(gate_pre)
    hidden = (gate_pre * gate_sig * up_pre).astype(jnp.bfloat16)
    produced = jnp.dot(hidden, down_mat, preferred_element_type=jnp.float32).astype(jnp.bfloat16)
    return (gate_pre, up_pre, gate_sig, hidden, produced)


def expert_backward(
    inputs, grad_out, gate_pre, up_pre, gate_sig, hidden, gate_mat, up_mat, down_mat
):
    grad_hidden = jnp.dot(grad_out, down_mat.T, preferred_element_type=jnp.float32)
    grad_gate_pre = (grad_hidden * up_pre * gate_sig * (1.0 + gate_pre * (1.0 - gate_sig))).astype(
        jnp.bfloat16
    )
    grad_up_pre = (grad_hidden * gate_pre * gate_sig).astype(jnp.bfloat16)
    grad_down = jnp.dot(hidden.T, grad_out, preferred_element_type=jnp.float32).astype(jnp.bfloat16)
    grad_gate = jnp.dot(inputs.T, grad_gate_pre, preferred_element_type=jnp.float32).astype(
        jnp.bfloat16
    )
    grad_up = jnp.dot(inputs.T, grad_up_pre, preferred_element_type=jnp.float32).astype(
        jnp.bfloat16
    )
    grad_inputs = (
        jnp.dot(grad_gate_pre, gate_mat.T, preferred_element_type=jnp.float32)
        + jnp.dot(grad_up_pre, up_mat.T, preferred_element_type=jnp.float32)
    ).astype(jnp.bfloat16)
    return (grad_inputs, grad_gate, grad_up, grad_down)


def slot_layout(flat_ids, experts_all, capacity):
    count_assign = flat_ids.shape[0]
    onehot = (flat_ids[:, None] == jnp.arange(experts_all, dtype=jnp.int32)[None, :]).astype(
        jnp.int32
    )
    before = jnp.cumsum(onehot, axis=0) - onehot
    slot_rank = jnp.sum(before * onehot, axis=1)
    slot_index = flat_ids * capacity + slot_rank
    source = (
        jnp.full((experts_all * capacity,), -1, jnp.int32)
        .at[slot_index]
        .set(jnp.arange(count_assign, dtype=jnp.int32))
    )
    return (slot_index, source)


def route_rows(block):
    return lax.all_to_all(block, ("dp", "ctx"), split_axis=0, concat_axis=0, tiled=True)


def local(
    queries,
    keys,
    values,
    prior_state,
    norm_gain,
    router_weight,
    expert_ids,
    w_gate,
    w_up,
    w_down,
    cotangent,
):
    token_count = queries.shape[1]
    experts_all = router_weight.shape[1]
    capacity = max(2, 3 * token_count * TOPK // (2 * experts_all))
    queries3 = queries[0].reshape(token_count, H, DH)
    keys3 = keys[0].reshape(token_count, H, DH)
    values3 = values[0].reshape(token_count, H, DH)
    state_term = jnp.einsum("shi,shj->hij", keys3, values3, preferred_element_type=jnp.float32)
    zero_state = jnp.zeros_like(state_term)
    earlier_states = carried_in(state_term, "ctx", add_states, zero_state)
    state_in = prior_state[0] + earlier_states
    causal = jnp.arange(token_count)[:, None] >= jnp.arange(token_count)[None, :]
    scores = jnp.einsum("thd,shd->hts", queries3, keys3, preferred_element_type=jnp.float32)
    attn_scores = jnp.where(causal[None], scores, 0.0).astype(jnp.bfloat16)
    intra = jnp.einsum("hts,shj->thj", attn_scores, values3, preferred_element_type=jnp.float32)
    inter = jnp.einsum("thi,hij->thj", queries3.astype(jnp.float32), state_in, precision=exact_mode)
    attended = intra + inter
    gain_heads = norm_gain.reshape(H, DH)
    mean_square = jnp.mean(attended * attended, axis=-1, keepdims=True)
    scale_root = jnp.sqrt(mean_square + epsilon)
    mixed_rows = (attended / scale_root * gain_heads).astype(jnp.bfloat16).reshape(token_count, D)
    logits = jnp.dot(mixed_rows, router_weight, preferred_element_type=jnp.float32)
    token_ids = expert_ids[0]
    onehot_sel = (
        token_ids[:, :, None] == jnp.arange(experts_all, dtype=jnp.int32)[None, None, :]
    ).astype(jnp.float32)
    selected = jnp.sum(logits[:, None, :] * onehot_sel, axis=-1)
    gate_sig_r = jax.nn.sigmoid(selected)
    sig_total = jnp.sum(gate_sig_r, axis=1, keepdims=True)
    gates = gate_sig_r / sig_total
    slot_index, source = slot_layout(token_ids.reshape(-1), experts_all, capacity)
    filled = source >= 0
    row_of = jnp.where(filled, source // TOPK, 0)
    send_block = jnp.where(
        filled[:, None], mixed_rows[row_of], jnp.zeros((), jnp.bfloat16)
    ).reshape(experts_all, capacity, D)
    grad_y = cotangent[0].astype(jnp.float32)
    grad_out_assign = (
        (gates[:, :, None] * grad_y[:, None, :]).astype(jnp.bfloat16).reshape(token_count * TOPK, D)
    )
    send_grad = jnp.where(
        filled[:, None], grad_out_assign[jnp.where(filled, source, 0)], jnp.zeros((), jnp.bfloat16)
    ).reshape(experts_all, capacity, D)
    gate_mat = w_gate[0]
    up_mat = w_up[0]
    down_mat = w_down[0]
    received = route_rows(send_block).reshape(-1, D)
    gate_pre, up_pre, gate_sig, hidden, produced = expert_forward(
        received, gate_mat, up_mat, down_mat
    )
    returned = route_rows(produced.reshape(experts_all, capacity, D)).reshape(-1, D)
    received_grad = route_rows(send_grad).reshape(-1, D)
    grad_inputs, grad_gate, grad_up, grad_down = expert_backward(
        received, received_grad, gate_pre, up_pre, gate_sig, hidden, gate_mat, up_mat, down_mat
    )
    returned_grad = route_rows(grad_inputs.reshape(experts_all, capacity, D)).reshape(-1, D)
    out_float = returned[slot_index].reshape(token_count, TOPK, D).astype(jnp.float32)
    moe_sum = jnp.sum(gates[:, :, None] * out_float, axis=1)
    output = (mixed_rows.astype(jnp.float32) + moe_sum).astype(jnp.bfloat16)
    grad_gates = jnp.sum(out_float * grad_y[:, None, :], axis=-1)
    grad_assign = returned_grad[slot_index].reshape(token_count, TOPK, D).astype(jnp.float32)
    grad_moe = jnp.sum(gates[:, :, None] * grad_assign, axis=1)
    weighted_sum = jnp.sum(gates * grad_gates, axis=1, keepdims=True)
    grad_selected = gate_sig_r * (1.0 - gate_sig_r) * (grad_gates - weighted_sum) / sig_total
    grad_logits = jnp.sum(grad_selected[:, :, None] * onehot_sel, axis=1)
    router_term = jnp.dot(mixed_rows.astype(jnp.float32).T, grad_logits, precision=exact_mode)
    grad_router = lax.psum(router_term, ("dp", "ctx"))
    router_back = jnp.dot(grad_logits, router_weight.astype(jnp.float32).T, precision=exact_mode)
    grad_mixed = grad_y + grad_moe + router_back
    weighted = gain_heads * grad_mixed.reshape(token_count, H, DH)
    inner = jnp.sum(weighted * attended, axis=-1, keepdims=True)
    grad_attended = (
        (weighted - attended * (inner / (DH * (mean_square + epsilon)))) / scale_root
    ).astype(jnp.bfloat16)
    grad_term = jnp.einsum(
        "thi,thj->hij", queries3, grad_attended, preferred_element_type=jnp.float32
    )
    later_states = entering(grad_term, "ctx", add_states, zero_state)
    grad_scores = jnp.where(
        causal[None],
        jnp.einsum("thj,shj->hts", grad_attended, values3, preferred_element_type=jnp.float32),
        0.0,
    ).astype(jnp.bfloat16)
    grad_q = jnp.einsum(
        "hts,shi->thi", grad_scores, keys3, preferred_element_type=jnp.float32
    ) + jnp.einsum(
        "thj,hij->thi", grad_attended.astype(jnp.float32), state_in, precision=exact_mode
    )
    grad_k = jnp.einsum(
        "hts,thi->shi", grad_scores, queries3, preferred_element_type=jnp.float32
    ) + jnp.einsum("shj,hij->shi", values3.astype(jnp.float32), later_states, precision=exact_mode)
    grad_v = jnp.einsum(
        "hts,thj->shj", attn_scores, grad_attended, preferred_element_type=jnp.float32
    ) + jnp.einsum("shi,hij->shj", keys3.astype(jnp.float32), later_states, precision=exact_mode)
    row_shape = (1, token_count, D)
    return (
        output.reshape(row_shape),
        grad_q.astype(jnp.bfloat16).reshape(row_shape),
        grad_k.astype(jnp.bfloat16).reshape(row_shape),
        grad_v.astype(jnp.bfloat16).reshape(row_shape),
        grad_gate[None],
        grad_up[None],
        grad_down[None],
        grad_router,
    )


def solution(mesh):
    placed = (
        P("dp", "ctx", None),
        P("dp", "ctx", None),
        P("dp", "ctx", None),
        P("dp", None, None, None),
        P(),
        P(),
        P("dp", "ctx", None),
        P(("dp", "ctx"), None, None),
        P(("dp", "ctx"), None, None),
        P(("dp", "ctx"), None, None),
        P("dp", "ctx", None),
    )
    return jax.shard_map(
        local,
        mesh=mesh,
        in_specs=placed,
        out_specs=(
            P("dp", "ctx", None),
            P("dp", "ctx", None),
            P("dp", "ctx", None),
            P("dp", "ctx", None),
            P(("dp", "ctx"), None, None),
            P(("dp", "ctx"), None, None),
            P(("dp", "ctx"), None, None),
            P(),
        ),
        check_vma=False,
    )
```

profile of v0, /device:TPU:0, one launch (start us, length us, event | category | flops | bytes accessed | tf_op | source)
XLA Modules:
  0.0 655.7 jit_solution(7271364659372480334)
XLA Ops:
  20.3 3.1 mul.169
  23.4 5.5 mul.170
  33.3 2.5 fusion.17
  35.8 37.3 %all-gather.5.cloned.1.call-done = f32[128,128,128]{2,1,0:T(8,128)} async-done(((f32[16,128,128]{2,1,0:T(8,128)}), f32[128,128,128]{2,1,0:T(8,128)}) %all-gather.5.cloned.1.call-update) | async-done | bytes 8388624 | tf_op jit(solution)/shard_map/all_gather | solution.py:18
  73.1 18.7 %while.27 = (s32[]{:T(128)}, f32[16,128,128]{2,1,0:T(8,128)}, s32[]{:T(128)}, f32[8,16,128,128]{3,2,1,0:T(8,128)}, s32[]{:T(128)}, /*index=5*/s32[]{:T(128)}) while((s32[]{:T(128)}, f32[16,128,128]{2,1,0:T(8,128)}, s32[]{:T(128)}, f32[8,16,128,128]{3,2,1,0:T(8,128)}, s32[]{:T(128)}, /*index=5*/s32[]{:T(128)}) %tuple.85), condition=%wide.region_1.2_spmd.clone, body=%wide.region_0.1_spmd.clone.sunk | while | flops 786436 | bytes 3145821 | solution.py:25
  75.5 2.7 add_select_fusion.3
  78.2 2.7 add_select_fusion.3
  81.0 2.7 add_select_fusion.3
  83.7 2.7 add_select_fusion.3
  86.4 2.7 add_select_fusion.3
  89.1 2.7 add_select_fusion.3
  91.8 2.8 convolution_bitcast_fusion.5
  100.9 3.8 multiply_convert_fusion
  104.7 8.9 %gather_fusion.2 = bf16[768,2048]{1,0:T(8,128)(2,1)} fusion(bf16[512,2048]{1,0:T(8,128)(2,1)} %multiply_convert_fusion, s32[1024]{0:T(1024)S(1)} %get-tuple-element.236), kind=kCustom, calls=%fused_computation.2 | custom fusion | bytes 6294528 | tf_op jit(solution)/shard_map/gather | solution.py:150
  113.6 8.2 %gather_fusion = bf16[768,2048]{1,0:T(8,128)(2,1)} fusion(bf16[128,2048]{1,0:T(8,128)(2,1)} %copy.143, s32[1024]{0:T(1024)S(1)} %get-tuple-element.237), kind=kCustom, calls=%fused_computation | custom fusion | bytes 6294528 | tf_op jit(solution)/shard_map/gather | solution.py:143
  121.8 4.3 broadcast_select_fusion
  126.1 75.8 %all_to_all.20 = bf16[32,24,2048]{2,1,0:T(8,128)(2,1)} all-to-all(bf16[32,24,2048]{2,1,0:T(8,128)(2,1)S(1)} %get-tuple-element.231), channel_id=1, replica_groups=mesh['dp'=4,'ctx'=8] {'dp','ctx'}, dimensions={0} | all-to-all | bytes 6291456 | tf_op jit(solution)/shard_map/all_to_all | solution.py:94
  201.9 3.8 all-to-all-start.2
  205.7 7.0 %fusion.4 = f32[768,768]{1,0:T(8,128)} fusion(bf16[768,2048]{1,0:T(8,128)(2,1)} %bitcast.170, bf16[1,2048,768]{2,1,0:T(8,128)(2,1)} %param.23), kind=kOutput, calls=%fused_computation.20 | convolution fusion | flops 2415919104 | bytes 8650752 | tf_op jit(solution)/shard_map/dot_general | solution.py:48
  212.7 4.0 fusion.8
  216.8 60.4 %all-to-all-done.2 = bf16[32,24,2048]{2,1,0:T(8,128)(2,1)} async-done(((bf16[32,24,2048]{2,1,0:T(8,128)(2,1)}), bf16[32,24,2048]{2,1,0:T(8,128)(2,1)}, u32[]{:S(2)}, u32[]{:S(2)}) %all-to-all-start.2) | async-done | bytes 3145760 | tf_op jit(solution)/shard_map/all_to_all | solution.py:94
  277.2 7.9 %multiply_convert_fusion.1 = (bf16[768,768]{1,0:T(8,128)(2,1)S(1)}, bf16[768,768]{1,0:T(8,128)(2,1)S(1)}, bf16[768,768]{1,0:T(8,128)(2,1)}) fusion(f32[768,768]{1,0:T(8,128)} %fusion.8, f32[768,768]{1,0:T(8,128)} %fusion.4, bf16[768,2048]{1,0:T(8,128)(2,1)} %bitcast.23, bf16[1,768,2048]{2,1,0:T(8,128)(2,1)S(1)} %copy-done), kind=kOutput, calls=%fused_computation.32 | convolution fusion | flops 2425356288 | bytes 14548992 | tf_op jit(solution)/shard_map/dot_general | solution.py:58
  285.1 2.6 fusion.6
  287.8 4.0 add_convert_fusion
  291.8 4.0 all-to-all-start.3
  295.8 5.2 convolution_convert_fusion.3
  301.1 66.2 %all-to-all-done.3 = bf16[32,24,2048]{2,1,0:T(8,128)(2,1)} async-done(((bf16[32,24,2048]{2,1,0:T(8,128)(2,1)}), bf16[32,24,2048]{2,1,0:T(8,128)(2,1)}, u32[]{:S(2)}, u32[]{:S(2)}) %all-to-all-start.3) | async-done | bytes 3145760 | tf_op jit(solution)/shard_map/all_to_all | solution.py:94
  367.3 4.0 all-to-all-start.1
  371.6 7.5 %gather_fusion.3 = bf16[512,2048]{1,0:T(8,128)(2,1)} fusion(bf16[768,2048]{1,0:T(8,128)(2,1)} %bitcast.25, s32[1024]{0:T(1024)S(1)} %pad_clamp_fusion.1), kind=kCustom, calls=%fused_computation.3 | custom fusion | bytes 4196352 | tf_op jit(solution)/shard_map/gather | solution.py:169
  379.1 4.7 reshape.283
  383.9 58.9 %all-to-all-done.1 = bf16[32,24,2048]{2,1,0:T(8,128)(2,1)} async-done(((bf16[32,24,2048]{2,1,0:T(8,128)(2,1)}), bf16[32,24,2048]{2,1,0:T(8,128)(2,1)}, u32[]{:S(2)}, u32[]{:S(2)}) %all-to-all-start.1) | async-done | bytes 3145760 | tf_op jit(solution)/shard_map/all_to_all | solution.py:94
  442.8 7.5 %gather_fusion.1 = bf16[512,2048]{1,0:T(8,128)(2,1)} fusion(bf16[768,2048]{1,0:T(8,128)(2,1)} %bitcast.18, s32[1024]{0:T(1024)S(1)} %pad_clamp_fusion.1), kind=kCustom, calls=%fused_computation.1 | custom fusion | bytes 4196352 | tf_op jit(solution)/shard_map/gather | solution.py:165
  450.3 4.7 reshape.279
  455.1 11.2 %multiply_reduce_fusion = (f32[128,4]{1,0:T(8,128)S(1)}, f32[128,2048]{1,0:T(8,128)}, f32[128,2048]{1,0:T(8,128)}) fusion(f32[128,4,2048]{2,1,0:T(4,128)} %reshape.279, f32[128,2048]{1,0:T(8,128)} %copy-done.4, f32[128,4]{1,0:T(8,128)S(1)} %copy.138, f32[128,4,2048]{2,1,0:T(4,128)} %reshape.283), kind=kLoop, calls=%fused_computation.8 | loop fusion | flops 5766656 | bytes 11538432 | tf_op jit(solution)/shard_map/reduce_sum | solution.py:168
  466.4 3.0 convolution_add_fusion
  469.4 2.5 copy.148
  482.1 2.5 copy.144
  484.6 7.0 %fusion.10 = bf16[1,2048,768]{2,1,0:T(8,128)(2,1)} fusion(bf16[768,2048]{1,0:T(8,128)(2,1)} %bitcast.171, bf16[768,768]{1,0:T(8,128)(2,1)} %copy-done.26), kind=kOutput, calls=%fused_computation.28 | convolution fusion | flops 2417491968 | bytes 7471104 | tf_op jit(solution)/shard_map/dot_general | solution.py:64
  491.7 4.1 fusion.11
  495.8 6.1 fusion.12
  517.0 17.3 %while.26 = (s32[]{:T(128)}, f32[16,128,128]{2,1,0:T(8,128)}, s32[]{:T(128)}, bf16[8,16,128,128]{3,2,1,0:T(8,128)(2,1)}, s32[]{:T(128)}, /*index=5*/s32[]{:T(128)}, s32[]{:T(128)}, s32[]{:T(128)}) while((s32[]{:T(128)}, f32[16,128,128]{2,1,0:T(8,128)}, s32[]{:T(128)}, bf16[8,16,128,128]{3,2,1,0:T(8,128)(2,1)}, s32[]{:T(128)}, ...), condition=%wide.region_16.17_spmd, body=%wide.region_15.16_spmd.sunk | while | flops 524294 | bytes 2621575 | solution.py:39
  517.0 2.5 convert_add_fusion.2
  519.5 2.5 convert_add_fusion.2
  526.9 2.5 convert_add_fusion.2
  531.9 2.5 convert_add_fusion.2
  534.4 2.7 convolution_bitcast_fusion.3
  537.1 2.9 fusion.16
  545.2 101.8 %all-reduce.2.cloned.1.call-done = f32[2048,32]{0,1:T(8,128)} async-done(((f32[2048,32]{0,1:T(8,128)}), f32[2048,32]{0,1:T(8,128)}) %all-reduce.2.cloned.1.call-update) | async-done | bytes 262160 | tf_op jit(solution)/shard_map/psum | solution.py:175
  (131 shorter events, 66.2 us)
Async XLA Ops:
  7.2 270.0 %copy-start = (bf16[1,768,2048]{2,1,0:T(8,128)(2,1)S(1)}, bf16[1,768,2048]{2,1,0:T(8,128)(2,1)}, u32[]{:S(2)}) copy-start(bf16[1,768,2048]{2,1,0:T(8,128)(2,1)} %param.24) | copy-start | bytes 9437188
  7.2 65.9 %all-gather.5.cloned.1.call-start = ((), (), s32[]{:S(2)}) async-start(), calls=%async_computation.5 | async-start | bytes 9437184 | tf_op jit(solution)/shard_map/all_gather | solution.py:18
  7.2 8.7 %copy-start.22 = (s32[1,128,4]{1,2,0:T(4,128)S(1)}, s32[1,128,4]{1,2,0:T(4,128)}, u32[]{:S(2)}) copy-start(s32[1,128,4]{1,2,0:T(4,128)} %param.21) | copy-start | bytes 6148
  12.7 0.8 copy-start.9
  19.3 1.0 copy-start.4
  91.8 2.8 copy-start.10
  91.8 2.8 copy-start.19
  91.8 4.3 copy-start.21
  94.6 4.7 copy-start.20
  95.2 1.0 copy-start.3
  201.9 75.2 %all-to-all-start.2 = ((bf16[32,24,2048]{2,1,0:T(8,128)(2,1)}), bf16[32,24,2048]{2,1,0:T(8,128)(2,1)}, u32[]{:S(2)}, u32[]{:S(2)}) async-start(bf16[32,24,2048]{2,1,0:T(8,128)(2,1)} %get-tuple-element.230), calls=%async_computation.2 | async-start | bytes 6291456 | tf_op jit(solution)/shard_map/all_to_all | solution.py:94
  205.7 7.0 %copy-start.15 = (bf16[32,24,2048]{2,1,0:T(8,128)(2,1)S(1)}, bf16[32,24,2048]{2,1,0:T(8,128)(2,1)}, u32[]{:S(2)}) copy-start(bf16[32,24,2048]{2,1,0:T(8,128)(2,1)} %all_to_all.20) | copy-start | bytes 9437188
  205.7 7.0 %copy-start.23 = (bf16[1,2048,768]{2,1,0:T(8,128)(2,1)S(1)}, bf16[1,2048,768]{2,1,0:T(8,128)(2,1)}, u32[]{:S(2)}) copy-start(bf16[1,2048,768]{2,1,0:T(8,128)(2,1)} %param.22) | copy-start | bytes 9437188
  277.2 7.9 %copy-start.24 = (bf16[1,2048,768]{2,1,0:T(8,128)(2,1)S(1)}, bf16[1,2048,768]{2,1,0:T(8,128)(2,1)}, u32[]{:S(2)}) copy-start(bf16[1,2048,768]{2,1,0:T(8,128)(2,1)} %param.22) | copy-start | bytes 9437188
  285.1 2.7 copy-start.26
  285.1 2.7 copy-start.28
  285.1 2.7 copy-start.25
  291.8 75.5 %all-to-all-start.3 = ((bf16[32,24,2048]{2,1,0:T(8,128)(2,1)}), bf16[32,24,2048]{2,1,0:T(8,128)(2,1)}, u32[]{:S(2)}, u32[]{:S(2)}) async-start(bf16[32,24,2048]{2,1,0:T(8,128)(2,1)} %bitcast.175), calls=%async_computation.3 | async-start | bytes 6291456 | tf_op jit(solution)/shard_map/all_to_all | solution.py:94
  367.3 75.5 %all-to-all-start.1 = ((bf16[32,24,2048]{2,1,0:T(8,128)(2,1)}), bf16[32,24,2048]{2,1,0:T(8,128)(2,1)}, u32[]{:S(2)}, u32[]{:S(2)}) async-start(bf16[32,24,2048]{2,1,0:T(8,128)(2,1)} %bitcast.174), calls=%async_computation.1 | async-start | bytes 6291456 | tf_op jit(solution)/shard_map/all_to_all | solution.py:94
  371.3 144.6 %all-gather.7.cloned.1.call-start = ((), (), s32[]{:S(2)}) async-start(), calls=%async_computation.6 | async-start | bytes 4718592 | tf_op jit(solution)/shard_map/all_gather | solution.py:32
  471.9 4.7 copy-start.5
  475.8 0.8 copy-start.7
  479.7 167.3 %all-reduce.2.cloned.1.call-start = ((), (), s32[]{:S(2)}) async-start(), calls=%async_computation.4 | async-start | bytes 524288 | tf_op jit(solution)/shard_map/psum | solution.py:175
  484.6 7.0 %copy-start.16 = (bf16[32,24,2048]{2,1,0:T(8,128)(2,1)S(1)}, bf16[32,24,2048]{2,1,0:T(8,128)(2,1)}, u32[]{:S(2)}) copy-start(bf16[32,24,2048]{2,1,0:T(8,128)(2,1)} %all_to_all.20) | copy-start | bytes 9437188
  484.6 7.0 %copy-start.29 = (bf16[768,768]{1,0:T(8,128)(2,1)S(1)}, bf16[768,768]{1,0:T(8,128)(2,1)}, u32[]{:S(2)}) copy-start(bf16[768,768]{1,0:T(8,128)(2,1)} %copy-done.28) | copy-start | bytes 3538948
  491.7 4.1 copy-start.27
  495.7 6.1 copy-start.8
  495.8 6.1 copy-start.11
  495.8 6.6 %copy-start.2 = (f32[16,128,128]{2,1,0:T(8,128)S(1)}, f32[16,128,128]{2,1,0:T(8,128)}, u32[]{:S(2)}) copy-start(f32[16,128,128]{2,1,0:T(8,128)} %get-tuple-element.143) | copy-start | bytes 3145732
  495.8 6.6 %copy-start.13 = (f32[1,16,128,128]{3,2,1,0:T(8,128)S(1)}, f32[1,16,128,128]{3,2,1,0:T(8,128)}, u32[]{:S(2)}) copy-start(f32[1,16,128,128]{3,2,1,0:T(8,128)} %param.18) | copy-start | bytes 3145732
  501.9 1.2 copy-start.12
  502.4 2.0 copy-start.17
  534.4 2.7 copy-start.1
  534.4 2.7 copy-start.14
  534.4 5.6 copy-start.6
  534.4 5.6 copy-start.18
Sparse Core Ops, SparseCore 0:
  16.0 57.0 all-gather.4
  479.8 36.0 all-gather.6
  522.0 124.9 all-reduce.1
where the time goes:
time: 666 us; the launch traced here: 656 us
  waiting for transfers between devices  327 us (49%)
  local copies, waits for them, and re-layouts  83.1 us (12%)
  blocking collectives  75.8 us (11%)
  matrix products  75.3 us (11%)
  other arithmetic  67.4 us (10%)
  between operations  14.6 us (2%)
  starting transfers between devices  12.5 us (2%)
    all_to_all x3, waiting for transfers between devices, route_rows(): lax.all_to_all(block, ('dp', 'ctx'), split_axis=0, concat_axis=0, tiled=T...  186 us
    psum x1, waiting for transfers between devices, local(): grad_router = lax.psum(router_term, ('dp', 'ctx'))  102 us
    all_to_all x1, blocking collectives, route_rows(): lax.all_to_all(block, ('dp', 'ctx'), split_axis=0, concat_axis=0, tiled=T...  75.8 us
    all_gather x1, waiting for transfers between devices, carried_in(): pieces = lax.all_gather(value, axis)  37.3 us
    select_n x7, other arithmetic, step(): return jnp.where(position < mine, longer, total)  18.7 us
    add x7, other arithmetic, add_states(): return earlier + later  17.3 us
    unnamed x68, local copies, waits for them, and re-layouts  16.8 us
  transfers between devices with their start and end apart: 6, of which 6 were waited for; matrix products, arithmetic and copies ran while one was open for 17% of the time, Pallas kernels for 0%

commit v1 on v0

v1 whole, which is shorter than its diff:
```python
import functools

import jax
import jax.numpy as jnp
from jax import lax
from jax.experimental import pallas as pl
from jax.experimental.pallas import tpu as pltpu
from jax.sharding import PartitionSpec as P

H = 16
DH = 128
D = 2048
TOPK = 4
HB = 4
WIDTH = HB * DH
EPS = 1e-05
ALL = ("dp", "ctx")
F32 = jnp.float32
BF16 = jnp.bfloat16
LIMIT = 48 << 20


def mm(a, b):
    return jnp.dot(a, b, preferred_element_type=F32)


def mm_tn(a, b):
    return lax.dot_general(a, b, (((0,), (0,)), ((), ())), preferred_element_type=F32)


def mm_nt(a, b):
    return lax.dot_general(a, b, (((1,), (1,)), ((), ())), preferred_element_type=F32)


def halves(x):
    high = x.astype(BF16)
    return high, (x - high.astype(F32)).astype(BF16)


def thirds(x):
    high, rest = x.astype(BF16), None
    rest = x - high.astype(F32)
    middle = rest.astype(BF16)
    return high, middle, (rest - middle.astype(F32)).astype(BF16)


def causal_mask(n):
    return lax.broadcasted_iota(jnp.int32, (n, n), 0) >= lax.broadcasted_iota(jnp.int32, (n, n), 1)


def head(h):
    return slice(h * DH, (h + 1) * DH)


def call(kernel, out_shape, grid, in_specs, out_specs, scratch=(), flops=0, moved=0):
    return pl.pallas_call(
        kernel,
        out_shape=out_shape,
        grid=grid,
        in_specs=in_specs,
        out_specs=out_specs,
        scratch_shapes=scratch,
        compiler_params=pltpu.CompilerParams(vmem_limit_bytes=LIMIT),
        cost_estimate=pl.CostEstimate(flops=flops, bytes_accessed=moved, transcendentals=0),
    )


def whole(shape):
    return pl.BlockSpec(shape, lambda *_: (0,) * len(shape))


def columns(rows, width=WIDTH):
    return pl.BlockSpec((rows, width), lambda i: (0, i))


def per_head(n=HB):
    return pl.BlockSpec((n, DH, DH), lambda i: (i, 0, 0))


def route_kernel(cap, ids_ref, dy_ref, pick_ref, chosen_ref, mask_ref, send_ref):
    tokens, top = ids_ref.shape
    experts = chosen_ref.shape[1]
    rows = pick_ref.shape[0]
    lane = lax.broadcasted_iota(jnp.int32, (tokens, experts), 1)
    chosen = jnp.zeros((tokens, experts), F32)
    for j in range(top):
        chosen += (ids_ref[:, j : j + 1] == lane).astype(F32)
    count = mm(causal_mask(tokens).astype(F32).astype(BF16), chosen.astype(BF16))
    place = (chosen * count).astype(BF16)
    row = lax.broadcasted_iota(jnp.int32, (rows, experts), 0)
    first = lax.broadcasted_iota(jnp.int32, (rows, experts), 1) * cap
    owns = (row >= first) & (row < first + cap)
    wanted = jnp.sum(jnp.where(owns, row - first + 1, 0), axis=1, keepdims=True).astype(F32)
    found = mm_nt(owns.astype(F32).astype(BF16), place)
    pick = (found == wanted).astype(F32).astype(BF16)
    pick_ref[...] = pick
    chosen_ref[...] = chosen
    mask_ref[...] = mm(pick, chosen.astype(BF16)).astype(BF16)
    for c in range(D // WIDTH):
        at = slice(c * WIDTH, (c + 1) * WIDTH)
        send_ref[:, at] = mm(pick, dy_ref[:, at]).astype(BF16)


def route(ids, dy, experts, cap):
    tokens, rows = ids.shape[0], experts * cap
    return call(
        functools.partial(route_kernel, cap),
        (
            jax.ShapeDtypeStruct((rows, tokens), BF16),
            jax.ShapeDtypeStruct((tokens, experts), F32),
            jax.ShapeDtypeStruct((rows, experts), BF16),
            jax.ShapeDtypeStruct((rows, D), BF16),
        ),
        (1,),
        [whole(ids.shape), whole(dy.shape)],
        (
            whole((rows, tokens)),
            whole((tokens, experts)),
            whole((rows, experts)),
            whole((rows, D)),
        ),
        flops=2 * rows * tokens * D,
        moved=2 * rows * D,
    )(ids, dy)


def state_kernel(k_ref, v_ref, out_ref):
    for h in range(HB):
        out_ref[h] = mm_tn(k_ref[:, head(h)], v_ref[:, head(h)]).astype(BF16)


def state_terms(k, v):
    tokens = k.shape[0]
    return call(
        state_kernel,
        jax.ShapeDtypeStruct((H, DH, DH), BF16),
        (H // HB,),
        [columns(tokens), columns(tokens)],
        per_head(),
        flops=2 * tokens * D * DH,
        moved=6 * tokens * D,
    )(k, v)


def running_kernel(backwards, in_ref, out_ref):
    n = in_ref.shape[0]
    total = jnp.zeros(in_ref.shape[1:], F32)
    for i in reversed(range(n)) if backwards else range(n):
        out_ref[i] = total.astype(BF16)
        total += in_ref[i].astype(F32)


def running_sum(terms, backwards):
    n = lax.axis_size("ctx")
    parts = terms.reshape(n, H // n * DH, DH)
    here = lax.all_to_all(parts, "ctx", split_axis=0, concat_axis=0, tiled=True)
    sums = call(
        functools.partial(running_kernel, backwards),
        jax.ShapeDtypeStruct(here.shape, BF16),
        (1,),
        [whole(here.shape)],
        whole(here.shape),
        flops=here.size,
        moved=4 * here.size,
    )(here)
    back = lax.all_to_all(sums, "ctx", split_axis=0, concat_axis=0, tiled=True)
    return back.reshape(H, DH, DH)


def forward_kernel(
    q_ref, k_ref, v_ref, prior_ref, earlier_ref, gain_ref, router_ref, chosen_ref, pick_ref,
    z_ref, att_ref, sig_ref, send_ref, logits_ref,
):
    tokens = q_ref.shape[0]
    causal = causal_mask(tokens)
    step = pl.program_id(0)

    @pl.when(step == 0)
    def _():
        logits_ref[...] = jnp.zeros_like(logits_ref)

    for h in range(HB):
        q, k, v = q_ref[:, head(h)], k_ref[:, head(h)], v_ref[:, head(h)]
        high, low = halves(prior_ref[h] + earlier_ref[h].astype(F32))
        scores = jnp.where(causal, mm_nt(q, k), 0.0).astype(BF16)
        att = mm(scores, v) + mm(q, high) + mm(q, low)
        mean = jnp.mean(att * att, axis=1, keepdims=True)
        z = (att / jnp.sqrt(mean + EPS) * gain_ref[:, head(h)]).astype(BF16)
        att_ref[:, head(h)] = att
        z_ref[:, head(h)] = z
    z = z_ref[...]
    logits_ref[...] += mm(z, router_ref[...])
    send_ref[...] = mm(pick_ref[...], z).astype(BF16)

    @pl.when(step == pl.num_programs(0) - 1)
    def _():
        sig_ref[...] = jax.nn.sigmoid(logits_ref[...]) * chosen_ref[...]


def attention_forward(q, k, v, prior, earlier, gain, router, chosen, pick):
    tokens, rows, experts = q.shape[0], pick.shape[0], router.shape[1]
    return call(
        forward_kernel,
        (
            jax.ShapeDtypeStruct((tokens, D), BF16),
            jax.ShapeDtypeStruct((tokens, D), F32),
            jax.ShapeDtypeStruct((tokens, experts), F32),
            jax.ShapeDtypeStruct((rows, D), BF16),
        ),
        (H // HB,),
        [
            columns(tokens),
            columns(tokens),
            columns(tokens),
            per_head(),
            per_head(),
            columns(1),
            pl.BlockSpec((WIDTH, experts), lambda i: (i, 0)),
            whole((tokens, experts)),
            whole((rows, tokens)),
        ],
        (columns(tokens), columns(tokens), whole((tokens, experts)), columns(rows)),
        scratch=[pltpu.VMEM((tokens, experts), F32)],
        flops=2 * tokens * D * (4 * DH + rows),
        moved=2 * D * (8 * tokens + rows),
    )(q, k, v, prior, earlier, gain, router, chosen, pick)


def middle_kernel(
    q_ref, z_ref, att_ref, dy_ref, back_ref, pick_ref, dg_ref, sig_ref, gain_ref, router_ref,
    datt_ref, term_ref, rterm_ref, dlog_ref,
):
    experts = sig_ref.shape[1]

    @pl.when(pl.program_id(0) == 0)
    def _():
        sig = sig_ref[...]
        both = mm_tn(pick_ref[...], dg_ref[...])
        dg = both[:, :experts] + both[:, experts:]
        total = jnp.sum(sig, axis=1, keepdims=True)
        mean = jnp.sum(sig * dg, axis=1, keepdims=True) / total
        dlog = sig * (1.0 - sig) * (dg - mean) / total
        for i, part in enumerate(thirds(dlog)):
            dlog_ref[i] = part

    z, router = z_ref[...], router_ref[...]
    dz = dy_ref[...].astype(F32) + mm_tn(pick_ref[...], back_ref[...])
    term = jnp.zeros(rterm_ref.shape, F32)
    for i in range(3):
        dlog = dlog_ref[i]
        dz += mm_nt(dlog, router)
        term += mm_tn(dlog, z)
    rterm_ref[...] = term
    weighted = dz * gain_ref[...]
    for h in range(HB):
        att, w = att_ref[:, head(h)], weighted[:, head(h)]
        mean = jnp.mean(att * att, axis=1, keepdims=True) + EPS
        inner = jnp.sum(w * att, axis=1, keepdims=True)
        datt = ((w - att * (inner / (DH * mean))) / jnp.sqrt(mean)).astype(BF16)
        datt_ref[:, head(h)] = datt
        term_ref[h] = mm_tn(q_ref[:, head(h)], datt).astype(BF16)


def attention_middle(q, z, att, dy, back, pick, dg, sig, gain, router):
    tokens, rows, experts = q.shape[0], pick.shape[0], router.shape[1]
    return call(
        middle_kernel,
        (
            jax.ShapeDtypeStruct((tokens, D), BF16),
            jax.ShapeDtypeStruct((H, DH, DH), BF16),
            jax.ShapeDtypeStruct((experts, D), F32),
        ),
        (H // HB,),
        [
            columns(tokens),
            columns(tokens),
            columns(tokens),
            columns(tokens),
            columns(rows),
            whole((rows, tokens)),
            whole((rows, 2 * experts)),
            whole((tokens, experts)),
            columns(1),
            pl.BlockSpec((WIDTH, experts), lambda i: (i, 0)),
        ],
        (columns(tokens), per_head(), columns(experts)),
        scratch=[pltpu.VMEM((3, tokens, experts), BF16)],
        flops=2 * tokens * D * (DH + rows + 6 * experts),
        moved=2 * D * (8 * tokens + rows),
    )(q, z, att, dy, back, pick, dg, sig, gain, router)


def early_kernel(q_ref, k_ref, v_ref, datt_ref, prior_ref, earlier_ref, gq_ref, gk_ref, gv_ref):
    causal = causal_mask(q_ref.shape[0])
    for h in range(HB):
        q, k, v = q_ref[:, head(h)], k_ref[:, head(h)], v_ref[:, head(h)]
        datt = datt_ref[:, head(h)]
        high, low = halves(prior_ref[h] + earlier_ref[h].astype(F32))
        dscores = jnp.where(causal, mm_nt(datt, v), 0.0).astype(BF16)
        scores = jnp.where(causal, mm_nt(q, k), 0.0).astype(BF16)
        gq = mm(dscores, k) + mm_nt(datt, high) + mm_nt(datt, low)
        gq_ref[:, head(h)] = gq.astype(BF16)
        gk_ref[:, head(h)] = mm_tn(dscores, q)
        gv_ref[:, head(h)] = mm_tn(scores, datt)


def attention_early(q, k, v, datt, prior, earlier):
    tokens = q.shape[0]
    block = columns(tokens)
    return call(
        early_kernel,
        (
            jax.ShapeDtypeStruct((tokens, D), BF16),
            jax.ShapeDtypeStruct((tokens, D), F32),
            jax.ShapeDtypeStruct((tokens, D), F32),
        ),
        (H // HB,),
        [block, block, block, block, per_head(), per_head()],
        (block, block, block),
        flops=2 * tokens * D * DH * 7,
        moved=22 * D * tokens,
    )(q, k, v, datt, prior, earlier)


def late_kernel(k_ref, v_ref, later_ref, gk_ref, gv_ref, out_k_ref, out_v_ref):
    for h in range(HB):
        later = later_ref[h]
        out_k_ref[:, head(h)] = (gk_ref[:, head(h)] + mm_nt(v_ref[:, head(h)], later)).astype(BF16)
        out_v_ref[:, head(h)] = (gv_ref[:, head(h)] + mm(k_ref[:, head(h)], later)).astype(BF16)


def attention_late(k, v, later, gk, gv):
    tokens = k.shape[0]
    block = columns(tokens)
    out = jax.ShapeDtypeStruct((tokens, D), BF16)
    return call(
        late_kernel,
        (out, out),
        (H // HB,),
        [block, block, per_head(), block, block],
        (block, block),
        flops=2 * tokens * D * DH * 2,
        moved=18 * D * tokens,
    )(k, v, later, gk, gv)


def output_kernel(z_ref, pick_ref, back_ref, out_ref):
    out_ref[...] = (z_ref[...].astype(F32) + mm_tn(pick_ref[...], back_ref[...])).astype(BF16)


def layer_output(z, pick, back):
    tokens, rows = z.shape[0], pick.shape[0]
    return call(
        output_kernel,
        jax.ShapeDtypeStruct((tokens, D), BF16),
        (D // WIDTH,),
        [columns(tokens), whole((rows, tokens)), columns(rows)],
        columns(tokens),
        flops=2 * tokens * D * rows,
        moved=2 * D * rows,
    )(z, pick, back)


def exchange(rows, experts):
    shaped = rows.reshape(experts, rows.shape[0] // experts, rows.shape[1])
    moved = lax.all_to_all(shaped, ALL, split_axis=0, concat_axis=0, tiled=True)
    return moved.reshape(rows.shape)


def local(
    queries,
    keys,
    values,
    prior_state,
    norm_gain,
    router_weight,
    expert_ids,
    w_gate,
    w_up,
    w_down,
    cotangent,
):
    q, k, v, dy = queries[0], keys[0], values[0], cotangent[0]
    tokens = q.shape[0]
    experts = router_weight.shape[1]
    cap = max(2, 3 * tokens * TOPK // (2 * experts))
    gate_mat, up_mat, down_mat = w_gate[0], w_up[0], w_down[0]
    prior = prior_state[0]
    gain = norm_gain.reshape(1, D)
    me = lax.axis_index(ALL)

    terms = state_terms(k, v)
    pick, chosen, mask_send, dy_send = route(expert_ids[0], dy, experts, cap)
    earlier = running_sum(terms, False)
    mask_rows = exchange(mask_send, experts)
    dy_rows = exchange(dy_send, experts)
    z, att, sig, z_send = attention_forward(
        q, k, v, prior, earlier, gain, router_weight, chosen, pick
    )
    z_rows = exchange(z_send, experts)

    dh_plain = mm_nt(dy_rows, down_mat)
    sig_rows = jax.nn.sigmoid(mm(z_rows, router_weight)) * mask_rows.astype(F32)
    total = jnp.sum(sig_rows, axis=1, keepdims=True)
    lane = lax.broadcasted_iota(jnp.int32, sig_rows.shape, 1)
    mine = jnp.sum(jnp.where(lane == me, sig_rows, 0.0), axis=1, keepdims=True)
    gate = jnp.where(total > 0, mine / jnp.where(total > 0, total, 1.0), 0.0)
    gp = mm(z_rows, gate_mat)
    up = mm(z_rows, up_mat)
    gs = jax.nn.sigmoid(gp)
    hid = (gp * gs * up).astype(BF16)
    eo = mm(hid, down_mat)
    dg = jnp.sum(dy_rows.astype(F32) * eo, axis=1, keepdims=True)
    dg_high = lax.reduce_precision(dg, 8, 7)
    dg_low = dg - dg_high
    wide = lax.broadcasted_iota(jnp.int32, (z_rows.shape[0], 2 * experts), 1)
    dg_send = jnp.where(
        wide == me, dg_high, jnp.where(wide == me + experts, dg_low, 0.0)
    ).astype(BF16)
    eo_send = (gate * eo).astype(BF16)
    dg_back = exchange(dg_send, experts)
    dh = dh_plain * gate
    dgp = (dh * up * gs * (1.0 + gp * (1.0 - gs))).astype(BF16)
    dup = (dh * gp * gs).astype(BF16)
    dz_send = (gate * (mm_nt(dgp, gate_mat) + mm_nt(dup, up_mat))).astype(BF16)
    dz_back = exchange(dz_send, experts)
    eo_back = exchange(eo_send, experts)
    de = (gate * dy_rows.astype(F32)).astype(BF16)
    grad_down = mm_tn(hid, de).astype(BF16)
    grad_gate = mm_tn(z_rows, dgp).astype(BF16)
    grad_up = mm_tn(z_rows, dup).astype(BF16)

    datt, dterms, rterm = attention_middle(
        q, z, att, dy, dz_back, pick, dg_back, sig, gain, router_weight
    )
    later = running_sum(dterms, True)
    gq, gk, gv = attention_early(q, k, v, datt, prior, earlier)
    grad_k, grad_v = attention_late(k, v, later, gk, gv)
    output = layer_output(z, pick, eo_back)

    parts = rterm.reshape(experts, D // DH, DH)
    ours = lax.all_to_all(parts, ALL, split_axis=0, concat_axis=0, tiled=True)
    summed = jnp.sum(ours, axis=0, keepdims=True)
    spread = jnp.broadcast_to(summed, parts.shape)
    grad_router = lax.all_to_all(spread, ALL, split_axis=0, concat_axis=0, tiled=True)
    grad_router = grad_router.reshape(experts, D).T
    return (
        output[None],
        gq[None],
        grad_k[None],
        grad_v[None],
        grad_gate[None],
        grad_up[None],
        grad_down[None],
        grad_router,
    )


def solution(mesh):
    tokens = P("dp", "ctx", None)
    weights = P(ALL, None, None)
    placed = (
        tokens,
        tokens,
        tokens,
        P("dp", None, None, None),
        P(),
        P(),
        tokens,
        weights,
        weights,
        weights,
        tokens,
    )
    return jax.shard_map(
        local,
        mesh=mesh,
        in_specs=placed,
        out_specs=(tokens, tokens, tokens, tokens, weights, weights, weights, P()),
        check_vma=False,
    )
```

time: 666 us -> 453 us (0.68); the launches traced: 656 us -> 451 us
  waiting for transfers between devices: 327 us -> 194 us
  other arithmetic: 67.4 us -> 2.58 us
  local copies, waits for them, and re-layouts: 83.1 us -> 37.6 us
  starting transfers between devices: 12.5 us -> 40.7 us
  Pallas kernels: 0 us -> 27 us
  matrix products: 75.3 us -> 58.5 us
  blocking collectives: 75.8 us -> 89.7 us
  between operations: 14.6 us -> 1.05 us
    psum x1 -> x0, waiting for transfers between devices: 102 us -> none  [local(): grad_router = lax.psum(router_term, ('dp', 'ctx'))]
    all_gather x2 -> x0, waiting for transfers between devices: 39.5 us -> none  [the longest x1 37.3 us: carried_in(): pieces = lax.all_gather(value, axis)]
    gather x4 -> x0, local copies, waits for them, and re-layouts: 32.2 us -> none  [the longest x1 8.95 us: local(): grad_out_assign[jnp.where(filled, source, 0)]]
    all_to_all x3 -> x10, starting transfers between devices: 11.9 us -> 40.7 us  [the longest x5 20.3 us: exchange(): moved = lax.all_to_all(shaped, ALL, split_axis=0, concat_axis=0, tiled=True)]
    pallas_call x0 -> x9, Pallas kernels: none -> 27 us  [the longest x1 5.38 us: attention_middle(): call(middle_kernel, (jax.ShapeDtypeStruct((tokens, D), BF16), jax.ShapeDt...]
    select_n x10 -> x1, other arithmetic: 23 us -> 0.01 us  [local(): gate = jnp.where(total > 0, mine / jnp.where(total > 0, total, 1.0), 0.0)]
    unnamed x68 -> x102, local copies, waits for them, and re-layouts: 16.8 us -> 35.7 us
    add x7 -> x0, other arithmetic: 17.3 us -> none  [add_states(): return earlier + later]
  transfers between devices with their start and end apart: 6 -> 10, of which waited for: 6 -> 9; matrix products, arithmetic and copies ran while one was open for 17% -> 10% of each run, Pallas kernels for 0% -> 6%
where the time goes in v1:
time: 453 us; the launch traced here: 451 us
  waiting for transfers between devices  194 us (43%)
  blocking collectives  89.7 us (20%)
  matrix products  58.5 us (13%)
  starting transfers between devices  40.7 us (9%)
  local copies, waits for them, and re-layouts  37.6 us (8%)
  Pallas kernels  27 us (6%)
    all_to_all x5, waiting for transfers between devices, exchange(): moved = lax.all_to_all(shaped, ALL, split_axis=0, concat_axis=0, tiled=True)  180 us
    all_to_all x1, blocking collectives, exchange(): moved = lax.all_to_all(shaped, ALL, split_axis=0, concat_axis=0, tiled=True)  75.9 us
    unnamed x102, local copies, waits for them, and re-layouts  35.7 us
    dot_general x4, matrix products, mm(): return jnp.dot(a, b, preferred_element_type=F32)  20.5 us
    all_to_all x5, starting transfers between devices, exchange(): moved = lax.all_to_all(shaped, ALL, split_axis=0, concat_axis=0, tiled=True)  20.3 us
    dot_general x3, matrix products, mm_tn(): lax.dot_general(a, b, (((0,), (0,)), ((), ())), preferred_element_type=F32)  19.9 us
    dot_general x3, matrix products, mm_nt(): lax.dot_general(a, b, (((1,), (1,)), ((), ())), preferred_element_type=F32)  18.1 us
    all_to_all x1, blocking collectives, running_sum(): back = lax.all_to_all(sums, 'ctx', split_axis=0, concat_axis=0, tiled=True)  13.9 us
  transfers between devices with their start and end apart: 10, of which 9 were waited for; matrix products, arithmetic and copies ran while one was open for 10% of the time, Pallas kernels for 6%

profile of v1, /device:TPU:0, one launch (start us, length us, event | category | flops | bytes accessed | tf_op | source)
XLA Modules:
  0.0 451.2 jit_solution(9306846502979758013)
XLA Ops:
  0.7 1.2 copy-done.2
  4.7 5.2 %all-to-all-start = ((bf16[8,256,128]{2,1,0:T(8,128)(2,1)}), bf16[8,256,128]{2,1,0:T(8,128)(2,1)}, u32[]{:S(2)}, u32[]{:S(2)}) async-start(bf16[8,256,128]{2,1,0:T(8,128)(2,1)} %bitcast.93), calls=%async_computation | async-start | bytes 1048576 | tf_op jit(solution)/shard_map/all_to_all | solution.py:156
  9.9 1.4 copy.27
  13.2 1.5 shard_map.172
  14.7 1.7 copy-done.17
  17.7 2.0 all-to-all-done.in_ref
  19.7 4.7 %all-to-all-start.3 = ((bf16[32,2,384]{2,1,0:T(2,128)(2,1)}), bf16[32,2,384]{2,1,0:T(2,128)(2,1)S(1)}, u32[]{:S(2)}, u32[]{:S(2)}) async-start(bf16[32,2,384]{2,1,0:T(2,128)(2,1)} %reshape.130), calls=%async_computation.3 | async-start | bytes 98304 | tf_op jit(solution)/shard_map/all_to_all | solution.py:366
  24.4 1.1 shard_map.171
  26.3 5.4 %all-to-all-done.3 = bf16[32,2,384]{2,1,0:T(2,128)(2,1)S(1)} async-done(((bf16[32,2,384]{2,1,0:T(2,128)(2,1)}), bf16[32,2,384]{2,1,0:T(2,128)(2,1)S(1)}, u32[]{:S(2)}, u32[]{:S(2)}) %all-to-all-start.3) | async-done | bytes 49184 | tf_op jit(solution)/shard_map/all_to_all | solution.py:366
  31.8 13.9 %all_to_all.60 = bf16[8,256,128]{2,1,0:T(8,128)(2,1)} all-to-all(bf16[8,256,128]{2,1,0:T(8,128)(2,1)} %copy-done.23), channel_id=1, replica_groups=mesh['dp'=4,'ctx'=8] {'ctx'}, dimensions={0} | all-to-all | bytes 1048576 | tf_op jit(solution)/shard_map/all_to_all | solution.py:166
  45.6 3.7 all-to-all-start.5
  50.3 1.0 copy-done.3
  55.6 1.2 copy-done.15
  56.8 5.3 %shard_map.173 = (bf16[128,2048]{1,0:T(8,128)(2,1)S(1)}, f32[128,2048]{1,0:T(8,128)S(1)}, f32[128,32]{1,0:T(8,128)S(1)}, bf16[768,2048]{1,0:T(8,128)(2,1)}) custom-call(bf16[128,2048]{1,0:T(8,128)(2,1)S(1)} %bitcast.85, bf16[128,2048]{1,0:T(8,128)(2,1)S(1)} %bitcast.78, bf16[128,2048]{1,0:T(8,128)(2,1)S(1)} %bitcast.82, f32[16,128,128]{2,1,0:T(8,128)S(1)} %bitcast.90, ...), custom_call_target="tpu_custom_call" | custom-call | flops 671088640 | bytes 7340032 | tf_op jit(solution)/shard_map/pallas_call | solution.py:202
  64.5 56.3 %all-to-all-done.5 = bf16[32,24,2048]{2,1,0:T(8,128)(2,1)} async-done(((bf16[32,24,2048]{2,1,0:T(8,128)(2,1)}), bf16[32,24,2048]{2,1,0:T(8,128)(2,1)}, u32[]{:S(2)}, u32[]{:S(2)}) %all-to-all-start.5) | async-done | bytes 3145760 | tf_op jit(solution)/shard_map/all_to_all | solution.py:366
  120.8 4.2 all-to-all-start.2
  127.3 1.1 copy.31
  128.4 6.9 %fusion.3 = f32[768,768]{1,0:T(8,128)} fusion(bf16[768,2048]{1,0:T(8,128)(2,1)} %bitcast.20, bf16[1,768,2048]{2,1,0:T(8,128)(2,1)} %param.20), kind=kOutput, calls=%fused_computation.9 | convolution fusion | flops 2415919104 | bytes 8650752 | tf_op jit(solution)/shard_map/dot_general | solution.py:32
  135.3 61.0 %all-to-all-done.2 = bf16[32,24,2048]{2,1,0:T(8,128)(2,1)} async-done(((bf16[32,24,2048]{2,1,0:T(8,128)(2,1)}), bf16[32,24,2048]{2,1,0:T(8,128)(2,1)}, u32[]{:S(2)}, u32[]{:S(2)}) %all-to-all-start.2) | async-done | bytes 3145760 | tf_op jit(solution)/shard_map/all_to_all | solution.py:366
  196.3 5.5 %fusion.8 = f32[768,768]{1,0:T(8,128)S(1)} fusion(bf16[768,2048]{1,0:T(8,128)(2,1)} %bitcast.10, bf16[1,2048,768]{2,1,0:T(8,128)(2,1)} %param.19), kind=kOutput, calls=%fused_computation.14 | convolution fusion | flops 2415919104 | bytes 8650752 | tf_op jit(solution)/shard_map/dot_general | solution.py:24
  201.8 3.1 select_reduce_fusion
  204.9 6.3 %multiply_convert_fusion.2 = (bf16[768,768]{1,0:T(8,128)(2,1)}, bf16[768,768]{1,0:T(8,128)(2,1)S(1)}, bf16[768,768]{1,0:T(8,128)(2,1)S(1)}) fusion(f32[768,768]{1,0:T(8,128)S(1)} %copy-done.45, f32[768]{0:T(1024)S(1)} %compare_select_fusion, f32[768,768]{1,0:T(8,128)S(1)} %fusion.8, bf16[768,2048]{1,0:T(8,128)(2,1)} %bitcast.10, ...), kind=kOutput, calls=%fused_computation.24 | convolution fusion | flops 2425946112 | bytes 14552064 | tf_op jit(solution)/shard_map/dot_general | solution.py:24
  211.3 4.5 fusion.10
  215.8 5.6 %fusion = (f32[768]{0:T(1024)S(1)}, bf16[768,2048]{1,0:T(8,128)(2,1)}) fusion(bf16[32,24,2048]{2,1,0:T(8,128)(2,1)} %all-to-all-done.5, f32[768]{0:T(1024)S(1)} %compare_select_fusion, bf16[768,768]{1,0:T(8,128)(2,1)S(1)} %get-tuple-element.46, bf16[1,768,2048]{2,1,0:T(8,128)(2,1)S(1)} %copy-done.43), kind=kOutput, calls=%fused_computation.2 | convolution fusion | flops 2423782656 | bytes 10622976 | tf_op jit(solution)/shard_map/dot_general | solution.py:24
  222.5 4.1 all-to-all-start.7
  226.6 6.7 %multiply_convert_fusion = bf16[768,2048]{1,0:T(8,128)(2,1)S(1)} fusion(f32[768,2048]{1,0:T(8,128)} %fusion.10, bf16[768,768]{1,0:T(8,128)(2,1)} %get-tuple-element.44, bf16[1,2048,768]{2,1,0:T(8,128)(2,1)} %param.19, f32[768]{0:T(1024)S(1)} %compare_select_fusion), kind=kOutput, calls=%fused_computation.4 | convolution fusion | flops 2420637696 | bytes 13765632 | tf_op jit(solution)/shard_map/dot_general | solution.py:32
  234.2 75.9 %all_to_all.61 = bf16[32,24,2048]{2,1,0:T(8,128)(2,1)} all-to-all(bf16[32,24,2048]{2,1,0:T(8,128)(2,1)S(1)} %bitcast.106), channel_id=1, replica_groups=mesh['dp'=4,'ctx'=8] {'dp','ctx'}, dimensions={0} | all-to-all | bytes 6291456 | tf_op jit(solution)/shard_map/all_to_all | solution.py:366
  310.1 3.7 all-to-all-start.4
  313.8 1.1 reshape.133
  318.0 1.2 copy-done.25
  321.1 5.4 %shard_map.175 = (bf16[128,2048]{1,0:T(8,128)(2,1)S(1)}, bf16[16,128,128]{2,1,0:T(8,128)(2,1)S(1)}, f32[32,2048]{1,0:T(8,128)S(1)}) custom-call(bf16[128,2048]{1,0:T(8,128)(2,1)S(1)} %bitcast.86, bf16[128,2048]{1,0:T(8,128)(2,1)S(1)} %copy-done.19, f32[128,2048]{1,0:T(8,128)S(1)} %copy-done.25, bf16[128,2048]{1,0:T(8,128)(2,1)S(1)} %bitcast.96, ...), custom_call_target="tpu_custom_call" | custom-call | flops 570425344 | bytes 7340032 | tf_op jit(solution)/shard_map/pallas_call | solution.py:266
  328.8 56.4 %all-to-all-done.4 = bf16[32,24,2048]{2,1,0:T(8,128)(2,1)S(1)} async-done(((bf16[32,24,2048]{2,1,0:T(8,128)(2,1)}), bf16[32,24,2048]{2,1,0:T(8,128)(2,1)S(1)}, u32[]{:S(2)}, u32[]{:S(2)}) %all-to-all-start.4) | async-done | bytes 3145760 | tf_op jit(solution)/shard_map/all_to_all | solution.py:366
  385.3 4.1 all-to-all-start.8
  389.4 1.7 copy.32
  391.1 8.1 %all-to-all-done.8.in_ref = bf16[8,256,128]{2,1,0:T(8,128)(2,1)} async-done(((bf16[8,256,128]{2,1,0:T(8,128)(2,1)}), bf16[8,256,128]{2,1,0:T(8,128)(2,1)}, u32[]{:S(2)}, u32[]{:S(2)}) %all-to-all-start.8) | async-done | bytes 524320 | tf_op jit(solution)/shard_map/all_to_all | solution.py:156
  399.2 3.3 all-to-all-start.10
  402.5 6.7 %fusion.17 = bf16[1,768,2048]{2,1,0:T(8,128)(2,1)} fusion(bf16[768,768]{1,0:T(8,128)(2,1)} %copy-done.46, bf16[768,2048]{1,0:T(8,128)(2,1)} %bitcast.20, f32[768]{0:T(1024)S(1)} %compare_select_fusion), kind=kOutput, calls=%fused_computation.23 | convolution fusion | flops 2422210560 | bytes 7474176 | tf_op jit(solution)/shard_map/dot_general | solution.py:28
  409.2 1.1 shard_map.177
  411.1 2.0 all-to-all-done.10
  413.1 4.1 all-to-all-start.9
  417.2 6.6 %fusion.15 = bf16[1,2048,768]{2,1,0:T(8,128)(2,1)} fusion(bf16[768,2048]{1,0:T(8,128)(2,1)} %bitcast.10, bf16[768,768]{1,0:T(8,128)(2,1)} %copy-done.44), kind=kOutput, calls=%fused_computation.21 | convolution fusion | flops 2417491968 | bytes 7471104 | tf_op jit(solution)/shard_map/dot_general | solution.py:28
  424.8 2.2 all-to-all-done.9
  427.7 3.6 all-to-all-start.11
  431.3 6.6 %fusion.16 = bf16[1,2048,768]{2,1,0:T(8,128)(2,1)} fusion(bf16[768,2048]{1,0:T(8,128)(2,1)} %bitcast.10, bf16[768,768]{1,0:T(8,128)(2,1)} %get-tuple-element.44), kind=kOutput, calls=%fused_computation.22 | convolution fusion | flops 2417491968 | bytes 7471104 | tf_op jit(solution)/shard_map/dot_general | solution.py:28
  438.0 2.4 shard_map.174
  440.4 5.3 %shard_map.176 = (bf16[128,2048]{1,0:T(8,128)(2,1)}, f32[128,2048]{1,0:T(8,128)S(1)}, f32[128,2048]{1,0:T(8,128)S(1)}) custom-call(bf16[128,2048]{1,0:T(8,128)(2,1)S(1)} %bitcast.87, bf16[128,2048]{1,0:T(8,128)(2,1)S(1)} %bitcast.79, bf16[128,2048]{1,0:T(8,128)(2,1)S(1)} %bitcast.83, bf16[128,2048]{1,0:T(8,128)(2,1)S(1)} %copy-done.29, ...), custom_call_target="tpu_custom_call" | custom-call | flops 469762048 | bytes 5767168 | tf_op jit(solution)/shard_map/pallas_call | solution.py:310
  445.7 3.7 shard_map.178
  449.5 1.7 copy.35
  (105 shorter events, 28.7 us)
Async XLA Ops:
  0.6 204.3 %copy-start = (bf16[1,2048,768]{2,1,0:T(8,128)(2,1)S(1)}, bf16[1,2048,768]{2,1,0:T(8,128)(2,1)}, u32[]{:S(2)}) copy-start(bf16[1,2048,768]{2,1,0:T(8,128)(2,1)} %param.18) | copy-start | bytes 9437188
  0.6 1.2 copy-start.2
  1.8 1.0 copy-start.5
  4.7 15.0 %all-to-all-start = ((bf16[8,256,128]{2,1,0:T(8,128)(2,1)}), bf16[8,256,128]{2,1,0:T(8,128)(2,1)}, u32[]{:S(2)}, u32[]{:S(2)}) async-start(bf16[8,256,128]{2,1,0:T(8,128)(2,1)} %bitcast.93), calls=%async_computation | async-start | bytes 1048576 | tf_op jit(solution)/shard_map/all_to_all | solution.py:156
  11.3 1.0 copy-start.26
  12.3 0.8 copy-start.36
  14.6 1.7 copy-start.17
  19.7 12.0 %all-to-all-start.3 = ((bf16[32,2,384]{2,1,0:T(2,128)(2,1)}), bf16[32,2,384]{2,1,0:T(2,128)(2,1)S(1)}, u32[]{:S(2)}, u32[]{:S(2)}) async-start(bf16[32,2,384]{2,1,0:T(2,128)(2,1)} %reshape.130), calls=%async_computation.3 | async-start | bytes 98304 | tf_op jit(solution)/shard_map/all_to_all | solution.py:366
  31.7 13.9 %copy-start.41 = (bf16[32,2,384]{2,1,0:T(2,128)(2,1)}, bf16[32,2,384]{2,1,0:T(2,128)(2,1)S(1)}, u32[]{:S(2)}) copy-start(bf16[32,2,384]{2,1,0:T(2,128)(2,1)S(1)} %all-to-all-done.3) | copy-start | bytes 147460
  45.6 3.7 copy-start.38
  45.6 4.7 %copy-start.35 = (f32[128,32]{1,0:T(8,128)S(1)}, f32[128,32]{1,0:T(8,128)}, u32[]{:S(2)}) copy-start(f32[128,32]{1,0:T(8,128)} %copy-done.34) | copy-start | bytes 49156
  45.6 4.7 %copy-start.37 = (f32[2048]{0:T(1024)S(1)}, f32[2048]{0:T(1024)}, u32[]{:S(2)}) copy-start(f32[2048]{0:T(1024)} %param.15) | copy-start | bytes 24580
  45.6 75.2 %all-to-all-start.5 = ((bf16[32,24,2048]{2,1,0:T(8,128)(2,1)}), bf16[32,24,2048]{2,1,0:T(8,128)(2,1)}, u32[]{:S(2)}, u32[]{:S(2)}) async-start(bf16[32,24,2048]{2,1,0:T(8,128)(2,1)} %bitcast.92), calls=%async_computation.5 | async-start | bytes 6291456 | tf_op jit(solution)/shard_map/all_to_all | solution.py:366
  50.3 1.0 copy-start.3
  51.4 1.0 copy-start.6
  52.4 1.0 copy-start.8
  53.5 1.0 copy-start.11
  54.5 1.0 copy-start.13
  55.6 1.2 copy-start.15
  62.9 1.0 copy-start.24
  120.8 75.5 %all-to-all-start.2 = ((bf16[32,24,2048]{2,1,0:T(8,128)(2,1)}), bf16[32,24,2048]{2,1,0:T(8,128)(2,1)}, u32[]{:S(2)}, u32[]{:S(2)}) async-start(bf16[32,24,2048]{2,1,0:T(8,128)(2,1)} %bitcast.104), calls=%async_computation.2 | async-start | bytes 6291456 | tf_op jit(solution)/shard_map/all_to_all | solution.py:366
  196.3 5.5 %copy-start.39 = (bf16[2048,32]{0,1:T(8,128)(2,1)S(1)}, bf16[2048,32]{0,1:T(8,128)(2,1)}, u32[]{:S(2)}) copy-start(bf16[2048,32]{0,1:T(8,128)(2,1)} %param.16) | copy-start | bytes 393220
  201.8 3.2 copy-start.45
  211.3 4.5 %copy-start.44 = (bf16[768,768]{1,0:T(8,128)(2,1)}, bf16[768,768]{1,0:T(8,128)(2,1)S(1)}, u32[]{:S(2)}) copy-start(bf16[768,768]{1,0:T(8,128)(2,1)S(1)} %get-tuple-element.45) | copy-start | bytes 3538948
  211.3 4.5 %copy-start.46 = (bf16[768,768]{1,0:T(8,128)(2,1)}, bf16[768,768]{1,0:T(8,128)(2,1)S(1)}, u32[]{:S(2)}) copy-start(bf16[768,768]{1,0:T(8,128)(2,1)S(1)} %get-tuple-element.46) | copy-start | bytes 3538948
  211.3 4.5 %copy-start.43 = (bf16[1,768,2048]{2,1,0:T(8,128)(2,1)S(1)}, bf16[1,768,2048]{2,1,0:T(8,128)(2,1)}, u32[]{:S(2)}) copy-start(bf16[1,768,2048]{2,1,0:T(8,128)(2,1)} %param.20) | copy-start | bytes 9437188
  215.8 5.7 %copy-start.42 = (pred[64]{0:T(512)(128)(4,1)S(1)}, pred[64]{0:T(512)(128)(4,1)}, u32[]{:S(2)}) copy-start(pred[64]{0:T(512)(128)(4,1)} %get-tuple-element.50) | copy-start | bytes 196
  222.5 11.7 %all-to-all-start.7 = ((bf16[32,2,768]{2,1,0:T(2,128)(2,1)}), bf16[32,2,768]{2,1,0:T(2,128)(2,1)S(1)}, u32[]{:S(2)}, u32[]{:S(2)}) async-start(bf16[32,2,768]{2,1,0:T(2,128)(2,1)} %reshape.132), calls=%async_computation.7 | async-start | bytes 196608 | tf_op jit(solution)/shard_map/all_to_all | solution.py:366
  234.2 75.9 %copy-start.40 = (bf16[32,2,768]{2,1,0:T(2,128)(2,1)}, bf16[32,2,768]{2,1,0:T(2,128)(2,1)S(1)}, u32[]{:S(2)}) copy-start(bf16[32,2,768]{2,1,0:T(2,128)(2,1)S(1)} %all-to-all-done.7) | copy-start | bytes 294916
  310.1 75.1 %all-to-all-start.4 = ((bf16[32,24,2048]{2,1,0:T(8,128)(2,1)}), bf16[32,24,2048]{2,1,0:T(8,128)(2,1)S(1)}, u32[]{:S(2)}, u32[]{:S(2)}) async-start(bf16[32,24,2048]{2,1,0:T(8,128)(2,1)} %bitcast.105), calls=%async_computation.4 | async-start | bytes 6291456 | tf_op jit(solution)/shard_map/all_to_all | solution.py:366
  314.9 1.0 copy-start.9
  315.9 1.0 copy-start.12
  317.0 1.0 copy-start.19
  318.0 1.2 copy-start.25
  319.2 1.0 copy-start.27
  320.3 0.8 copy-start.33
  385.3 13.9 %all-to-all-start.8 = ((bf16[8,256,128]{2,1,0:T(8,128)(2,1)}), bf16[8,256,128]{2,1,0:T(8,128)(2,1)}, u32[]{:S(2)}, u32[]{:S(2)}) async-start(bf16[8,256,128]{2,1,0:T(8,128)(2,1)} %bitcast.97), calls=%async_computation.8 | async-start | bytes 1048576 | tf_op jit(solution)/shard_map/all_to_all | solution.py:156
  399.2 13.9 %all-to-all-start.10 = ((f32[32,16,128]{2,1,0:T(8,128)}), f32[32,16,128]{2,1,0:T(8,128)}, u32[]{:S(2)}, u32[]{:S(2)}) async-start(f32[32,16,128]{2,1,0:T(8,128)} %bitcast.107), calls=%async_computation.10 | async-start | bytes 524288 | tf_op jit(solution)/shard_map/all_to_all | solution.py:442
  413.1 13.9 %all-to-all-start.9 = ((bf16[8,256,128]{2,1,0:T(8,128)(2,1)}), bf16[8,256,128]{2,1,0:T(8,128)(2,1)}, u32[]{:S(2)}, u32[]{:S(2)}) async-start(bf16[8,256,128]{2,1,0:T(8,128)(2,1)} %copy-done.22), calls=%async_computation.9 | async-start | bytes 1048576 | tf_op jit(solution)/shard_map/all_to_all | solution.py:166
  427.7 21.8 %all-to-all-start.11 = ((f32[32,16,128]{2,1,0:T(8,128)}), f32[32,16,128]{2,1,0:T(8,128)}, u32[]{:S(2)}, u32[]{:S(2)}) async-start(f32[32,16,128]{2,1,0:T(8,128)} %broadcast_in_dim.71), calls=%async_computation.11 | async-start | bytes 524288 | tf_op jit(solution)/shard_map/all_to_all | solution.py:445
  431.3 6.7 %copy-start.20 = (bf16[128,2048]{1,0:T(8,128)(2,1)S(1)}, bf16[128,2048]{1,0:T(8,128)(2,1)}, u32[]{:S(2)}) copy-start(bf16[128,2048]{1,0:T(8,128)(2,1)} %copy-done.18) | copy-start | bytes 1572868
  437.9 2.5 copy-start.4
  437.9 2.5 copy-start.7
  437.9 2.5 copy-start.10
  437.9 2.5 copy-start.14
  437.9 2.5 copy-start.16
  437.9 2.5 copy-start.29
  440.4 10.8 %copy-start.1 = (bf16[1,2048,768]{2,1,0:T(8,128)(2,1)S(1)}, bf16[1,2048,768]{2,1,0:T(8,128)(2,1)}, u32[]{:S(2)}) copy-start(bf16[1,2048,768]{2,1,0:T(8,128)(2,1)} %param.18) | copy-start | bytes 9437188
  (9 other events, 6.7 us)

commit v2 on v1

v2 whole, which is shorter than its diff:
```python
import functools

import jax
import jax.numpy as jnp
from jax import lax
from jax.experimental import pallas as pl
from jax.experimental.pallas import tpu as pltpu
from jax.sharding import Mesh
from jax.sharding import PartitionSpec as P

H = 16
DH = 128
D = 2048
TOPK = 4
HB = 8
WIDTH = 512
HEADS = HB * DH
EPS = 1e-05
ALL = ("far", "near", "ctx")
F32 = jnp.float32
BF16 = jnp.bfloat16
LIMIT = 60 << 20


def mm(a, b):
    return jnp.dot(a, b, preferred_element_type=F32)


def mm_tn(a, b):
    return lax.dot_general(a, b, (((0,), (0,)), ((), ())), preferred_element_type=F32)


def mm_nt(a, b):
    return lax.dot_general(a, b, (((1,), (1,)), ((), ())), preferred_element_type=F32)


def halves(x):
    high = x.astype(BF16)
    return high, (x - high.astype(F32)).astype(BF16)


def thirds(x):
    high, rest = x.astype(BF16), None
    rest = x - high.astype(F32)
    middle = rest.astype(BF16)
    return high, middle, (rest - middle.astype(F32)).astype(BF16)


def causal_mask(n):
    return lax.broadcasted_iota(jnp.int32, (n, n), 0) >= lax.broadcasted_iota(jnp.int32, (n, n), 1)


def head(h):
    return slice(h * DH, (h + 1) * DH)


def call(kernel, out_shape, grid, in_specs, out_specs, scratch=(), flops=0, moved=0):
    return pl.pallas_call(
        kernel,
        out_shape=out_shape,
        grid=grid,
        in_specs=in_specs,
        out_specs=out_specs,
        scratch_shapes=scratch,
        compiler_params=pltpu.CompilerParams(vmem_limit_bytes=LIMIT),
        cost_estimate=pl.CostEstimate(flops=flops, bytes_accessed=moved, transcendentals=0),
    )


def whole(shape):
    return pl.BlockSpec(shape, lambda *_: (0,) * len(shape))


def columns(rows, width=HEADS):
    return pl.BlockSpec((rows, width), lambda i: (0, i))


def per_head(n=HB):
    return pl.BlockSpec((n, DH, DH), lambda i: (i, 0, 0))


def lanes_of(n):
    return -(-n // 128) * 128


def route_kernel(cap, top, plane_ref, *refs):
    *ids_refs, pick_ref, chosen_ref = refs
    tokens = ids_refs[0].shape[0]
    experts = chosen_ref.shape[1]
    rows = pick_ref.shape[0]
    slots = len(ids_refs) * cap
    group = rows // slots
    row = lax.broadcasted_iota(jnp.int32, (rows, experts), 0)
    first = lax.broadcasted_iota(jnp.int32, (rows, experts), 1) - plane_ref[0, 0] * group
    first = first * slots
    owns = (row >= first) & (row < first + slots)
    wanted = jnp.sum(jnp.where(owns, row - first + 1, 0), axis=1, keepdims=True).astype(F32)
    owns = owns.astype(F32).astype(BF16)
    lane = lax.broadcasted_iota(jnp.int32, (tokens, experts), 1)
    earlier = causal_mask(tokens).astype(F32).astype(BF16)
    for b, ref in enumerate(ids_refs):
        ids = ref[...].astype(F32)
        chosen = jnp.zeros((tokens, experts), F32)
        for j in range(top):
            chosen += (ids[:, j : j + 1] == lane.astype(F32)).astype(F32)
        place = chosen * (mm(earlier, chosen.astype(BF16)) + float(b * cap))
        found = mm_nt(owns, place.astype(BF16))
        at = slice(b * tokens, (b + 1) * tokens)
        pick_ref[:, at] = (found == wanted).astype(F32).astype(BF16)
        chosen_ref[at] = chosen


def smem():
    return pl.BlockSpec(memory_space=pltpu.SMEM)


def route(plane, blocks, experts, rows, cap):
    tokens, n = blocks[0].shape[0], len(blocks)
    return call(
        functools.partial(route_kernel, cap, TOPK),
        (
            jax.ShapeDtypeStruct((rows, n * tokens), BF16),
            jax.ShapeDtypeStruct((n * tokens, experts), F32),
        ),
        (1,),
        [smem()] + [pl.BlockSpec((tokens, 128), lambda i: (0, D // 128))] * n,
        (whole((rows, n * tokens)), whole((n * tokens, experts))),
        flops=2 * n * rows * tokens * experts,
        moved=2 * n * rows * tokens,
    )(plane, *blocks)


def gather_kernel(masked, pick_ref, chosen_ref, *refs):
    *block_refs, send_ref, stack_ref = refs
    tokens = block_refs[0].shape[0]
    pick = pick_ref[...]
    for b, ref in enumerate(block_refs):
        stack_ref[b * tokens : (b + 1) * tokens] = ref[:, :D]
    for c in range(D // WIDTH):
        at = slice(c * WIDTH, (c + 1) * WIDTH)
        send_ref[:, at] = mm(pick, stack_ref[:, at]).astype(BF16)
    if masked:
        experts = chosen_ref.shape[1]
        if send_ref.shape[1] > D + experts:
            send_ref[:, D:] = jnp.zeros((send_ref.shape[0], send_ref.shape[1] - D), BF16)
        mask = mm(pick, chosen_ref[...].astype(BF16))
        send_ref[:, D : D + experts] = mask.astype(BF16)


def gather(pick, chosen, blocks, masked):
    rows = pick.shape[0]
    width = D + (lanes_of(chosen.shape[1]) if masked else 0)
    return call(
        functools.partial(gather_kernel, masked),
        jax.ShapeDtypeStruct((rows, width), BF16),
        (1,),
        [whole(pick.shape), whole(chosen.shape)] + [whole(blocks[0].shape)] * len(blocks),
        whole((rows, width)),
        scratch=[pltpu.VMEM((pick.shape[1], D), BF16)],
        flops=2 * rows * pick.shape[1] * D,
        moved=2 * rows * D,
    )(pick, chosen, *blocks)


def partial_kernel(pick_ref, back_ref, *out_refs):
    tokens, width = out_refs[0].shape
    for b, ref in enumerate(out_refs):
        pick = pick_ref[:, (b + 1) * tokens : (b + 2) * tokens]
        for c in range(0, width, WIDTH):
            at = slice(c, min(c + WIDTH, width))
            ref[:, at] = mm_tn(pick, back_ref[:, at]).astype(BF16)


def partials(pick, back, tokens):
    others = pick.shape[1] // tokens - 1
    rows, width = back.shape
    return call(
        partial_kernel,
        (jax.ShapeDtypeStruct((tokens, width), BF16),) * others,
        (1,),
        [whole(pick.shape), whole(back.shape)],
        (whole((tokens, width)),) * others,
        flops=2 * others * rows * width * tokens,
        moved=2 * rows * width,
    )(pick, back)


def state_kernel(k_ref, v_ref, out_ref):
    for h in range(HB):
        out_ref[h] = mm_tn(k_ref[:, head(h)], v_ref[:, head(h)]).astype(BF16)


def state_terms(k, v):
    tokens = k.shape[0]
    return call(
        state_kernel,
        jax.ShapeDtypeStruct((H, DH, DH), BF16),
        (H // HB,),
        [columns(tokens), columns(tokens)],
        per_head(),
        flops=2 * tokens * D * DH,
        moved=6 * tokens * D,
    )(k, v)


def running_kernel(backwards, states, in_ref, out_ref):
    n, rows, _ = in_ref.shape
    total = jnp.zeros((states, DH), F32)
    for i in reversed(range(n)) if backwards else range(n):
        out_ref[i, :states] = total.astype(BF16)
        total += in_ref[i, :states].astype(F32)
    if rows > states:
        half = (rows - states) // 2
        whole_sum = jnp.zeros((half, DH), F32)
        for i in range(n):
            whole_sum += in_ref[i, states : states + half].astype(F32)
            whole_sum += in_ref[i, states + half :].astype(F32)
        high, low = halves(whole_sum)
        for i in range(n):
            out_ref[i, states : states + half] = high
            out_ref[i, states + half :] = low


def to_heads(block):
    return lax.all_to_all(block, "ctx", split_axis=0, concat_axis=0, tiled=True)


def running_sum(here, backwards):
    states = H // here.shape[0] * DH
    return call(
        functools.partial(running_kernel, backwards, states),
        jax.ShapeDtypeStruct(here.shape, BF16),
        (1,),
        [whole(here.shape)],
        whole(here.shape),
        flops=here.size,
        moved=4 * here.size,
    )(here)


def forward_kernel(
    q_ref, k_ref, v_ref, prior_ref, earlier_ref, gain_ref, router_ref, ids_ref,
    z_ref, att_ref, sig_ref, logits_ref,
):
    tokens = q_ref.shape[0]
    causal = causal_mask(tokens)
    step = pl.program_id(0)

    @pl.when(step == 0)
    def _():
        logits_ref[...] = jnp.zeros_like(logits_ref)

    for h in range(HB):
        q, k, v = q_ref[:, head(h)], k_ref[:, head(h)], v_ref[:, head(h)]
        high, low = halves(prior_ref[h] + earlier_ref[h].astype(F32))
        scores = jnp.where(causal, mm_nt(q, k), 0.0).astype(BF16)
        att = mm(scores, v) + mm(q, high) + mm(q, low)
        mean = jnp.mean(att * att, axis=1, keepdims=True)
        z = (att / jnp.sqrt(mean + EPS) * gain_ref[:, head(h)]).astype(BF16)
        att_ref[:, head(h)] = att
        z_ref[:, head(h)] = z
    logits_ref[...] += mm(z_ref[...], router_ref[...])

    @pl.when(step == pl.num_programs(0) - 1)
    def _():
        experts = sig_ref.shape[1]
        lane = lax.broadcasted_iota(jnp.int32, (tokens, experts), 1)
        chosen = jnp.zeros((tokens, experts), F32)
        for j in range(ids_ref.shape[1]):
            chosen += (ids_ref[:, j : j + 1] == lane).astype(F32)
        sig_ref[...] = jax.nn.sigmoid(logits_ref[...]) * chosen


def attention_forward(q, k, v, prior, earlier, gain, router, ids):
    tokens, experts = q.shape[0], router.shape[1]
    return call(
        forward_kernel,
        (
            jax.ShapeDtypeStruct((tokens, D), BF16),
            jax.ShapeDtypeStruct((tokens, D), F32),
            jax.ShapeDtypeStruct((tokens, experts), F32),
        ),
        (H // HB,),
        [
            columns(tokens),
            columns(tokens),
            columns(tokens),
            per_head(),
            per_head(),
            columns(1),
            pl.BlockSpec((HEADS, experts), lambda i: (i, 0)),
            whole(ids.shape),
        ],
        (columns(tokens), columns(tokens), whole((tokens, experts))),
        scratch=[pltpu.VMEM((tokens, experts), F32)],
        flops=2 * tokens * D * 4 * DH,
        moved=2 * D * 8 * tokens,
    )(q, k, v, prior, earlier, gain, router, ids)


def router_kernel(*refs):
    z_ref, dg_ref, pick_ref, sig_ref, *more_refs, dlog_ref, term_ref = refs
    tokens, experts = sig_ref.shape

    @pl.when(pl.program_id(0) == 0)
    def _():
        sig = sig_ref[...]
        both = mm_tn(pick_ref[:, :tokens], dg_ref[...])
        for ref in more_refs:
            both += ref[...].astype(F32)
        dg = both[:, :experts] + both[:, experts : 2 * experts]
        total = jnp.sum(sig, axis=1, keepdims=True)
        mean = jnp.sum(sig * dg, axis=1, keepdims=True) / total
        dlog = sig * (1.0 - sig) * (dg - mean) / total
        for i, part in enumerate(thirds(dlog)):
            dlog_ref[i] = part

    z = z_ref[...]
    term_ref[...] = mm_tn(dlog_ref[0], z) + mm_tn(dlog_ref[1], z) + mm_tn(dlog_ref[2], z)


def router_gradient(z, back, more, pick, sig):
    tokens, experts = sig.shape
    rows = pick.shape[0]
    wide = lanes_of(2 * experts)
    return call(
        router_kernel,
        (
            jax.ShapeDtypeStruct((3, tokens, experts), BF16),
            jax.ShapeDtypeStruct((experts, D), F32),
        ),
        (D // WIDTH,),
        [
            columns(tokens, WIDTH),
            whole((rows, wide)),
            whole(pick.shape),
            whole(sig.shape),
        ]
        + [whole((tokens, wide))] * len(more),
        (whole((3, tokens, experts)), columns(experts, WIDTH)),
        flops=6 * tokens * experts * D,
        moved=2 * tokens * D,
    )(z, back, pick, sig, *more)


def middle_kernel(*refs):
    q_ref, att_ref, dy_ref, back_ref, pick_ref, dlog_ref, gain_ref, router_ref, rterm_ref = refs[:9]
    *more_refs, datt_ref, term_ref = refs[9:]
    experts = router_ref.shape[1]
    per = HB // term_ref.shape[0]
    tokens = q_ref.shape[0]
    router = router_ref[...]
    dz = dy_ref[...].astype(F32) + mm_tn(pick_ref[:, :tokens], back_ref[...])
    for ref in more_refs:
        dz += ref[...].astype(F32)
    for i in range(3):
        dz += mm_nt(dlog_ref[i], router)
    weighted = dz * gain_ref[...]
    for h in range(HB):
        att, w = att_ref[:, head(h)], weighted[:, head(h)]
        mean = jnp.mean(att * att, axis=1, keepdims=True) + EPS
        inner = jnp.sum(w * att, axis=1, keepdims=True)
        datt = ((w - att * (inner / (DH * mean))) / jnp.sqrt(mean)).astype(BF16)
        datt_ref[:, head(h)] = datt
        to, i = h // per, h % per
        term_ref[to, head(i)] = mm_tn(q_ref[:, head(h)], datt).astype(BF16)
        high, low = halves(rterm_ref[:, head(h)])
        at = per * DH + i * experts
        term_ref[to, at : at + experts] = high
        term_ref[to, at + per * experts : at + per * experts + experts] = low


def attention_middle(q, att, dy, back, more, pick, dlog, gain, router, rterm, n):
    tokens, rows, experts = q.shape[0], pick.shape[0], router.shape[1]
    per = H // n
    length = per * (DH + 2 * experts)
    return call(
        middle_kernel,
        (
            jax.ShapeDtypeStruct((tokens, D), BF16),
            jax.ShapeDtypeStruct((n, length, DH), BF16),
        ),
        (H // HB,),
        [
            columns(tokens),
            columns(tokens),
            columns(tokens),
            columns(rows),
            whole(pick.shape),
            whole(dlog.shape),
            columns(1),
            pl.BlockSpec((HEADS, experts), lambda i: (i, 0)),
            columns(experts),
        ]
        + [columns(tokens)] * len(more),
        (columns(tokens), pl.BlockSpec((HB // per, length, DH), lambda i: (i, 0, 0))),
        flops=2 * tokens * D * (DH + rows + 3 * experts),
        moved=2 * D * (8 * tokens + rows),
    )(q, att, dy, back, pick, dlog, gain, router, rterm, *more)


def early_kernel(q_ref, k_ref, v_ref, datt_ref, prior_ref, earlier_ref, gq_ref, gk_ref, gv_ref):
    causal = causal_mask(q_ref.shape[0])
    for h in range(HB):
        q, k, v = q_ref[:, head(h)], k_ref[:, head(h)], v_ref[:, head(h)]
        datt = datt_ref[:, head(h)]
        high, low = halves(prior_ref[h] + earlier_ref[h].astype(F32))
        dscores = jnp.where(causal, mm_nt(datt, v), 0.0).astype(BF16)
        scores = jnp.where(causal, mm_nt(q, k), 0.0).astype(BF16)
        gq = mm(dscores, k) + mm_nt(datt, high) + mm_nt(datt, low)
        gq_ref[:, head(h)] = gq.astype(BF16)
        gk_ref[:, head(h)] = mm_tn(dscores, q)
        gv_ref[:, head(h)] = mm_tn(scores, datt)


def attention_early(q, k, v, datt, prior, earlier):
    tokens = q.shape[0]
    block = columns(tokens)
    return call(
        early_kernel,
        (
            jax.ShapeDtypeStruct((tokens, D), BF16),
            jax.ShapeDtypeStruct((tokens, D), F32),
            jax.ShapeDtypeStruct((tokens, D), F32),
        ),
        (H // HB,),
        [block, block, block, block, per_head(), per_head()],
        (block, block, block),
        flops=2 * tokens * D * DH * 7,
        moved=22 * D * tokens,
    )(q, k, v, datt, prior, earlier)


def late_kernel(k_ref, v_ref, later_ref, gk_ref, gv_ref, out_k_ref, out_v_ref, router_ref):
    experts = router_ref.shape[1]
    per = HB // later_ref.shape[0]
    for h in range(HB):
        to, i = h // per, h % per
        later = later_ref[to, head(i)]
        out_k_ref[:, head(h)] = (gk_ref[:, head(h)] + mm_nt(v_ref[:, head(h)], later)).astype(BF16)
        out_v_ref[:, head(h)] = (gv_ref[:, head(h)] + mm(k_ref[:, head(h)], later)).astype(BF16)
        at = per * DH + i * experts
        high = later_ref[to, at : at + experts].astype(F32)
        low = later_ref[to, at + per * experts : at + per * experts + experts].astype(F32)
        router_ref[head(h)] = (high + low).T


def attention_late(k, v, later, gk, gv, experts):
    tokens = k.shape[0]
    block = columns(tokens)
    out = jax.ShapeDtypeStruct((tokens, D), BF16)
    n, length, _ = later.shape
    return call(
        late_kernel,
        (out, out, jax.ShapeDtypeStruct((D, experts), F32)),
        (H // HB,),
        [
            block,
            block,
            pl.BlockSpec((HB * n // H, length, DH), lambda i: (i, 0, 0)),
            block,
            block,
        ],
        (block, block, pl.BlockSpec((HEADS, experts), lambda i: (i, 0))),
        flops=2 * tokens * D * DH * 2,
        moved=18 * D * tokens,
    )(k, v, later, gk, gv)


def output_kernel(z_ref, pick_ref, back_ref, *refs):
    *more_refs, out_ref = refs
    tokens = z_ref.shape[0]
    total = z_ref[...].astype(F32) + mm_tn(pick_ref[:, :tokens], back_ref[...])
    for ref in more_refs:
        total += ref[...].astype(F32)
    out_ref[...] = total.astype(BF16)


def layer_output(z, pick, back, more):
    tokens, rows = z.shape[0], pick.shape[0]
    return call(
        output_kernel,
        jax.ShapeDtypeStruct((tokens, D), BF16),
        (D // HEADS,),
        [columns(tokens), whole(pick.shape), columns(rows)] + [columns(tokens)] * len(more),
        columns(tokens),
        flops=2 * tokens * D * rows,
        moved=2 * D * rows,
    )(z, pick, back, *more)


def down_kernel(dy_ref, down_ref, out_ref):
    out_ref[...] = mm_nt(dy_ref[...], down_ref[...])


def expert_down_back(dy_rows, down_mat):
    rows, hidden = dy_rows.shape[0], down_mat.shape[0]
    tile = 256
    return call(
        down_kernel,
        jax.ShapeDtypeStruct((rows, hidden), F32),
        (hidden // tile,),
        [
            pl.BlockSpec((rows, D), lambda i: (0, 0)),
            pl.BlockSpec((tile, D), lambda i: (i, 0)),
        ],
        columns(rows, tile),
        flops=2 * rows * hidden * D,
        moved=2 * (rows + hidden) * D,
    )(dy_rows, down_mat)


def expert_kernel(
    me_ref, z_ref, mask_ref, router_ref, gate_ref, up_ref, dh_ref,
    hid_ref, dgp_ref, dup_ref, weight_ref, pair_ref, dg_ref,
):
    experts = router_ref.shape[1]

    @pl.when(pl.program_id(0) == 0)
    def _():
        sig = jax.nn.sigmoid(mm(z_ref[...], router_ref[...]))
        sig *= mask_ref[:, :experts].astype(F32)
        total = jnp.sum(sig, axis=1, keepdims=True)
        lane = lax.broadcasted_iota(jnp.int32, sig.shape, 1)
        mine = jnp.sum(jnp.where(lane == me_ref[0, 0], sig, 0.0), axis=1, keepdims=True)
        some = total > 0
        weight_ref[...] = jnp.where(some, mine / jnp.where(some, total, 1.0), 0.0)
        dg_ref[...] = jnp.zeros_like(dg_ref)

    z = z_ref[...]
    gp = mm(z, gate_ref[...])
    up = mm(z, up_ref[...])
    gs = jax.nn.sigmoid(gp)
    hid = (gp * gs * up).astype(BF16)
    plain = dh_ref[...]
    dg_ref[...] += jnp.sum(plain * hid.astype(F32), axis=1, keepdims=True)
    dh = plain * weight_ref[...]
    hid_ref[...] = hid
    dgp_ref[...] = (dh * up * gs * (1.0 + gp * (1.0 - gs))).astype(BF16)
    dup_ref[...] = (dh * gp * gs).astype(BF16)

    @pl.when(pl.program_id(0) == pl.num_programs(0) - 1)
    def _():
        lane = lax.broadcasted_iota(jnp.int32, pair_ref.shape, 1)
        dg = dg_ref[...]
        high = dg.astype(BF16).astype(F32)
        pair = jnp.where(lane == me_ref[0, 0], high, 0.0)
        pair = jnp.where(lane == me_ref[0, 0] + experts, dg - high, pair)
        pair_ref[...] = pair.astype(BF16)


def expert_forward(me, z_rows, dy_rows, router, gate_mat, up_mat, dh_plain):
    rows, hidden, experts = z_rows.shape[0], gate_mat.shape[1], router.shape[1]
    tile, wide = 256, lanes_of(experts)
    beside = D // wide
    inner = jax.ShapeDtypeStruct((rows, hidden), BF16)
    column = jax.ShapeDtypeStruct((rows, 1), F32)
    pair = jax.ShapeDtypeStruct((rows, lanes_of(2 * experts)), BF16)
    return call(
        expert_kernel,
        (inner, inner, inner, column, pair),
        (hidden // tile,),
        [
            smem(),
            whole((rows, D)),
            pl.BlockSpec((rows, wide), lambda i: (0, beside)),
            whole(router.shape),
            columns(D, tile),
            columns(D, tile),
            columns(rows, tile),
        ],
        (columns(rows, tile),) * 3 + (whole((rows, 1)), whole(pair.shape)),
        scratch=[pltpu.VMEM((rows, 1), F32)],
        flops=4 * rows * hidden * D,
        moved=2 * (rows + 2 * hidden) * D,
    )(me, z_rows, dy_rows, router, gate_mat, up_mat, dh_plain)


def back_kernel(dgp_ref, dup_ref, gate_ref, up_ref, weight_ref, out_ref):
    total = mm_nt(dgp_ref[...], gate_ref[...]) + mm_nt(dup_ref[...], up_ref[...])
    out_ref[...] = (total * weight_ref[...]).astype(BF16)


def expert_back(dgp, dup, gate_mat, up_mat, weight):
    rows, hidden = dgp.shape
    stripe = pl.BlockSpec((WIDTH, hidden), lambda i: (i, 0))
    return call(
        back_kernel,
        jax.ShapeDtypeStruct((rows, D), BF16),
        (D // WIDTH,),
        [whole(dgp.shape), whole(dup.shape), stripe, stripe, whole((rows, 1))],
        columns(rows, WIDTH),
        flops=4 * rows * hidden * D,
        moved=2 * (rows + 2 * hidden) * D,
    )(dgp, dup, gate_mat, up_mat, weight)


def product_kernel(hid_ref, down_ref, weight_ref, out_ref):
    out_ref[...] = (mm(hid_ref[...], down_ref[...]) * weight_ref[...]).astype(BF16)


def expert_product(hid, down_mat, weight):
    rows, hidden = hid.shape
    return call(
        product_kernel,
        jax.ShapeDtypeStruct((rows, D), BF16),
        (D // WIDTH,),
        [whole(hid.shape), columns(hidden, WIDTH), whole((rows, 1))],
        columns(rows, WIDTH),
        flops=2 * rows * hidden * D,
        moved=2 * (rows + hidden) * D,
    )(hid, down_mat, weight)


def weights_kernel(
    z_ref, dy_ref, hid_ref, dgp_ref, dup_ref, weight_ref, gate_ref, up_ref, down_ref
):
    z = z_ref[...]
    gate_ref[...] = mm_tn(z, dgp_ref[...]).astype(BF16)
    up_ref[...] = mm_tn(z, dup_ref[...]).astype(BF16)
    de = (dy_ref[...].astype(F32) * weight_ref[...]).astype(BF16)
    down_ref[...] = mm_tn(hid_ref[...], de).astype(BF16)


def expert_weights(z_rows, dy_rows, hid, dgp, dup, weight):
    rows, hidden = hid.shape
    stripe = pl.BlockSpec((WIDTH, hidden), lambda i: (i, 0))
    return call(
        weights_kernel,
        (
            jax.ShapeDtypeStruct((D, hidden), BF16),
            jax.ShapeDtypeStruct((D, hidden), BF16),
            jax.ShapeDtypeStruct((hidden, D), BF16),
        ),
        (D // WIDTH,),
        [columns(rows, WIDTH), columns(rows, WIDTH)] + [whole(hid.shape)] * 3 + [whole((rows, 1))],
        (stripe, stripe, columns(hidden, WIDTH)),
        flops=6 * rows * hidden * D,
        moved=2 * (2 * rows + 3 * hidden) * D,
    )(z_rows, dy_rows, hid, dgp, dup, weight)


def exchange(rows):
    group = lax.axis_size("ctx")
    shaped = rows.reshape(group, rows.shape[0] // group, rows.shape[1])
    moved = lax.all_to_all(shaped, "ctx", split_axis=0, concat_axis=0, tiled=True)
    return moved.reshape(rows.shape)


def after(value, *earlier):
    return lax.optimization_barrier((value, *earlier))[0]


def swap(block, axis, by=1):
    return lax.ppermute(block, axis, [(i, i ^ by) for i in range(lax.axis_size(axis))])


def peers():
    return [(b % 2, b // 2) for b in range(2 * lax.axis_size("near"))]


def replicate(block, *gate):
    far = swap(block, "far")
    near = range(1, lax.axis_size("near"))
    own = [swap(block, "near", n) for n in near]
    gated = after(far, *gate) if gate else far
    other = [swap(gated, "near", n) for n in near]
    return [block, far] + [x for pair in zip(own, other) for x in pair]


def collect_far(parts):
    far = parts[0]
    near = range(1, lax.axis_size("near"))
    if len(near):
        arrived = [swap(parts[2 * n], "near", n) for n in near]
        far = sum((a.astype(F32) for a in arrived), far.astype(F32)).astype(BF16)
    return far


def collect(parts, far):
    near = range(1, lax.axis_size("near"))
    return [swap(far, "far")] + [swap(parts[2 * n - 1], "near", n) for n in near]


def collect_small(parts):
    near = lax.axis_size("near")
    steps = peers()[1:]
    return [swap(part, ("far", "near"), f * near + n) for part, (f, n) in zip(parts, steps)]


def doublings():
    steps = []
    for axis in ("far", "near"):
        by = 1
        while by < lax.axis_size(axis):
            steps.append((axis, by))
            by *= 2
    return steps


def sum_over(term, steps, gate):
    for axis, by in steps:
        term = term + after(swap(term, axis, by), gate)
    return term


def local(
    queries,
    keys,
    values,
    prior_state,
    norm_gain,
    router_weight,
    expert_ids,
    w_gate,
    w_up,
    w_down,
    cotangent,
):
    q, k, v, dy = queries[0], keys[0], values[0], cotangent[0]
    tokens = q.shape[0]
    experts = router_weight.shape[1]
    cap = max(2, 3 * tokens * TOPK // (2 * experts))
    gate_mat, up_mat, down_mat = w_gate[0], w_up[0], w_down[0]
    prior = prior_state[0]
    gain = norm_gain.reshape(1, D)
    me = jnp.stack([lax.axis_index(ALL), jnp.int32(experts)]).reshape(1, 2).astype(jnp.int32)
    plane = lax.axis_index(("far", "near")).reshape(1, 1).astype(jnp.int32)
    rows = experts * cap

    n = lax.axis_size("ctx")
    ids = expert_ids[0]
    beside = jnp.pad(ids.astype(BF16), ((0, 0), (0, 128 - TOPK)))
    terms = state_terms(k, v).reshape(n, H // n * DH, DH)
    here = to_heads(terms)
    sums = running_sum(here, False)
    dy_blocks = replicate(jnp.concatenate([dy, beside], axis=1), sums)
    earlier = to_heads(sums).reshape(H, DH, DH)
    z, att, sig = attention_forward(q, k, v, prior, earlier, gain, router_weight, ids)
    z_blocks = replicate(z)
    pick, chosen = route(plane, after(dy_blocks, z), experts, rows, cap)
    dy_rows = exchange(gather(pick, chosen, dy_blocks, True))
    z_rows = exchange(gather(pick, chosen, z_blocks, False))

    dh_plain = expert_down_back(dy_rows, down_mat)
    hid, dgp, dup, weight, dg_send = expert_forward(
        me, z_rows, dy_rows, router_weight, gate_mat, up_mat, dh_plain
    )
    dg_back = exchange(dg_send)
    dz_send = expert_back(dgp, dup, gate_mat, up_mat, weight)
    dz_back = exchange(dz_send)
    dg_more = collect_small(partials(pick, after(dg_back, dz_send), tokens))
    dlog, rterm = router_gradient(z, dg_back, dg_more, pick, sig)
    eo_send = expert_product(after(hid, dlog), down_mat, weight)
    steps = doublings()
    rterm = sum_over(rterm, steps[:1], eo_send)
    grad_gate, grad_up, grad_down = expert_weights(
        after(z_rows, rterm), dy_rows, hid, dgp, dup, weight
    )
    rterm = sum_over(rterm, steps[1:], grad_gate)

    dz_parts = partials(pick, after(dz_back, rterm), tokens)
    dz_far = collect_far(dz_parts)
    dz_more = collect(dz_parts, dz_far)
    eo_back = exchange(after(eo_send, *dz_parts))
    eo_parts = partials(pick, after(eo_back, dz_far), tokens)
    datt, dterms = attention_middle(
        q, att, dy, dz_back, after(dz_more, *eo_parts), pick, dlog, gain, router_weight, rterm, n
    )
    there = to_heads(dterms)
    gq, gk, gv = attention_early(q, k, v, datt, prior, earlier)
    eo_more = collect(eo_parts, collect_far(eo_parts))
    later = to_heads(running_sum(there, True))
    grad_k, grad_v, grad_router = attention_late(k, v, later, gk, gv, experts)
    output = layer_output(z, pick, eo_back, eo_more)
    return (
        output[None],
        gq[None],
        grad_k[None],
        grad_v[None],
        grad_gate[None],
        grad_up[None],
        grad_down[None],
        grad_router,
    )


def solution(mesh):
    tokens = P(("far", "near"), "ctx", None)
    weights = P(ALL, None, None)
    split = Mesh(
        mesh.devices.reshape(2, mesh.shape["dp"] // 2, mesh.shape["ctx"]), ("far", "near", "ctx")
    )
    placed = (
        tokens,
        tokens,
        tokens,
        P(("far", "near"), None, None, None),
        P(),
        P(),
        tokens,
        weights,
        weights,
        weights,
        tokens,
    )
    return jax.shard_map(
        local,
        mesh=split,
        in_specs=placed,
        out_specs=(tokens, tokens, tokens, tokens, weights, weights, weights, P()),
        check_vma=False,
    )
```

time: 453 us -> 349 us (0.77)
  blocking collectives: 89.7 us -> 0 us
  Pallas kernels: 27 us -> 107 us
  matrix products: 58.5 us -> 0 us
  waiting for transfers between devices: 194 us -> 161 us
  local copies, waits for them, and re-layouts: 37.6 us -> 16.4 us
  starting transfers between devices: 40.7 us -> 57.7 us
    all_to_all x10 -> x9, waiting for transfers between devices: 194 us -> 76.7 us  [the longest x5 49.4 us: exchange(): lax.all_to_all(shaped, 'ctx', split_axis=0, concat_axis=0, tiled=True)]
    all_to_all x2 -> x0, blocking collectives: 89.7 us -> none  [the longest x1 75.9 us: exchange(): moved = lax.all_to_all(shaped, ALL, split_axis=0, concat_axis=0, tiled=True)]
    ppermute x0 -> x17, waiting for transfers between devices: none -> 84.7 us  [swap(): lax.ppermute(block, axis, [(i, i ^ by) for i in range(lax.axis_size(axis))])]
    pallas_call x5 -> x16, Pallas kernels: 9.93 us -> 86.5 us  [the longest x1 12.3 us: expert_forward(): call(expert_kernel, (inner, inner, inner, column, pair), (hidden // tile,...]
    dot_general x10 -> x0, matrix products: 58.5 us -> none  [the longest x4 20.5 us: mm(): return jnp.dot(a, b, preferred_element_type=F32)]
    ppermute x0 -> x17, starting transfers between devices: none -> 23 us  [swap(): lax.ppermute(block, axis, [(i, i ^ by) for i in range(lax.axis_size(axis))])]
    unnamed x102 -> x57, local copies, waits for them, and re-layouts: 35.7 us -> 16.4 us
    all_to_all x10 -> x9, starting transfers between devices: 40.7 us -> 34.6 us  [the longest x5 19.9 us: exchange(): lax.all_to_all(shaped, 'ctx', split_axis=0, concat_axis=0, tiled=True)]
  transfers between devices with their start and end apart: 10 -> 26, of which waited for: 9 -> 15; matrix products, arithmetic and copies ran while one was open for 10% -> 1% of each run, Pallas kernels for 6% -> 21%
where the time goes in v2:
time: 349 us; the launch traced here: 348 us
  waiting for transfers between devices  161 us (46%)
  Pallas kernels  107 us (31%)
  starting transfers between devices  57.7 us (17%)
  local copies, waits for them, and re-layouts  16.4 us (5%)
  other arithmetic  4.57 us (1%)
    ppermute x17, waiting for transfers between devices, swap(): lax.ppermute(block, axis, [(i, i ^ by) for i in range(lax.axis_size(axis))])  84.7 us
    all_to_all x5, waiting for transfers between devices, exchange(): lax.all_to_all(shaped, 'ctx', split_axis=0, concat_axis=0, tiled=True)  49.4 us
    all_to_all x4, waiting for transfers between devices, to_heads(): return lax.all_to_all(block, 'ctx', split_axis=0, concat_axis=0, tiled=True)  27.3 us
    ppermute x17, starting transfers between devices, swap(): lax.ppermute(block, axis, [(i, i ^ by) for i in range(lax.axis_size(axis))])  23 us
    all_to_all x5, starting transfers between devices, exchange(): lax.all_to_all(shaped, 'ctx', split_axis=0, concat_axis=0, tiled=True)  19.9 us
    unnamed x57, local copies, waits for them, and re-layouts  16.4 us
    all_to_all x4, starting transfers between devices, to_heads(): return lax.all_to_all(block, 'ctx', split_axis=0, concat_axis=0, tiled=True)  14.7 us
    pallas_call x1, Pallas kernels, expert_forward(): call(expert_kernel, (inner, inner, inner, column, pair), (hidden // tile,...  12.3 us
  transfers between devices with their start and end apart: 26, of which 15 were waited for; matrix products, arithmetic and copies ran while one was open for 1% of the time, Pallas kernels for 21%

profile of v2, /device:TPU:0, one launch (start us, length us, event | category | flops | bytes accessed | tf_op | source)
XLA Modules:
  0.0 347.7 jit_solution(4780511915047965359)
XLA Ops:
  2.6 4.1 %collective-permute-start = (bf16[128,2176]{1,0:T(8,128)(2,1)S(1)}, bf16[128,2176]{1,0:T(8,128)(2,1)S(1)}, u32[]{:S(2)}, u32[]{:S(2)}) collective-permute-start(bf16[128,2176]{1,0:T(8,128)(2,1)S(1)} %fusion.1.refs_0_), channel_id=1, source_target_pairs={{0,16},{16,0},{1,17},{17,1},{2,18},{18,2},{3,19},{19,3},{4,20},{20... | collective-permute-start | bytes 1671176 | tf_op jit(solution)/shard_map/ppermute | solution.py:655
  6.7 2.3 shard_map.170
  9.0 3.7 %all-to-all-start = ((bf16[8,256,128]{2,1,0:T(8,128)(2,1)}), bf16[8,256,128]{2,1,0:T(8,128)(2,1)S(1)}, u32[]{:S(2)}, u32[]{:S(2)}) async-start(bf16[8,256,128]{2,1,0:T(8,128)(2,1)} %bitcast.61), calls=%async_computation | async-start | bytes 1048576 | tf_op jit(solution)/shard_map/all_to_all | solution.py:225
  14.3 8.2 %all-to-all-done.in_ref = bf16[8,256,128]{2,1,0:T(8,128)(2,1)S(1)} async-done(((bf16[8,256,128]{2,1,0:T(8,128)(2,1)}), bf16[8,256,128]{2,1,0:T(8,128)(2,1)S(1)}, u32[]{:S(2)}, u32[]{:S(2)}) %all-to-all-start) | async-done | bytes 524320 | tf_op jit(solution)/shard_map/all_to_all | solution.py:225
  25.2 6.2 %collective-permute-done.refs_1_ = bf16[128,2176]{1,0:T(8,128)(2,1)S(1)} collective-permute-done((bf16[128,2176]{1,0:T(8,128)(2,1)S(1)}, bf16[128,2176]{1,0:T(8,128)(2,1)S(1)}, u32[]{:S(2)}, u32[]{:S(2)}) %collective-permute-start) | collective-permute-done | bytes 557088 | tf_op jit(solution)/shard_map/ppermute | solution.py:655
  32.0 3.7 %all-to-all-start.1 = ((bf16[8,256,128]{2,1,0:T(8,128)(2,1)}), bf16[8,256,128]{2,1,0:T(8,128)(2,1)S(1)}, u32[]{:S(2)}, u32[]{:S(2)}) async-start(bf16[8,256,128]{2,1,0:T(8,128)(2,1)} %shard_map.171), calls=%async_computation.1 | async-start | bytes 1048576 | tf_op jit(solution)/shard_map/all_to_all | solution.py:225
  36.8 8.7 %all-to-all-done.1 = bf16[8,256,128]{2,1,0:T(8,128)(2,1)S(1)} async-done(((bf16[8,256,128]{2,1,0:T(8,128)(2,1)}), bf16[8,256,128]{2,1,0:T(8,128)(2,1)S(1)}, u32[]{:S(2)}, u32[]{:S(2)}) %all-to-all-start.1) | async-done | bytes 524320 | tf_op jit(solution)/shard_map/all_to_all | solution.py:225
  46.3 5.3 %shard_map.172 = (bf16[128,2048]{1,0:T(8,128)(2,1)}, f32[128,2048]{1,0:T(8,128)}, f32[128,32]{1,0:T(8,128)}) custom-call(bf16[128,2048]{1,0:T(8,128)(2,1)} %bitcast.48, bf16[128,2048]{1,0:T(8,128)(2,1)} %bitcast.41, bf16[128,2048]{1,0:T(8,128)(2,1)} %bitcast.45, f32[16,128,128]{2,1,0:T(8,128)} %bitcast.53, bf16[16,128,128]{2,1,0:T(8,128)(2,1)} %bitcast.51, ...), custom_call_target="tpu_custom_call" | custom-call | flops 268435456 | bytes 4194304 | tf_op jit(solution)/shard_map/pallas_call | solution.py:276
  52.6 2.7 shard_map.173
  55.3 5.6 %shard_map.175 = bf16[768,2176]{1,0:T(8,128)(2,1)} custom-call(bf16[768,512]{1,0:T(8,128)(2,1)} %get-tuple-element.61.pick_ref.refs_2_.refs_4_, f32[512,32]{1,0:T(8,128)} %get-tuple-element.62.chosen_ref, bf16[128,2176]{1,0:T(8,128)(2,1)} %copy-done.2, bf16[128,2176]{1,0:T(8,128)(2,1)} %copy-done.8, bf16[128,2176]{1,0:T(8,128)(2,1)} %copy-done.9, ...), custom_call_target="tpu_custom_call" | custom-call | flops 1610612736 | bytes 3145728 | tf_op jit(solution)/shard_map/pallas_call | solution.py:153
  60.9 4.6 %all-to-all-start.3 = ((bf16[8,96,2176]{2,1,0:T(8,128)(2,1)}), bf16[8,96,2176]{2,1,0:T(8,128)(2,1)}, u32[]{:S(2)}, u32[]{:S(2)}) async-start(bf16[8,96,2176]{2,1,0:T(8,128)(2,1)} %bitcast.34), calls=%async_computation.3 | async-start | bytes 6684672 | tf_op jit(solution)/shard_map/all_to_all | solution.py:646
  65.5 3.5 %collective-permute-start.3 = (bf16[128,2048]{1,0:T(8,128)(2,1)S(1)}, bf16[128,2048]{1,0:T(8,128)(2,1)S(1)}, u32[]{:S(2)}, u32[]{:S(2)}) collective-permute-start(bf16[128,2048]{1,0:T(8,128)(2,1)S(1)} %copy-done.3), channel_id=1, source_target_pairs={{0,16},{16,0},{1,17},{17,1},{2,18},{18,2},{3,19},{19,3},{4,20},{20... | collective-permute-start | bytes 1572872 | tf_op jit(solution)/shard_map/ppermute | solution.py:655
  69.1 23.7 %collective-permute-done.3.refs_1_ = bf16[128,2048]{1,0:T(8,128)(2,1)S(1)} collective-permute-done((bf16[128,2048]{1,0:T(8,128)(2,1)S(1)}, bf16[128,2048]{1,0:T(8,128)(2,1)S(1)}, u32[]{:S(2)}, u32[]{:S(2)}) %collective-permute-start.3) | collective-permute-done | bytes 524320 | tf_op jit(solution)/shard_map/ppermute | solution.py:655
  94.0 12.5 %collective-permute-done.5.refs_3_ = bf16[128,2048]{1,0:T(8,128)(2,1)S(1)} collective-permute-done((bf16[128,2048]{1,0:T(8,128)(2,1)S(1)}, bf16[128,2048]{1,0:T(8,128)(2,1)S(1)}, u32[]{:S(2)}, u32[]{:S(2)}) %collective-permute-start.5) | collective-permute-done | bytes 524320 | tf_op jit(solution)/shard_map/ppermute | solution.py:655
  107.3 5.3 %shard_map.174 = bf16[768,2048]{1,0:T(8,128)(2,1)} custom-call(bf16[768,512]{1,0:T(8,128)(2,1)} %get-tuple-element.61.pick_ref.refs_2_.refs_4_, f32[512,32]{1,0:T(8,128)} %get-tuple-element.62.chosen_ref, bf16[128,2048]{1,0:T(8,128)(2,1)} %get-tuple-element.55.refs_0_.z_ref, bf16[128,2048]{1,0:T(8,128)(2,1)} %copy-done.17, bf16[128,2048]{1,0:T(8,128)(2,1)} %copy-done.18, ...), custom_call_target="tpu_custom_call" | custom-call | flops 1610612736 | bytes 3145728 | tf_op jit(solution)/shard_map/pallas_call | solution.py:153
  112.6 4.0 %all-to-all-start.2 = ((bf16[8,96,2048]{2,1,0:T(8,128)(2,1)}), bf16[8,96,2048]{2,1,0:T(8,128)(2,1)S(1)}, u32[]{:S(2)}, u32[]{:S(2)}) async-start(bf16[8,96,2048]{2,1,0:T(8,128)(2,1)} %bitcast.39), calls=%async_computation.2 | async-start | bytes 6291456 | tf_op jit(solution)/shard_map/all_to_all | solution.py:646
  117.2 6.6 %shard_map.176.dh_ref = f32[768,768]{1,0:T(8,128)} custom-call(bf16[768,2176]{1,0:T(8,128)(2,1)} %bitcast.15.dy_ref.mask_ref, bf16[768,2048]{1,0:T(8,128)(2,1)} %bitcast.73), custom_call_target="tpu_custom_call" | custom-call | flops 2415919104 | bytes 6291456 | tf_op jit(solution)/shard_map/pallas_call | solution.py:499
  123.8 30.7 %all-to-all-done.2 = bf16[8,96,2048]{2,1,0:T(8,128)(2,1)S(1)} async-done(((bf16[8,96,2048]{2,1,0:T(8,128)(2,1)}), bf16[8,96,2048]{2,1,0:T(8,128)(2,1)S(1)}, u32[]{:S(2)}, u32[]{:S(2)}) %all-to-all-start.2) | async-done | bytes 3145760 | tf_op jit(solution)/shard_map/all_to_all | solution.py:646
  156.1 12.3 %shard_map.177 = (bf16[768,768]{1,0:T(8,128)(2,1)}, bf16[768,768]{1,0:T(8,128)(2,1)}, bf16[768,768]{1,0:T(8,128)(2,1)}, f32[768,1]{1,0:T(8,128)}, bf16[768,128]{1,0:T(8,128)(2,1)}) custom-call(s32[1,2]{1,0:T(1,128)} %add_bitcast_fusion.me_ref, bf16[768,2048]{1,0:T(8,128)(2,1)} %bitcast.55, bf16[768,2176]{1,0:T(8,128)(2,1)} %bitcast.15.dy_ref.mask_ref, ...), custom_call_target="tpu_custom_call" | custom-call | flops 4831838208 | bytes 9437184 | tf_op jit(solution)/shard_map/pallas_call | solution.py:559
  168.4 3.4 all-to-all-start.4
  171.9 9.1 %shard_map.178 = bf16[768,2048]{1,0:T(8,128)(2,1)} custom-call(bf16[768,768]{1,0:T(8,128)(2,1)} %get-tuple-element.66.dgp_ref, bf16[768,768]{1,0:T(8,128)(2,1)} %get-tuple-element.67.dup_ref, bf16[2048,768]{1,0:T(8,128)(2,1)} %bitcast.70, bf16[2048,768]{1,0:T(8,128)(2,1)} %bitcast.72, f32[768,1]{1,0:T(8,128)} %get-tuple-element.68.weight_ref), custom_call_target="tpu_custom_call" | custom-call | flops 4831838208 | bytes 9437184 | tf_op jit(solution)/shard_map/pallas_call | solution.py:587
  181.7 4.1 %all-to-all-start.5 = ((bf16[8,96,2048]{2,1,0:T(8,128)(2,1)}), bf16[8,96,2048]{2,1,0:T(8,128)(2,1)S(1)}, u32[]{:S(2)}, u32[]{:S(2)}) async-start(bf16[8,96,2048]{2,1,0:T(8,128)(2,1)} %bitcast.57), calls=%async_computation.5 | async-start | bytes 6291456 | tf_op jit(solution)/shard_map/all_to_all | solution.py:646
  185.8 2.1 shard_map.179
  189.9 2.4 collective-permute-start.8
  193.4 2.5 collective-permute-done.8.refs_6_
  196.5 4.3 %shard_map.180 = (bf16[3,128,32]{2,1,0:T(8,128)(2,1)}, f32[32,2048]{1,0:T(8,128)}) custom-call(bf16[128,2048]{1,0:T(8,128)(2,1)} %get-tuple-element.55.refs_0_.z_ref, bf16[768,128]{1,0:T(8,128)(2,1)} %bitcast.63, bf16[768,512]{1,0:T(8,128)(2,1)} %get-tuple-element.61.pick_ref.refs_2_.refs_4_, f32[128,32]{1,0:T(8,128)} %get-tuple-element.65.refs_3_, ...), custom_call_target="tpu_custom_call" | custom-call | flops 50331648 | bytes 524288 | tf_op jit(solution)/shard_map/pallas_call | solution.py:326
  200.8 6.4 %shard_map.181 = bf16[768,2048]{1,0:T(8,128)(2,1)} custom-call(bf16[768,768]{1,0:T(8,128)(2,1)} %get-tuple-element.74.hid_ref, bf16[768,2048]{1,0:T(8,128)(2,1)} %bitcast.74, f32[768,1]{1,0:T(8,128)} %get-tuple-element.68.weight_ref), custom_call_target="tpu_custom_call" | custom-call | flops 2415919104 | bytes 6291456 | tf_op jit(solution)/shard_map/pallas_call | solution.py:604
  207.2 7.0 %collective-permute-done.9 = f32[32,2048]{1,0:T(8,128)S(1)} collective-permute-done((f32[32,2048]{1,0:T(8,128)}, f32[32,2048]{1,0:T(8,128)S(1)}, u32[]{:S(2)}, u32[]{:S(2)}) %collective-permute-start.9) | collective-permute-done | bytes 262176 | tf_op jit(solution)/shard_map/ppermute | solution.py:655
  214.4 11.8 %shard_map.182 = (bf16[2048,768]{1,0:T(8,128)(2,1)}, bf16[2048,768]{1,0:T(8,128)(2,1)}, bf16[768,2048]{1,0:T(8,128)(2,1)}) custom-call(bf16[768,2048]{1,0:T(8,128)(2,1)} %bitcast.56, bf16[768,2176]{1,0:T(8,128)(2,1)} %bitcast.15.dy_ref.mask_ref, bf16[768,768]{1,0:T(8,128)(2,1)} %get-tuple-element.74.hid_ref, bf16[768,768]{1,0:T(8,128)(2,1)} %get-tuple-element.66.dgp_ref, ...), custom_call_target="tpu_custom_call" | custom-call | flops 7247757312 | bytes 15728640 | tf_op jit(solution)/shard_map/pallas_call | solution.py:628
  228.7 4.4 %shard_map.183 = (bf16[128,2048]{1,0:T(8,128)(2,1)}, bf16[128,2048]{1,0:T(8,128)(2,1)}, bf16[128,2048]{1,0:T(8,128)(2,1)}) custom-call(bf16[768,512]{1,0:T(8,128)(2,1)} %get-tuple-element.61.pick_ref.refs_2_.refs_4_, bf16[768,2048]{1,0:T(8,128)(2,1)} %bitcast.35), custom_call_target="tpu_custom_call" | custom-call | flops 1207959552 | bytes 3145728 | tf_op jit(solution)/shard_map/pallas_call | solution.py:177
  233.1 3.8 %all-to-all-start.6 = ((bf16[8,96,2048]{2,1,0:T(8,128)(2,1)}), bf16[8,96,2048]{2,1,0:T(8,128)(2,1)S(1)}, u32[]{:S(2)}, u32[]{:S(2)}) async-start(bf16[8,96,2048]{2,1,0:T(8,128)(2,1)} %bitcast.58), calls=%async_computation.6 | async-start | bytes 6291456 | tf_op jit(solution)/shard_map/all_to_all | solution.py:646
  239.0 13.0 %collective-permute-done.11 = bf16[128,2048]{1,0:T(8,128)(2,1)S(1)} collective-permute-done((bf16[128,2048]{1,0:T(8,128)(2,1)}, bf16[128,2048]{1,0:T(8,128)(2,1)S(1)}, u32[]{:S(2)}, u32[]{:S(2)}) %collective-permute-start.11) | collective-permute-done | bytes 524320 | tf_op jit(solution)/shard_map/ppermute | solution.py:655
  251.9 2.0 add_convert_fusion.1
  253.9 2.2 collective-permute-start.15
  256.1 18.7 %all-to-all-done.6 = bf16[8,96,2048]{2,1,0:T(8,128)(2,1)S(1)} async-done(((bf16[8,96,2048]{2,1,0:T(8,128)(2,1)}), bf16[8,96,2048]{2,1,0:T(8,128)(2,1)S(1)}, u32[]{:S(2)}, u32[]{:S(2)}) %all-to-all-start.6) | async-done | bytes 3145760 | tf_op jit(solution)/shard_map/all_to_all | solution.py:646
  276.5 4.4 %shard_map.184 = (bf16[128,2048]{1,0:T(8,128)(2,1)}, bf16[128,2048]{1,0:T(8,128)(2,1)}, bf16[128,2048]{1,0:T(8,128)(2,1)}) custom-call(bf16[768,512]{1,0:T(8,128)(2,1)} %get-tuple-element.61.pick_ref.refs_2_.refs_4_, bf16[768,2048]{1,0:T(8,128)(2,1)} %bitcast.37), custom_call_target="tpu_custom_call" | custom-call | flops 1207959552 | bytes 3145728 | tf_op jit(solution)/shard_map/pallas_call | solution.py:177
  280.9 6.1 %shard_map.186 = (bf16[128,2048]{1,0:T(8,128)(2,1)}, bf16[8,384,128]{2,1,0:T(8,128)(2,1)}) custom-call(bf16[128,2048]{1,0:T(8,128)(2,1)} %bitcast.49, f32[128,2048]{1,0:T(8,128)} %get-tuple-element.89.refs_1_, bf16[128,2048]{1,0:T(8,128)(2,1)} %bitcast.60, bf16[768,2048]{1,0:T(8,128)(2,1)} %bitcast.36, ...), custom_call_target="tpu_custom_call" | custom-call | flops 520093696 | bytes 7340032 | tf_op jit(solution)/shard_map/pallas_call | solution.py:377
  287.0 3.7 %all-to-all-start.7 = ((bf16[8,384,128]{2,1,0:T(8,128)(2,1)}), bf16[8,384,128]{2,1,0:T(8,128)(2,1)S(1)}, u32[]{:S(2)}, u32[]{:S(2)}) async-start(bf16[8,384,128]{2,1,0:T(8,128)(2,1)} %get-tuple-element.94), calls=%async_computation.7 | async-start | bytes 1572864 | tf_op jit(solution)/shard_map/all_to_all | solution.py:225
  290.7 2.0 collective-permute-start.12
  292.8 10.4 %all-to-all-done.7.in_ref = bf16[8,384,128]{2,1,0:T(8,128)(2,1)S(1)} async-done(((bf16[8,384,128]{2,1,0:T(8,128)(2,1)}), bf16[8,384,128]{2,1,0:T(8,128)(2,1)S(1)}, u32[]{:S(2)}, u32[]{:S(2)}) %all-to-all-start.7) | async-done | bytes 786464 | tf_op jit(solution)/shard_map/all_to_all | solution.py:225
  304.1 2.1 shard_map.188
  306.2 3.5 %all-to-all-start.8 = ((bf16[8,384,128]{2,1,0:T(8,128)(2,1)}), bf16[8,384,128]{2,1,0:T(8,128)(2,1)S(1)}, u32[]{:S(2)}, u32[]{:S(2)}) async-start(bf16[8,384,128]{2,1,0:T(8,128)(2,1)} %shard_map.188), calls=%async_computation.8 | async-start | bytes 1572864 | tf_op jit(solution)/shard_map/all_to_all | solution.py:225
  309.9 2.4 collective-permute-start.13
  312.3 6.6 %shard_map.187 = (bf16[128,2048]{1,0:T(8,128)(2,1)}, f32[128,2048]{1,0:T(8,128)}, f32[128,2048]{1,0:T(8,128)}) custom-call(bf16[128,2048]{1,0:T(8,128)(2,1)} %bitcast.50, bf16[128,2048]{1,0:T(8,128)(2,1)} %bitcast.42, bf16[128,2048]{1,0:T(8,128)(2,1)} %bitcast.46, bf16[128,2048]{1,0:T(8,128)(2,1)} %get-tuple-element.92.datt_ref, f32[16,128,128]{2,1,0:T(8,128)} %bitcast.54, ...), custom_call_target="tpu_custom_call" | custom-call | flops 469762048 | bytes 5767168 | tf_op jit(solution)/shard_map/pallas_call | solution.py:419
  320.4 16.0 %collective-permute-done.13.refs_0_ = bf16[128,2048]{1,0:T(8,128)(2,1)S(1)} collective-permute-done((bf16[128,2048]{1,0:T(8,128)(2,1)S(1)}, bf16[128,2048]{1,0:T(8,128)(2,1)S(1)}, u32[]{:S(2)}, u32[]{:S(2)}) %collective-permute-start.13) | collective-permute-done | bytes 524320 | tf_op jit(solution)/shard_map/ppermute | solution.py:655
  337.2 3.9 %shard_map.185 = bf16[128,2048]{1,0:T(8,128)(2,1)} custom-call(bf16[128,2048]{1,0:T(8,128)(2,1)} %get-tuple-element.55.refs_0_.z_ref, bf16[768,512]{1,0:T(8,128)(2,1)} %get-tuple-element.61.pick_ref.refs_2_.refs_4_, bf16[768,2048]{1,0:T(8,128)(2,1)} %bitcast.38, bf16[128,2048]{1,0:T(8,128)(2,1)} %copy-done.16, bf16[128,2048]{1,0:T(8,128)(2,1)} %copy-done.15), custom_call_target="tpu_custom_call" | custom-call | flops 402653184 | bytes 3145728 | tf_op jit(solution)/shard_map/pallas_call | solution.py:481
  342.0 3.4 shard_map.189
  345.4 2.2 copy.23
  (88 shorter events, 28.9 us)
Async XLA Ops:
  0.6 35.1 %copy-start.21 = (bf16[2048,32]{0,1:T(8,128)(2,1)S(1)}, bf16[2048,32]{0,1:T(8,128)(2,1)}, u32[]{:S(2)}) copy-start(bf16[2048,32]{0,1:T(8,128)(2,1)} %param.16) | copy-start | bytes 393220
  1.5 35.3 %copy-start.13 = (s32[1,128,4]{2,1,0:T(8,128)}, s32[1,128,4]{2,1,0:T(8,128)S(1)}, u32[]{:S(2)}) copy-start(s32[1,128,4]{2,1,0:T(8,128)S(1)} %copy.19) | copy-start | bytes 6148
  2.6 49.0 %copy-start.2 = (bf16[128,2176]{1,0:T(8,128)(2,1)}, bf16[128,2176]{1,0:T(8,128)(2,1)S(1)}, u32[]{:S(2)}) copy-start(bf16[128,2176]{1,0:T(8,128)(2,1)S(1)} %fusion.1.refs_0_) | copy-start | bytes 1671172
  2.6 28.8 %collective-permute-start = (bf16[128,2176]{1,0:T(8,128)(2,1)S(1)}, bf16[128,2176]{1,0:T(8,128)(2,1)S(1)}, u32[]{:S(2)}, u32[]{:S(2)}) collective-permute-start(bf16[128,2176]{1,0:T(8,128)(2,1)S(1)} %fusion.1.refs_0_), channel_id=1, source_target_pairs={{0,16},{16,0},{1,17},{17,1},{2,18},{18,2},{3,19},{19,3},{4,20},{20... | collective-permute-start | bytes 1671176 | tf_op jit(solution)/shard_map/ppermute | solution.py:655
  9.0 13.5 %all-to-all-start = ((bf16[8,256,128]{2,1,0:T(8,128)(2,1)}), bf16[8,256,128]{2,1,0:T(8,128)(2,1)S(1)}, u32[]{:S(2)}, u32[]{:S(2)}) async-start(bf16[8,256,128]{2,1,0:T(8,128)(2,1)} %bitcast.61), calls=%async_computation | async-start | bytes 1048576 | tf_op jit(solution)/shard_map/all_to_all | solution.py:225
  12.7 38.9 %collective-permute-start.1 = (bf16[128,2176]{1,0:T(8,128)(2,1)S(1)}, bf16[128,2176]{1,0:T(8,128)(2,1)S(1)}, u32[]{:S(2)}, u32[]{:S(2)}) collective-permute-start(bf16[128,2176]{1,0:T(8,128)(2,1)S(1)} %fusion.1.refs_0_), channel_id=1, source_target_pairs={{0,8},{8,0},{1,9},{9,1},{2,10},{10,2},{3,11},{11,3},{4,12},{12,4},... | collective-permute-start | bytes 1671176 | tf_op jit(solution)/shard_map/ppermute | solution.py:655
  31.4 20.3 %copy-start.8 = (bf16[128,2176]{1,0:T(8,128)(2,1)}, bf16[128,2176]{1,0:T(8,128)(2,1)S(1)}, u32[]{:S(2)}) copy-start(bf16[128,2176]{1,0:T(8,128)(2,1)S(1)} %collective-permute-done.refs_1_) | copy-start | bytes 1671172
  31.4 20.3 %collective-permute-start.2 = (bf16[128,2176]{1,0:T(8,128)(2,1)S(1)}, bf16[128,2176]{1,0:T(8,128)(2,1)S(1)}, u32[]{:S(2)}, u32[]{:S(2)}) collective-permute-start(bf16[128,2176]{1,0:T(8,128)(2,1)S(1)} %collective-permute-done.refs_1_), channel_id=1, source_target_pairs={{0,8},{8,0},{1,9},{9,1},{2,10},{10,2},{3,11},{11,3},{4,12},{12,4},... | collective-permute-start | bytes 1671176 | tf_op jit(solution)/shard_map/ppermute | solution.py:655
  32.0 13.5 %all-to-all-start.1 = ((bf16[8,256,128]{2,1,0:T(8,128)(2,1)}), bf16[8,256,128]{2,1,0:T(8,128)(2,1)S(1)}, u32[]{:S(2)}, u32[]{:S(2)}) async-start(bf16[8,256,128]{2,1,0:T(8,128)(2,1)} %shard_map.171), calls=%async_computation.1 | async-start | bytes 1048576 | tf_op jit(solution)/shard_map/all_to_all | solution.py:225
  51.6 0.8 copy-start.9
  51.7 1.0 copy-start.10
  60.9 4.6 %copy-start.3 = (bf16[128,2048]{1,0:T(8,128)(2,1)S(1)}, bf16[128,2048]{1,0:T(8,128)(2,1)}, u32[]{:S(2)}) copy-start(bf16[128,2048]{1,0:T(8,128)(2,1)} %get-tuple-element.55.refs_0_.z_ref) | copy-start | bytes 1572868
  60.9 51.7 %all-to-all-start.3 = ((bf16[8,96,2176]{2,1,0:T(8,128)(2,1)}), bf16[8,96,2176]{2,1,0:T(8,128)(2,1)}, u32[]{:S(2)}, u32[]{:S(2)}) async-start(bf16[8,96,2176]{2,1,0:T(8,128)(2,1)} %bitcast.34), calls=%async_computation.3 | async-start | bytes 6684672 | tf_op jit(solution)/shard_map/all_to_all | solution.py:646
  65.5 27.2 %collective-permute-start.3 = (bf16[128,2048]{1,0:T(8,128)(2,1)S(1)}, bf16[128,2048]{1,0:T(8,128)(2,1)S(1)}, u32[]{:S(2)}, u32[]{:S(2)}) collective-permute-start(bf16[128,2048]{1,0:T(8,128)(2,1)S(1)} %copy-done.3), channel_id=1, source_target_pairs={{0,16},{16,0},{1,17},{17,1},{2,18},{18,2},{3,19},{19,3},{4,20},{20... | collective-permute-start | bytes 1572872 | tf_op jit(solution)/shard_map/ppermute | solution.py:655
  69.0 24.9 %collective-permute-start.4 = (bf16[128,2048]{1,0:T(8,128)(2,1)S(1)}, bf16[128,2048]{1,0:T(8,128)(2,1)S(1)}, u32[]{:S(2)}, u32[]{:S(2)}) collective-permute-start(bf16[128,2048]{1,0:T(8,128)(2,1)S(1)} %copy-done.3), channel_id=1, source_target_pairs={{0,8},{8,0},{1,9},{9,1},{2,10},{10,2},{3,11},{11,3},{4,12},{12,4},... | collective-permute-start | bytes 1572872 | tf_op jit(solution)/shard_map/ppermute | solution.py:655
  92.8 13.7 %copy-start.17 = (bf16[128,2048]{1,0:T(8,128)(2,1)}, bf16[128,2048]{1,0:T(8,128)(2,1)S(1)}, u32[]{:S(2)}) copy-start(bf16[128,2048]{1,0:T(8,128)(2,1)S(1)} %collective-permute-done.3.refs_1_) | copy-start | bytes 1572868
  92.8 13.7 %collective-permute-start.5 = (bf16[128,2048]{1,0:T(8,128)(2,1)S(1)}, bf16[128,2048]{1,0:T(8,128)(2,1)S(1)}, u32[]{:S(2)}, u32[]{:S(2)}) collective-permute-start(bf16[128,2048]{1,0:T(8,128)(2,1)S(1)} %collective-permute-done.3.refs_1_), channel_id=1, source_target_pairs={{0,8},{8,0},{1,9},{9,1},{2,10},{10,2},{3,11},{11,3},{4,12},{12,4},... | collective-permute-start | bytes 1572872 | tf_op jit(solution)/shard_map/ppermute | solution.py:655
  94.0 12.5 %copy-start.18 = (bf16[128,2048]{1,0:T(8,128)(2,1)}, bf16[128,2048]{1,0:T(8,128)(2,1)S(1)}, u32[]{:S(2)}) copy-start(bf16[128,2048]{1,0:T(8,128)(2,1)S(1)} %collective-permute-done.4.refs_2_) | copy-start | bytes 1572868
  106.5 0.8 copy-start.19
  112.6 41.9 %all-to-all-start.2 = ((bf16[8,96,2048]{2,1,0:T(8,128)(2,1)}), bf16[8,96,2048]{2,1,0:T(8,128)(2,1)S(1)}, u32[]{:S(2)}, u32[]{:S(2)}) async-start(bf16[8,96,2048]{2,1,0:T(8,128)(2,1)} %bitcast.39), calls=%async_computation.2 | async-start | bytes 6291456 | tf_op jit(solution)/shard_map/all_to_all | solution.py:646
  154.5 1.7 copy-start.5
  168.4 12.6 %all-to-all-start.4 = ((bf16[8,96,128]{2,1,0:T(8,128)(2,1)}), bf16[8,96,128]{2,1,0:T(8,128)(2,1)S(1)}, u32[]{:S(2)}, u32[]{:S(2)}) async-start(bf16[8,96,128]{2,1,0:T(8,128)(2,1)} %bitcast.66), calls=%async_computation.4 | async-start | bytes 393216 | tf_op jit(solution)/shard_map/all_to_all | solution.py:646
  181.7 45.3 %all-to-all-start.5 = ((bf16[8,96,2048]{2,1,0:T(8,128)(2,1)}), bf16[8,96,2048]{2,1,0:T(8,128)(2,1)S(1)}, u32[]{:S(2)}, u32[]{:S(2)}) async-start(bf16[8,96,2048]{2,1,0:T(8,128)(2,1)} %bitcast.57), calls=%async_computation.5 | async-start | bytes 6291456 | tf_op jit(solution)/shard_map/all_to_all | solution.py:646
  187.9 5.4 %collective-permute-start.6 = (bf16[128,128]{1,0:T(8,128)(2,1)}, bf16[128,128]{1,0:T(8,128)(2,1)S(1)}, u32[]{:S(2)}, u32[]{:S(2)}) collective-permute-start(bf16[128,128]{1,0:T(8,128)(2,1)} %get-tuple-element.70), channel_id=1, source_target_pairs={{0,16},{8,24},{16,0},{24,8},{1,17},{9,25},{17,1},{25,9},{2,18},{10... | collective-permute-start | bytes 98312 | tf_op jit(solution)/shard_map/ppermute | solution.py:655
  188.2 5.2 %collective-permute-start.7 = (bf16[128,128]{1,0:T(8,128)(2,1)}, bf16[128,128]{1,0:T(8,128)(2,1)S(1)}, u32[]{:S(2)}, u32[]{:S(2)}) collective-permute-start(bf16[128,128]{1,0:T(8,128)(2,1)} %get-tuple-element.71), channel_id=1, source_target_pairs={{0,8},{8,0},{16,24},{24,16},{1,9},{9,1},{17,25},{25,17},{2,10},{10... | collective-permute-start | bytes 98312 | tf_op jit(solution)/shard_map/ppermute | solution.py:655
  189.9 5.9 %collective-permute-start.8 = (bf16[128,128]{1,0:T(8,128)(2,1)}, bf16[128,128]{1,0:T(8,128)(2,1)S(1)}, u32[]{:S(2)}, u32[]{:S(2)}) collective-permute-start(bf16[128,128]{1,0:T(8,128)(2,1)} %get-tuple-element.72), channel_id=1, source_target_pairs={{0,24},{8,16},{16,8},{24,0},{1,25},{9,17},{17,9},{25,1},{2,26},{10... | collective-permute-start | bytes 98312 | tf_op jit(solution)/shard_map/ppermute | solution.py:655
  193.4 2.5 copy-start.22
  193.4 2.5 copy-start.23
  200.8 13.5 %collective-permute-start.9 = (f32[32,2048]{1,0:T(8,128)}, f32[32,2048]{1,0:T(8,128)S(1)}, u32[]{:S(2)}, u32[]{:S(2)}) collective-permute-start(f32[32,2048]{1,0:T(8,128)} %get-tuple-element.75), channel_id=1, source_target_pairs={{0,16},{16,0},{1,17},{17,1},{2,18},{18,2},{3,19},{19,3},{4,20},{20... | collective-permute-start | bytes 786440 | tf_op jit(solution)/shard_map/ppermute | solution.py:655
  200.8 13.5 %copy-start.20 = (f32[32,2048]{1,0:T(8,128)S(1)}, f32[32,2048]{1,0:T(8,128)}, u32[]{:S(2)}) copy-start(f32[32,2048]{1,0:T(8,128)} %get-tuple-element.75) | copy-start | bytes 786436
  214.3 11.9 %collective-permute-start.10 = (f32[32,2048]{1,0:T(8,128)S(1)}, f32[32,2048]{1,0:T(8,128)S(1)}, u32[]{:S(2)}, u32[]{:S(2)}) collective-permute-start(f32[32,2048]{1,0:T(8,128)S(1)} %add.26), channel_id=1, source_target_pairs={{0,8},{8,0},{1,9},{9,1},{2,10},{10,2},{3,11},{11,3},{4,12},{12,4},... | collective-permute-start | bytes 786440 | tf_op jit(solution)/shard_map/ppermute | solution.py:655
  227.0 1.7 copy-start
  233.1 41.7 %all-to-all-start.6 = ((bf16[8,96,2048]{2,1,0:T(8,128)(2,1)}), bf16[8,96,2048]{2,1,0:T(8,128)(2,1)S(1)}, u32[]{:S(2)}, u32[]{:S(2)}) async-start(bf16[8,96,2048]{2,1,0:T(8,128)(2,1)} %bitcast.58), calls=%async_computation.6 | async-start | bytes 6291456 | tf_op jit(solution)/shard_map/all_to_all | solution.py:646
  236.9 15.0 %collective-permute-start.11 = (bf16[128,2048]{1,0:T(8,128)(2,1)}, bf16[128,2048]{1,0:T(8,128)(2,1)S(1)}, u32[]{:S(2)}, u32[]{:S(2)}) collective-permute-start(bf16[128,2048]{1,0:T(8,128)(2,1)} %get-tuple-element.83), channel_id=1, source_target_pairs={{0,8},{8,0},{1,9},{9,1},{2,10},{10,2},{3,11},{11,3},{4,12},{12,4},... | collective-permute-start | bytes 1572872 | tf_op jit(solution)/shard_map/ppermute | solution.py:655
  238.9 42.0 %collective-permute-start.16 = (bf16[128,2048]{1,0:T(8,128)(2,1)}, bf16[128,2048]{1,0:T(8,128)(2,1)}, u32[]{:S(2)}, u32[]{:S(2)}) collective-permute-start(bf16[128,2048]{1,0:T(8,128)(2,1)} %get-tuple-element.82), channel_id=1, source_target_pairs={{0,8},{8,0},{1,9},{9,1},{2,10},{10,2},{3,11},{11,3},{4,12},{12,4},... | collective-permute-start | bytes 1572872 | tf_op jit(solution)/shard_map/ppermute | solution.py:655
  253.9 27.0 %collective-permute-start.15 = (bf16[128,2048]{1,0:T(8,128)(2,1)}, bf16[128,2048]{1,0:T(8,128)(2,1)}, u32[]{:S(2)}, u32[]{:S(2)}) collective-permute-start(bf16[128,2048]{1,0:T(8,128)(2,1)} %add_convert_fusion.1), channel_id=1, source_target_pairs={{0,16},{16,0},{1,17},{17,1},{2,18},{18,2},{3,19},{19,3},{4,20},{20... | collective-permute-start | bytes 1572872 | tf_op jit(solution)/shard_map/ppermute | solution.py:655
  274.8 1.7 copy-start.1
  280.9 9.8 %copy-start.26 = (bf16[128,2048]{1,0:T(8,128)(2,1)S(1)}, bf16[128,2048]{1,0:T(8,128)(2,1)}, u32[]{:S(2)}) copy-start(bf16[128,2048]{1,0:T(8,128)(2,1)} %get-tuple-element.87) | copy-start | bytes 1572868
  280.9 11.9 %copy-start.25 = (bf16[128,2048]{1,0:T(8,128)(2,1)S(1)}, bf16[128,2048]{1,0:T(8,128)(2,1)}, u32[]{:S(2)}) copy-start(bf16[128,2048]{1,0:T(8,128)(2,1)} %get-tuple-element.88) | copy-start | bytes 1572868
  287.0 22.8 %copy-start.14 = (bf16[128,2048]{1,0:T(8,128)(2,1)S(1)}, bf16[128,2048]{1,0:T(8,128)(2,1)}, u32[]{:S(2)}) copy-start(bf16[128,2048]{1,0:T(8,128)(2,1)} %get-tuple-element.86) | copy-start | bytes 1572868
  287.0 16.2 %all-to-all-start.7 = ((bf16[8,384,128]{2,1,0:T(8,128)(2,1)}), bf16[8,384,128]{2,1,0:T(8,128)(2,1)S(1)}, u32[]{:S(2)}, u32[]{:S(2)}) async-start(bf16[8,384,128]{2,1,0:T(8,128)(2,1)} %get-tuple-element.94), calls=%async_computation.7 | async-start | bytes 1572864 | tf_op jit(solution)/shard_map/all_to_all | solution.py:225
  290.7 19.1 %collective-permute-start.12 = (bf16[128,2048]{1,0:T(8,128)(2,1)S(1)}, bf16[128,2048]{1,0:T(8,128)(2,1)S(1)}, u32[]{:S(2)}, u32[]{:S(2)}) collective-permute-start(bf16[128,2048]{1,0:T(8,128)(2,1)S(1)} %copy-done.26), channel_id=1, source_target_pairs={{0,8},{8,0},{1,9},{9,1},{2,10},{10,2},{3,11},{11,3},{4,12},{12,4},... | collective-permute-start | bytes 1572872 | tf_op jit(solution)/shard_map/ppermute | solution.py:655
  292.7 27.7 %collective-permute-start.14 = (bf16[128,2048]{1,0:T(8,128)(2,1)S(1)}, bf16[128,2048]{1,0:T(8,128)(2,1)S(1)}, u32[]{:S(2)}, u32[]{:S(2)}) collective-permute-start(bf16[128,2048]{1,0:T(8,128)(2,1)S(1)} %copy-done.25), channel_id=1, source_target_pairs={{0,8},{8,0},{1,9},{9,1},{2,10},{10,2},{3,11},{11,3},{4,12},{12,4},... | collective-permute-start | bytes 1572872 | tf_op jit(solution)/shard_map/ppermute | solution.py:655
  303.2 0.9 copy-start.6
  306.2 34.9 %all-to-all-start.8 = ((bf16[8,384,128]{2,1,0:T(8,128)(2,1)}), bf16[8,384,128]{2,1,0:T(8,128)(2,1)S(1)}, u32[]{:S(2)}, u32[]{:S(2)}) async-start(bf16[8,384,128]{2,1,0:T(8,128)(2,1)} %shard_map.188), calls=%async_computation.8 | async-start | bytes 1572864 | tf_op jit(solution)/shard_map/all_to_all | solution.py:225
  309.9 26.5 %collective-permute-start.13 = (bf16[128,2048]{1,0:T(8,128)(2,1)S(1)}, bf16[128,2048]{1,0:T(8,128)(2,1)S(1)}, u32[]{:S(2)}, u32[]{:S(2)}) collective-permute-start(bf16[128,2048]{1,0:T(8,128)(2,1)S(1)} %add_convert_fusion), channel_id=1, source_target_pairs={{0,16},{16,0},{1,17},{17,1},{2,18},{18,2},{3,19},{19,3},{4,20},{20... | collective-permute-start | bytes 1572872 | tf_op jit(solution)/shard_map/ppermute | solution.py:655
  320.4 16.0 %copy-start.15 = (bf16[128,2048]{1,0:T(8,128)(2,1)}, bf16[128,2048]{1,0:T(8,128)(2,1)S(1)}, u32[]{:S(2)}) copy-start(bf16[128,2048]{1,0:T(8,128)(2,1)S(1)} %collective-permute-done.14.refs_1_) | copy-start | bytes 1572868
  341.1 0.9 copy-start.7
  (5 other events, 3.7 us)

commit v3 on v2

--- a/solution.py
+++ b/solution.py
@@ -432,7 +432,7 @@
 
 
 def late_kernel(k_ref, v_ref, later_ref, gk_ref, gv_ref, out_k_ref, out_v_ref, router_ref):
-    experts = router_ref.shape[1]
+    experts = router_ref.shape[0]
     per = HB // later_ref.shape[0]
     for h in range(HB):
         to, i = h // per, h % per
@@ -442,7 +442,7 @@
         at = per * DH + i * experts
         high = later_ref[to, at : at + experts].astype(F32)
         low = later_ref[to, at + per * experts : at + per * experts + experts].astype(F32)
-        router_ref[head(h)] = (high + low).T
+        router_ref[:, head(h)] = high + low
 
 
 def attention_late(k, v, later, gk, gv, experts):
@@ -452,7 +452,7 @@
     n, length, _ = later.shape
     return call(
         late_kernel,
-        (out, out, jax.ShapeDtypeStruct((D, experts), F32)),
+        (out, out, jax.ShapeDtypeStruct((experts, D), F32)),
         (H // HB,),
         [
             block,
@@ -461,7 +461,7 @@
             block,
             block,
         ],
-        (block, block, pl.BlockSpec((HEADS, experts), lambda i: (i, 0))),
+        (block, block, columns(experts)),
         flops=2 * tokens * D * DH * 2,
         moved=18 * D * tokens,
     )(k, v, later, gk, gv)
@@ -763,15 +763,16 @@
     dz_far = collect_far(dz_parts)
     dz_more = collect(dz_parts, dz_far)
     eo_back = exchange(after(eo_send, *dz_parts))
-    eo_parts = partials(pick, after(eo_back, dz_far), tokens)
     datt, dterms = attention_middle(
-        q, att, dy, dz_back, after(dz_more, *eo_parts), pick, dlog, gain, router_weight, rterm, n
+        q, att, dy, dz_back, dz_more, pick, dlog, gain, router_weight, rterm, n
     )
     there = to_heads(dterms)
-    gq, gk, gv = attention_early(q, k, v, datt, prior, earlier)
+    eo_parts = partials(pick, after(eo_back, datt), tokens)
     eo_more = collect(eo_parts, collect_far(eo_parts))
+    gq, gk, gv = attention_early(q, k, v, after(datt, *eo_parts), prior, earlier)
     later = to_heads(running_sum(there, True))
     grad_k, grad_v, grad_router = attention_late(k, v, later, gk, gv, experts)
+    grad_router = grad_router.T
     output = layer_output(z, pick, eo_back, eo_more)
     return (
         output[None],

time: 349 us -> 341 us (0.977)
  local copies, waits for them, and re-layouts: 16.4 us -> 11.7 us
    all_to_all x5, waiting for transfers between devices: 49.4 us -> 30.7 us  [exchange(): lax.all_to_all(shaped, 'ctx', split_axis=0, concat_axis=0, tiled=True)]
    ppermute x17, waiting for transfers between devices: 84.7 us -> 101 us  [swap(): lax.ppermute(block, axis, [(i, i ^ by) for i in range(lax.axis_size(axis))])]
    unnamed x57 -> x54, local copies, waits for them, and re-layouts: 16.4 us -> 11.7 us
  transfers between devices with their start and end apart: 26 -> 26, of which waited for: 15 -> 18; matrix products, arithmetic and copies ran while one was open for 1% -> 1% of each run, Pallas kernels for 21% -> 23%
where the time goes in v3:
time: 341 us; the launch traced here: 339 us
  waiting for transfers between devices  160 us (47%)
  Pallas kernels  107 us (31%)
  starting transfers between devices  55.8 us (16%)
  local copies, waits for them, and re-layouts  11.7 us (3%)
  other arithmetic  3.75 us (1%)
    ppermute x17, waiting for transfers between devices, swap(): lax.ppermute(block, axis, [(i, i ^ by) for i in range(lax.axis_size(axis))])  101 us
    all_to_all x5, waiting for transfers between devices, exchange(): lax.all_to_all(shaped, 'ctx', split_axis=0, concat_axis=0, tiled=True)  30.7 us
    all_to_all x4, waiting for transfers between devices, to_heads(): return lax.all_to_all(block, 'ctx', split_axis=0, concat_axis=0, tiled=True)  28.5 us
    ppermute x17, starting transfers between devices, swap(): lax.ppermute(block, axis, [(i, i ^ by) for i in range(lax.axis_size(axis))])  20.7 us
    all_to_all x5, starting transfers between devices, exchange(): lax.all_to_all(shaped, 'ctx', split_axis=0, concat_axis=0, tiled=True)  19.9 us
    all_to_all x4, starting transfers between devices, to_heads(): return lax.all_to_all(block, 'ctx', split_axis=0, concat_axis=0, tiled=True)  15.2 us
    pallas_call x1, Pallas kernels, expert_forward(): call(expert_kernel, (inner, inner, inner, column, pair), (hidden // tile,...  12.3 us
    pallas_call x1, Pallas kernels, expert_weights(): call(weights_kernel, (jax.ShapeDtypeStruct((D, hidden), BF16), jax.ShapeD...  11.8 us
  transfers between devices with their start and end apart: 26, of which 18 were waited for; matrix products, arithmetic and copies ran while one was open for 1% of the time, Pallas kernels for 23%

profile of v3, /device:TPU:0, one launch (start us, length us, event | category | flops | bytes accessed | tf_op | source)
XLA Modules:
  0.0 339.0 jit_solution(358013307371275402)
XLA Ops:
  2.6 4.1 %collective-permute-start = (bf16[128,2176]{1,0:T(8,128)(2,1)S(1)}, bf16[128,2176]{1,0:T(8,128)(2,1)S(1)}, u32[]{:S(2)}, u32[]{:S(2)}) collective-permute-start(bf16[128,2176]{1,0:T(8,128)(2,1)S(1)} %fusion.1.refs_0_), channel_id=1, source_target_pairs={{0,16},{16,0},{1,17},{17,1},{2,18},{18,2},{3,19},{19,3},{4,20},{20... | collective-permute-start | bytes 1671176 | tf_op jit(solution)/shard_map/ppermute | solution.py:655
  6.7 2.3 shard_map.170
  9.0 3.7 %all-to-all-start = ((bf16[8,256,128]{2,1,0:T(8,128)(2,1)}), bf16[8,256,128]{2,1,0:T(8,128)(2,1)S(1)}, u32[]{:S(2)}, u32[]{:S(2)}) async-start(bf16[8,256,128]{2,1,0:T(8,128)(2,1)} %bitcast.62), calls=%async_computation | async-start | bytes 1048576 | tf_op jit(solution)/shard_map/all_to_all | solution.py:225
  14.3 8.2 %all-to-all-done.in_ref = bf16[8,256,128]{2,1,0:T(8,128)(2,1)S(1)} async-done(((bf16[8,256,128]{2,1,0:T(8,128)(2,1)}), bf16[8,256,128]{2,1,0:T(8,128)(2,1)S(1)}, u32[]{:S(2)}, u32[]{:S(2)}) %all-to-all-start) | async-done | bytes 524320 | tf_op jit(solution)/shard_map/all_to_all | solution.py:225
  25.2 6.2 %collective-permute-done.refs_1_ = bf16[128,2176]{1,0:T(8,128)(2,1)S(1)} collective-permute-done((bf16[128,2176]{1,0:T(8,128)(2,1)S(1)}, bf16[128,2176]{1,0:T(8,128)(2,1)S(1)}, u32[]{:S(2)}, u32[]{:S(2)}) %collective-permute-start) | collective-permute-done | bytes 557088 | tf_op jit(solution)/shard_map/ppermute | solution.py:655
  32.0 3.7 %all-to-all-start.1 = ((bf16[8,256,128]{2,1,0:T(8,128)(2,1)}), bf16[8,256,128]{2,1,0:T(8,128)(2,1)S(1)}, u32[]{:S(2)}, u32[]{:S(2)}) async-start(bf16[8,256,128]{2,1,0:T(8,128)(2,1)} %shard_map.171), calls=%async_computation.1 | async-start | bytes 1048576 | tf_op jit(solution)/shard_map/all_to_all | solution.py:225
  36.8 8.7 %all-to-all-done.1 = bf16[8,256,128]{2,1,0:T(8,128)(2,1)S(1)} async-done(((bf16[8,256,128]{2,1,0:T(8,128)(2,1)}), bf16[8,256,128]{2,1,0:T(8,128)(2,1)S(1)}, u32[]{:S(2)}, u32[]{:S(2)}) %all-to-all-start.1) | async-done | bytes 524320 | tf_op jit(solution)/shard_map/all_to_all | solution.py:225
  46.3 5.3 %shard_map.172 = (bf16[128,2048]{1,0:T(8,128)(2,1)}, f32[128,2048]{1,0:T(8,128)}, f32[128,32]{1,0:T(8,128)}) custom-call(bf16[128,2048]{1,0:T(8,128)(2,1)} %bitcast.49, bf16[128,2048]{1,0:T(8,128)(2,1)} %bitcast.42, bf16[128,2048]{1,0:T(8,128)(2,1)} %bitcast.46, f32[16,128,128]{2,1,0:T(8,128)} %bitcast.54, bf16[16,128,128]{2,1,0:T(8,128)(2,1)} %bitcast.52, ...), custom_call_target="tpu_custom_call" | custom-call | flops 268435456 | bytes 4194304 | tf_op jit(solution)/shard_map/pallas_call | solution.py:276
  52.6 2.7 shard_map.173
  55.3 5.7 %shard_map.175 = bf16[768,2176]{1,0:T(8,128)(2,1)} custom-call(bf16[768,512]{1,0:T(8,128)(2,1)} %get-tuple-element.60.pick_ref.refs_2_.refs_4_, f32[512,32]{1,0:T(8,128)} %get-tuple-element.61.chosen_ref, bf16[128,2176]{1,0:T(8,128)(2,1)} %copy-done.2, bf16[128,2176]{1,0:T(8,128)(2,1)} %copy-done.7, bf16[128,2176]{1,0:T(8,128)(2,1)} %copy-done.8, ...), custom_call_target="tpu_custom_call" | custom-call | flops 1610612736 | bytes 3145728 | tf_op jit(solution)/shard_map/pallas_call | solution.py:153
  61.0 4.6 %all-to-all-start.3 = ((bf16[8,96,2176]{2,1,0:T(8,128)(2,1)}), bf16[8,96,2176]{2,1,0:T(8,128)(2,1)}, u32[]{:S(2)}, u32[]{:S(2)}) async-start(bf16[8,96,2176]{2,1,0:T(8,128)(2,1)} %bitcast.35), calls=%async_computation.3 | async-start | bytes 6684672 | tf_op jit(solution)/shard_map/all_to_all | solution.py:646
  65.6 3.5 %collective-permute-start.3 = (bf16[128,2048]{1,0:T(8,128)(2,1)S(1)}, bf16[128,2048]{1,0:T(8,128)(2,1)S(1)}, u32[]{:S(2)}, u32[]{:S(2)}) collective-permute-start(bf16[128,2048]{1,0:T(8,128)(2,1)S(1)} %copy-done.3), channel_id=1, source_target_pairs={{0,16},{16,0},{1,17},{17,1},{2,18},{18,2},{3,19},{19,3},{4,20},{20... | collective-permute-start | bytes 1572872 | tf_op jit(solution)/shard_map/ppermute | solution.py:655
  69.1 23.7 %collective-permute-done.3.refs_1_ = bf16[128,2048]{1,0:T(8,128)(2,1)S(1)} collective-permute-done((bf16[128,2048]{1,0:T(8,128)(2,1)S(1)}, bf16[128,2048]{1,0:T(8,128)(2,1)S(1)}, u32[]{:S(2)}, u32[]{:S(2)}) %collective-permute-start.3) | collective-permute-done | bytes 524320 | tf_op jit(solution)/shard_map/ppermute | solution.py:655
  94.0 12.5 %collective-permute-done.5.refs_3_ = bf16[128,2048]{1,0:T(8,128)(2,1)S(1)} collective-permute-done((bf16[128,2048]{1,0:T(8,128)(2,1)S(1)}, bf16[128,2048]{1,0:T(8,128)(2,1)S(1)}, u32[]{:S(2)}, u32[]{:S(2)}) %collective-permute-start.5) | collective-permute-done | bytes 524320 | tf_op jit(solution)/shard_map/ppermute | solution.py:655
  107.4 5.3 %shard_map.174 = bf16[768,2048]{1,0:T(8,128)(2,1)} custom-call(bf16[768,512]{1,0:T(8,128)(2,1)} %get-tuple-element.60.pick_ref.refs_2_.refs_4_, f32[512,32]{1,0:T(8,128)} %get-tuple-element.61.chosen_ref, bf16[128,2048]{1,0:T(8,128)(2,1)} %get-tuple-element.54.refs_0_.z_ref, bf16[128,2048]{1,0:T(8,128)(2,1)} %copy-done.17, bf16[128,2048]{1,0:T(8,128)(2,1)} %copy-done.18, ...), custom_call_target="tpu_custom_call" | custom-call | flops 1610612736 | bytes 3145728 | tf_op jit(solution)/shard_map/pallas_call | solution.py:153
  112.7 4.0 %all-to-all-start.2 = ((bf16[8,96,2048]{2,1,0:T(8,128)(2,1)}), bf16[8,96,2048]{2,1,0:T(8,128)(2,1)S(1)}, u32[]{:S(2)}, u32[]{:S(2)}) async-start(bf16[8,96,2048]{2,1,0:T(8,128)(2,1)} %bitcast.40), calls=%async_computation.2 | async-start | bytes 6291456 | tf_op jit(solution)/shard_map/all_to_all | solution.py:646
  117.2 6.6 %shard_map.176.dh_ref = f32[768,768]{1,0:T(8,128)} custom-call(bf16[768,2176]{1,0:T(8,128)(2,1)} %bitcast.15.dy_ref.mask_ref, bf16[768,2048]{1,0:T(8,128)(2,1)} %bitcast.74), custom_call_target="tpu_custom_call" | custom-call | flops 2415919104 | bytes 6291456 | tf_op jit(solution)/shard_map/pallas_call | solution.py:499
  123.9 30.7 %all-to-all-done.2 = bf16[8,96,2048]{2,1,0:T(8,128)(2,1)S(1)} async-done(((bf16[8,96,2048]{2,1,0:T(8,128)(2,1)}), bf16[8,96,2048]{2,1,0:T(8,128)(2,1)S(1)}, u32[]{:S(2)}, u32[]{:S(2)}) %all-to-all-start.2) | async-done | bytes 3145760 | tf_op jit(solution)/shard_map/all_to_all | solution.py:646
  156.2 12.3 %shard_map.177 = (bf16[768,768]{1,0:T(8,128)(2,1)}, bf16[768,768]{1,0:T(8,128)(2,1)}, bf16[768,768]{1,0:T(8,128)(2,1)}, f32[768,1]{1,0:T(8,128)}, bf16[768,128]{1,0:T(8,128)(2,1)}) custom-call(s32[1,2]{1,0:T(1,128)} %add_bitcast_fusion.me_ref, bf16[768,2048]{1,0:T(8,128)(2,1)} %bitcast.56, bf16[768,2176]{1,0:T(8,128)(2,1)} %bitcast.15.dy_ref.mask_ref, ...), custom_call_target="tpu_custom_call" | custom-call | flops 4831838208 | bytes 9437184 | tf_op jit(solution)/shard_map/pallas_call | solution.py:559
  168.5 3.4 %all-to-all-start.4 = ((bf16[8,96,128]{2,1,0:T(8,128)(2,1)}), bf16[8,96,128]{2,1,0:T(8,128)(2,1)S(1)}, u32[]{:S(2)}, u32[]{:S(2)}) async-start(bf16[8,96,128]{2,1,0:T(8,128)(2,1)} %bitcast.67), calls=%async_computation.4 | async-start | bytes 393216 | tf_op jit(solution)/shard_map/all_to_all | solution.py:646
  171.9 9.1 %shard_map.178 = bf16[768,2048]{1,0:T(8,128)(2,1)} custom-call(bf16[768,768]{1,0:T(8,128)(2,1)} %get-tuple-element.65.dgp_ref, bf16[768,768]{1,0:T(8,128)(2,1)} %get-tuple-element.66.dup_ref, bf16[2048,768]{1,0:T(8,128)(2,1)} %bitcast.71, bf16[2048,768]{1,0:T(8,128)(2,1)} %bitcast.73, f32[768,1]{1,0:T(8,128)} %get-tuple-element.67.weight_ref), custom_call_target="tpu_custom_call" | custom-call | flops 4831838208 | bytes 9437184 | tf_op jit(solution)/shard_map/pallas_call | solution.py:587
  181.7 4.1 %all-to-all-start.5 = ((bf16[8,96,2048]{2,1,0:T(8,128)(2,1)}), bf16[8,96,2048]{2,1,0:T(8,128)(2,1)S(1)}, u32[]{:S(2)}, u32[]{:S(2)}) async-start(bf16[8,96,2048]{2,1,0:T(8,128)(2,1)} %bitcast.58), calls=%async_computation.5 | async-start | bytes 6291456 | tf_op jit(solution)/shard_map/all_to_all | solution.py:646
  185.8 2.1 shard_map.179
  190.0 2.4 collective-permute-start.8
  193.4 2.5 collective-permute-done.8.refs_6_
  196.5 4.3 %shard_map.180 = (bf16[3,128,32]{2,1,0:T(8,128)(2,1)}, f32[32,2048]{1,0:T(8,128)}) custom-call(bf16[128,2048]{1,0:T(8,128)(2,1)} %get-tuple-element.54.refs_0_.z_ref, bf16[768,128]{1,0:T(8,128)(2,1)} %bitcast.64, bf16[768,512]{1,0:T(8,128)(2,1)} %get-tuple-element.60.pick_ref.refs_2_.refs_4_, f32[128,32]{1,0:T(8,128)} %get-tuple-element.64.refs_3_, ...), custom_call_target="tpu_custom_call" | custom-call | flops 50331648 | bytes 524288 | tf_op jit(solution)/shard_map/pallas_call | solution.py:326
  200.9 6.4 %shard_map.181 = bf16[768,2048]{1,0:T(8,128)(2,1)} custom-call(bf16[768,768]{1,0:T(8,128)(2,1)} %get-tuple-element.73.hid_ref, bf16[768,2048]{1,0:T(8,128)(2,1)} %bitcast.75, f32[768,1]{1,0:T(8,128)} %get-tuple-element.67.weight_ref), custom_call_target="tpu_custom_call" | custom-call | flops 2415919104 | bytes 6291456 | tf_op jit(solution)/shard_map/pallas_call | solution.py:604
  207.3 7.1 %collective-permute-done.9 = f32[32,2048]{1,0:T(8,128)S(1)} collective-permute-done((f32[32,2048]{1,0:T(8,128)}, f32[32,2048]{1,0:T(8,128)S(1)}, u32[]{:S(2)}, u32[]{:S(2)}) %collective-permute-start.9) | collective-permute-done | bytes 262176 | tf_op jit(solution)/shard_map/ppermute | solution.py:655
  214.5 11.8 %shard_map.182 = (bf16[2048,768]{1,0:T(8,128)(2,1)}, bf16[2048,768]{1,0:T(8,128)(2,1)}, bf16[768,2048]{1,0:T(8,128)(2,1)}) custom-call(bf16[768,2048]{1,0:T(8,128)(2,1)} %bitcast.57, bf16[768,2176]{1,0:T(8,128)(2,1)} %bitcast.15.dy_ref.mask_ref, bf16[768,768]{1,0:T(8,128)(2,1)} %get-tuple-element.73.hid_ref, bf16[768,768]{1,0:T(8,128)(2,1)} %get-tuple-element.65.dgp_ref, ...), custom_call_target="tpu_custom_call" | custom-call | flops 7247757312 | bytes 15728640 | tf_op jit(solution)/shard_map/pallas_call | solution.py:628
  228.8 4.4 %shard_map.183 = (bf16[128,2048]{1,0:T(8,128)(2,1)}, bf16[128,2048]{1,0:T(8,128)(2,1)}, bf16[128,2048]{1,0:T(8,128)(2,1)}) custom-call(bf16[768,512]{1,0:T(8,128)(2,1)} %get-tuple-element.60.pick_ref.refs_2_.refs_4_, bf16[768,2048]{1,0:T(8,128)(2,1)} %bitcast.36), custom_call_target="tpu_custom_call" | custom-call | flops 1207959552 | bytes 3145728 | tf_op jit(solution)/shard_map/pallas_call | solution.py:177
  233.2 3.8 %all-to-all-start.6 = ((bf16[8,96,2048]{2,1,0:T(8,128)(2,1)}), bf16[8,96,2048]{2,1,0:T(8,128)(2,1)S(1)}, u32[]{:S(2)}, u32[]{:S(2)}) async-start(bf16[8,96,2048]{2,1,0:T(8,128)(2,1)} %bitcast.59), calls=%async_computation.6 | async-start | bytes 6291456 | tf_op jit(solution)/shard_map/all_to_all | solution.py:646
  239.1 13.0 %collective-permute-done.11 = bf16[128,2048]{1,0:T(8,128)(2,1)S(1)} collective-permute-done((bf16[128,2048]{1,0:T(8,128)(2,1)}, bf16[128,2048]{1,0:T(8,128)(2,1)S(1)}, u32[]{:S(2)}, u32[]{:S(2)}) %collective-permute-start.11) | collective-permute-done | bytes 524320 | tf_op jit(solution)/shard_map/ppermute | solution.py:655
  253.2 2.2 collective-permute-start.12
  255.4 15.7 %collective-permute-done.13.refs_10_ = bf16[128,2048]{1,0:T(8,128)(2,1)S(1)} collective-permute-done((bf16[128,2048]{1,0:T(8,128)(2,1)}, bf16[128,2048]{1,0:T(8,128)(2,1)S(1)}, u32[]{:S(2)}, u32[]{:S(2)}) %collective-permute-start.13) | collective-permute-done | bytes 524320 | tf_op jit(solution)/shard_map/ppermute | solution.py:655
  271.2 7.9 %collective-permute-done.12.refs_9_ = bf16[128,2048]{1,0:T(8,128)(2,1)} collective-permute-done((bf16[128,2048]{1,0:T(8,128)(2,1)S(1)}, bf16[128,2048]{1,0:T(8,128)(2,1)}, u32[]{:S(2)}, u32[]{:S(2)}) %collective-permute-start.12) | collective-permute-done | bytes 524320 | tf_op jit(solution)/shard_map/ppermute | solution.py:655
  279.0 6.0 %shard_map.184 = (bf16[128,2048]{1,0:T(8,128)(2,1)}, bf16[8,384,128]{2,1,0:T(8,128)(2,1)}) custom-call(bf16[128,2048]{1,0:T(8,128)(2,1)} %bitcast.50, f32[128,2048]{1,0:T(8,128)} %get-tuple-element.84.refs_1_, bf16[128,2048]{1,0:T(8,128)(2,1)} %bitcast.61, bf16[768,2048]{1,0:T(8,128)(2,1)} %bitcast.37, ...), custom_call_target="tpu_custom_call" | custom-call | flops 520093696 | bytes 7340032 | tf_op jit(solution)/shard_map/pallas_call | solution.py:377
  285.1 4.2 %all-to-all-start.7 = ((bf16[8,384,128]{2,1,0:T(8,128)(2,1)}), bf16[8,384,128]{2,1,0:T(8,128)(2,1)}, u32[]{:S(2)}, u32[]{:S(2)}) async-start(bf16[8,384,128]{2,1,0:T(8,128)(2,1)} %get-tuple-element.92), calls=%async_computation.7 | async-start | bytes 1572864 | tf_op jit(solution)/shard_map/all_to_all | solution.py:225
  289.3 4.4 %shard_map.185 = (bf16[128,2048]{1,0:T(8,128)(2,1)}, bf16[128,2048]{1,0:T(8,128)(2,1)}, bf16[128,2048]{1,0:T(8,128)(2,1)}) custom-call(bf16[768,512]{1,0:T(8,128)(2,1)} %get-tuple-element.60.pick_ref.refs_2_.refs_4_, bf16[768,2048]{1,0:T(8,128)(2,1)} %bitcast.38), custom_call_target="tpu_custom_call" | custom-call | flops 1207959552 | bytes 3145728 | tf_op jit(solution)/shard_map/pallas_call | solution.py:177
  293.7 8.2 %all-to-all-done.7.in_ref = bf16[8,384,128]{2,1,0:T(8,128)(2,1)} async-done(((bf16[8,384,128]{2,1,0:T(8,128)(2,1)}), bf16[8,384,128]{2,1,0:T(8,128)(2,1)}, u32[]{:S(2)}, u32[]{:S(2)}) %all-to-all-start.7) | async-done | bytes 786464 | tf_op jit(solution)/shard_map/all_to_all | solution.py:225
  301.9 2.2 shard_map.188
  304.1 3.5 %all-to-all-start.8 = ((bf16[8,384,128]{2,1,0:T(8,128)(2,1)}), bf16[8,384,128]{2,1,0:T(8,128)(2,1)S(1)}, u32[]{:S(2)}, u32[]{:S(2)}) async-start(bf16[8,384,128]{2,1,0:T(8,128)(2,1)} %shard_map.188), calls=%async_computation.8 | async-start | bytes 1572864 | tf_op jit(solution)/shard_map/all_to_all | solution.py:225
  308.2 2.0 collective-permute-start.15
  310.2 6.6 %shard_map.187 = (bf16[128,2048]{1,0:T(8,128)(2,1)}, f32[128,2048]{1,0:T(8,128)}, f32[128,2048]{1,0:T(8,128)}) custom-call(bf16[128,2048]{1,0:T(8,128)(2,1)} %bitcast.51, bf16[128,2048]{1,0:T(8,128)(2,1)} %bitcast.43, bf16[128,2048]{1,0:T(8,128)(2,1)} %bitcast.47, bf16[128,2048]{1,0:T(8,128)(2,1)} %get-tuple-element.90.datt_ref, f32[16,128,128]{2,1,0:T(8,128)} %bitcast.55, ...), custom_call_target="tpu_custom_call" | custom-call | flops 469762048 | bytes 5767168 | tf_op jit(solution)/shard_map/pallas_call | solution.py:419
  316.9 3.3 all-to-all-done.8.later_ref
  321.1 3.3 shard_map.189
  324.4 7.7 %collective-permute-done.16.refs_1_ = bf16[128,2048]{1,0:T(8,128)(2,1)S(1)} collective-permute-done((bf16[128,2048]{1,0:T(8,128)(2,1)S(1)}, bf16[128,2048]{1,0:T(8,128)(2,1)S(1)}, u32[]{:S(2)}, u32[]{:S(2)}) %collective-permute-start.16) | collective-permute-done | bytes 524320 | tf_op jit(solution)/shard_map/ppermute | solution.py:655
  332.0 2.3 collective-permute-done.15.refs_0_
  335.1 3.9 %shard_map.186 = bf16[128,2048]{1,0:T(8,128)(2,1)} custom-call(bf16[128,2048]{1,0:T(8,128)(2,1)} %get-tuple-element.54.refs_0_.z_ref, bf16[768,512]{1,0:T(8,128)(2,1)} %get-tuple-element.60.pick_ref.refs_2_.refs_4_, bf16[768,2048]{1,0:T(8,128)(2,1)} %bitcast.39, bf16[128,2048]{1,0:T(8,128)(2,1)} %copy-done.14, bf16[128,2048]{1,0:T(8,128)(2,1)} %copy-done.13), custom_call_target="tpu_custom_call" | custom-call | flops 402653184 | bytes 3145728 | tf_op jit(solution)/shard_map/pallas_call | solution.py:481
  (85 shorter events, 26.4 us)
Async XLA Ops:
  0.6 35.1 %copy-start.21 = (bf16[2048,32]{0,1:T(8,128)(2,1)S(1)}, bf16[2048,32]{0,1:T(8,128)(2,1)}, u32[]{:S(2)}) copy-start(bf16[2048,32]{0,1:T(8,128)(2,1)} %param.16) | copy-start | bytes 393220
  1.5 35.3 %copy-start.12 = (s32[1,128,4]{2,1,0:T(8,128)}, s32[1,128,4]{2,1,0:T(8,128)S(1)}, u32[]{:S(2)}) copy-start(s32[1,128,4]{2,1,0:T(8,128)S(1)} %copy.19) | copy-start | bytes 6148
  2.6 49.0 %copy-start.2 = (bf16[128,2176]{1,0:T(8,128)(2,1)}, bf16[128,2176]{1,0:T(8,128)(2,1)S(1)}, u32[]{:S(2)}) copy-start(bf16[128,2176]{1,0:T(8,128)(2,1)S(1)} %fusion.1.refs_0_) | copy-start | bytes 1671172
  2.6 28.8 %collective-permute-start = (bf16[128,2176]{1,0:T(8,128)(2,1)S(1)}, bf16[128,2176]{1,0:T(8,128)(2,1)S(1)}, u32[]{:S(2)}, u32[]{:S(2)}) collective-permute-start(bf16[128,2176]{1,0:T(8,128)(2,1)S(1)} %fusion.1.refs_0_), channel_id=1, source_target_pairs={{0,16},{16,0},{1,17},{17,1},{2,18},{18,2},{3,19},{19,3},{4,20},{20... | collective-permute-start | bytes 1671176 | tf_op jit(solution)/shard_map/ppermute | solution.py:655
  9.0 13.5 %all-to-all-start = ((bf16[8,256,128]{2,1,0:T(8,128)(2,1)}), bf16[8,256,128]{2,1,0:T(8,128)(2,1)S(1)}, u32[]{:S(2)}, u32[]{:S(2)}) async-start(bf16[8,256,128]{2,1,0:T(8,128)(2,1)} %bitcast.62), calls=%async_computation | async-start | bytes 1048576 | tf_op jit(solution)/shard_map/all_to_all | solution.py:225
  12.7 38.9 %collective-permute-start.1 = (bf16[128,2176]{1,0:T(8,128)(2,1)S(1)}, bf16[128,2176]{1,0:T(8,128)(2,1)S(1)}, u32[]{:S(2)}, u32[]{:S(2)}) collective-permute-start(bf16[128,2176]{1,0:T(8,128)(2,1)S(1)} %fusion.1.refs_0_), channel_id=1, source_target_pairs={{0,8},{8,0},{1,9},{9,1},{2,10},{10,2},{3,11},{11,3},{4,12},{12,4},... | collective-permute-start | bytes 1671176 | tf_op jit(solution)/shard_map/ppermute | solution.py:655
  31.4 20.3 %copy-start.7 = (bf16[128,2176]{1,0:T(8,128)(2,1)}, bf16[128,2176]{1,0:T(8,128)(2,1)S(1)}, u32[]{:S(2)}) copy-start(bf16[128,2176]{1,0:T(8,128)(2,1)S(1)} %collective-permute-done.refs_1_) | copy-start | bytes 1671172
  31.4 20.3 %collective-permute-start.2 = (bf16[128,2176]{1,0:T(8,128)(2,1)S(1)}, bf16[128,2176]{1,0:T(8,128)(2,1)S(1)}, u32[]{:S(2)}, u32[]{:S(2)}) collective-permute-start(bf16[128,2176]{1,0:T(8,128)(2,1)S(1)} %collective-permute-done.refs_1_), channel_id=1, source_target_pairs={{0,8},{8,0},{1,9},{9,1},{2,10},{10,2},{3,11},{11,3},{4,12},{12,4},... | collective-permute-start | bytes 1671176 | tf_op jit(solution)/shard_map/ppermute | solution.py:655
  32.0 13.5 %all-to-all-start.1 = ((bf16[8,256,128]{2,1,0:T(8,128)(2,1)}), bf16[8,256,128]{2,1,0:T(8,128)(2,1)S(1)}, u32[]{:S(2)}, u32[]{:S(2)}) async-start(bf16[8,256,128]{2,1,0:T(8,128)(2,1)} %shard_map.171), calls=%async_computation.1 | async-start | bytes 1048576 | tf_op jit(solution)/shard_map/all_to_all | solution.py:225
  51.6 0.8 copy-start.8
  51.7 1.0 copy-start.9
  61.0 4.6 %copy-start.3 = (bf16[128,2048]{1,0:T(8,128)(2,1)S(1)}, bf16[128,2048]{1,0:T(8,128)(2,1)}, u32[]{:S(2)}) copy-start(bf16[128,2048]{1,0:T(8,128)(2,1)} %get-tuple-element.54.refs_0_.z_ref) | copy-start | bytes 1572868
  61.0 51.7 %all-to-all-start.3 = ((bf16[8,96,2176]{2,1,0:T(8,128)(2,1)}), bf16[8,96,2176]{2,1,0:T(8,128)(2,1)}, u32[]{:S(2)}, u32[]{:S(2)}) async-start(bf16[8,96,2176]{2,1,0:T(8,128)(2,1)} %bitcast.35), calls=%async_computation.3 | async-start | bytes 6684672 | tf_op jit(solution)/shard_map/all_to_all | solution.py:646
  65.6 27.2 %collective-permute-start.3 = (bf16[128,2048]{1,0:T(8,128)(2,1)S(1)}, bf16[128,2048]{1,0:T(8,128)(2,1)S(1)}, u32[]{:S(2)}, u32[]{:S(2)}) collective-permute-start(bf16[128,2048]{1,0:T(8,128)(2,1)S(1)} %copy-done.3), channel_id=1, source_target_pairs={{0,16},{16,0},{1,17},{17,1},{2,18},{18,2},{3,19},{19,3},{4,20},{20... | collective-permute-start | bytes 1572872 | tf_op jit(solution)/shard_map/ppermute | solution.py:655
  69.1 24.9 %collective-permute-start.4 = (bf16[128,2048]{1,0:T(8,128)(2,1)S(1)}, bf16[128,2048]{1,0:T(8,128)(2,1)S(1)}, u32[]{:S(2)}, u32[]{:S(2)}) collective-permute-start(bf16[128,2048]{1,0:T(8,128)(2,1)S(1)} %copy-done.3), channel_id=1, source_target_pairs={{0,8},{8,0},{1,9},{9,1},{2,10},{10,2},{3,11},{11,3},{4,12},{12,4},... | collective-permute-start | bytes 1572872 | tf_op jit(solution)/shard_map/ppermute | solution.py:655
  92.8 13.7 %copy-start.17 = (bf16[128,2048]{1,0:T(8,128)(2,1)}, bf16[128,2048]{1,0:T(8,128)(2,1)S(1)}, u32[]{:S(2)}) copy-start(bf16[128,2048]{1,0:T(8,128)(2,1)S(1)} %collective-permute-done.3.refs_1_) | copy-start | bytes 1572868
  92.8 13.7 %collective-permute-start.5 = (bf16[128,2048]{1,0:T(8,128)(2,1)S(1)}, bf16[128,2048]{1,0:T(8,128)(2,1)S(1)}, u32[]{:S(2)}, u32[]{:S(2)}) collective-permute-start(bf16[128,2048]{1,0:T(8,128)(2,1)S(1)} %collective-permute-done.3.refs_1_), channel_id=1, source_target_pairs={{0,8},{8,0},{1,9},{9,1},{2,10},{10,2},{3,11},{11,3},{4,12},{12,4},... | collective-permute-start | bytes 1572872 | tf_op jit(solution)/shard_map/ppermute | solution.py:655
  94.0 12.5 %copy-start.18 = (bf16[128,2048]{1,0:T(8,128)(2,1)}, bf16[128,2048]{1,0:T(8,128)(2,1)S(1)}, u32[]{:S(2)}) copy-start(bf16[128,2048]{1,0:T(8,128)(2,1)S(1)} %collective-permute-done.4.refs_2_) | copy-start | bytes 1572868
  106.6 0.8 copy-start.19
  112.7 41.9 %all-to-all-start.2 = ((bf16[8,96,2048]{2,1,0:T(8,128)(2,1)}), bf16[8,96,2048]{2,1,0:T(8,128)(2,1)S(1)}, u32[]{:S(2)}, u32[]{:S(2)}) async-start(bf16[8,96,2048]{2,1,0:T(8,128)(2,1)} %bitcast.40), calls=%async_computation.2 | async-start | bytes 6291456 | tf_op jit(solution)/shard_map/all_to_all | solution.py:646
  154.5 1.7 copy-start.5
  168.5 12.5 %all-to-all-start.4 = ((bf16[8,96,128]{2,1,0:T(8,128)(2,1)}), bf16[8,96,128]{2,1,0:T(8,128)(2,1)S(1)}, u32[]{:S(2)}, u32[]{:S(2)}) async-start(bf16[8,96,128]{2,1,0:T(8,128)(2,1)} %bitcast.67), calls=%async_computation.4 | async-start | bytes 393216 | tf_op jit(solution)/shard_map/all_to_all | solution.py:646
  181.7 45.3 %all-to-all-start.5 = ((bf16[8,96,2048]{2,1,0:T(8,128)(2,1)}), bf16[8,96,2048]{2,1,0:T(8,128)(2,1)S(1)}, u32[]{:S(2)}, u32[]{:S(2)}) async-start(bf16[8,96,2048]{2,1,0:T(8,128)(2,1)} %bitcast.58), calls=%async_computation.5 | async-start | bytes 6291456 | tf_op jit(solution)/shard_map/all_to_all | solution.py:646
  188.0 5.4 %collective-permute-start.6 = (bf16[128,128]{1,0:T(8,128)(2,1)}, bf16[128,128]{1,0:T(8,128)(2,1)S(1)}, u32[]{:S(2)}, u32[]{:S(2)}) collective-permute-start(bf16[128,128]{1,0:T(8,128)(2,1)} %get-tuple-element.69), channel_id=1, source_target_pairs={{0,16},{8,24},{16,0},{24,8},{1,17},{9,25},{17,1},{25,9},{2,18},{10... | collective-permute-start | bytes 98312 | tf_op jit(solution)/shard_map/ppermute | solution.py:655
  188.2 5.2 %collective-permute-start.7 = (bf16[128,128]{1,0:T(8,128)(2,1)}, bf16[128,128]{1,0:T(8,128)(2,1)S(1)}, u32[]{:S(2)}, u32[]{:S(2)}) collective-permute-start(bf16[128,128]{1,0:T(8,128)(2,1)} %get-tuple-element.70), channel_id=1, source_target_pairs={{0,8},{8,0},{16,24},{24,16},{1,9},{9,1},{17,25},{25,17},{2,10},{10... | collective-permute-start | bytes 98312 | tf_op jit(solution)/shard_map/ppermute | solution.py:655
  190.0 5.9 %collective-permute-start.8 = (bf16[128,128]{1,0:T(8,128)(2,1)}, bf16[128,128]{1,0:T(8,128)(2,1)S(1)}, u32[]{:S(2)}, u32[]{:S(2)}) collective-permute-start(bf16[128,128]{1,0:T(8,128)(2,1)} %get-tuple-element.71), channel_id=1, source_target_pairs={{0,24},{8,16},{16,8},{24,0},{1,25},{9,17},{17,9},{25,1},{2,26},{10... | collective-permute-start | bytes 98312 | tf_op jit(solution)/shard_map/ppermute | solution.py:655
  193.4 2.5 copy-start.22
  193.4 2.5 copy-start.23
  200.9 13.5 %collective-permute-start.9 = (f32[32,2048]{1,0:T(8,128)}, f32[32,2048]{1,0:T(8,128)S(1)}, u32[]{:S(2)}, u32[]{:S(2)}) collective-permute-start(f32[32,2048]{1,0:T(8,128)} %get-tuple-element.74), channel_id=1, source_target_pairs={{0,16},{16,0},{1,17},{17,1},{2,18},{18,2},{3,19},{19,3},{4,20},{20... | collective-permute-start | bytes 786440 | tf_op jit(solution)/shard_map/ppermute | solution.py:655
  200.9 13.5 %copy-start.20 = (f32[32,2048]{1,0:T(8,128)S(1)}, f32[32,2048]{1,0:T(8,128)}, u32[]{:S(2)}) copy-start(f32[32,2048]{1,0:T(8,128)} %get-tuple-element.74) | copy-start | bytes 786436
  214.4 11.9 %collective-permute-start.10 = (f32[32,2048]{1,0:T(8,128)S(1)}, f32[32,2048]{1,0:T(8,128)S(1)}, u32[]{:S(2)}, u32[]{:S(2)}) collective-permute-start(f32[32,2048]{1,0:T(8,128)S(1)} %add.26), channel_id=1, source_target_pairs={{0,8},{8,0},{1,9},{9,1},{2,10},{10,2},{3,11},{11,3},{4,12},{12,4},... | collective-permute-start | bytes 786440 | tf_op jit(solution)/shard_map/ppermute | solution.py:655
  227.0 1.8 copy-start
  233.2 51.9 %all-to-all-start.6 = ((bf16[8,96,2048]{2,1,0:T(8,128)(2,1)}), bf16[8,96,2048]{2,1,0:T(8,128)(2,1)S(1)}, u32[]{:S(2)}, u32[]{:S(2)}) async-start(bf16[8,96,2048]{2,1,0:T(8,128)(2,1)} %bitcast.59), calls=%async_computation.6 | async-start | bytes 6291456 | tf_op jit(solution)/shard_map/all_to_all | solution.py:646
  237.0 15.0 %collective-permute-start.11 = (bf16[128,2048]{1,0:T(8,128)(2,1)}, bf16[128,2048]{1,0:T(8,128)(2,1)S(1)}, u32[]{:S(2)}, u32[]{:S(2)}) collective-permute-start(bf16[128,2048]{1,0:T(8,128)(2,1)} %get-tuple-element.82), channel_id=1, source_target_pairs={{0,8},{8,0},{1,9},{9,1},{2,10},{10,2},{3,11},{11,3},{4,12},{12,4},... | collective-permute-start | bytes 1572872 | tf_op jit(solution)/shard_map/ppermute | solution.py:655
  239.0 32.2 %collective-permute-start.13 = (bf16[128,2048]{1,0:T(8,128)(2,1)}, bf16[128,2048]{1,0:T(8,128)(2,1)S(1)}, u32[]{:S(2)}, u32[]{:S(2)}) collective-permute-start(bf16[128,2048]{1,0:T(8,128)(2,1)} %get-tuple-element.81), channel_id=1, source_target_pairs={{0,8},{8,0},{1,9},{9,1},{2,10},{10,2},{3,11},{11,3},{4,12},{12,4},... | collective-permute-start | bytes 1572872 | tf_op jit(solution)/shard_map/ppermute | solution.py:655
  253.2 25.8 %collective-permute-start.12 = (bf16[128,2048]{1,0:T(8,128)(2,1)S(1)}, bf16[128,2048]{1,0:T(8,128)(2,1)}, u32[]{:S(2)}, u32[]{:S(2)}) collective-permute-start(bf16[128,2048]{1,0:T(8,128)(2,1)S(1)} %add_convert_fusion.1), channel_id=1, source_target_pairs={{0,16},{16,0},{1,17},{17,1},{2,18},{18,2},{3,19},{19,3},{4,20},{20... | collective-permute-start | bytes 1572872 | tf_op jit(solution)/shard_map/ppermute | solution.py:655
  271.2 7.9 %copy-start.15 = (bf16[128,2048]{1,0:T(8,128)(2,1)}, bf16[128,2048]{1,0:T(8,128)(2,1)S(1)}, u32[]{:S(2)}) copy-start(bf16[128,2048]{1,0:T(8,128)(2,1)S(1)} %collective-permute-done.13.refs_10_) | copy-start | bytes 1572868
  285.1 4.2 %copy-start.1 = (bf16[8,96,2048]{2,1,0:T(8,128)(2,1)}, bf16[8,96,2048]{2,1,0:T(8,128)(2,1)S(1)}, u32[]{:S(2)}) copy-start(bf16[8,96,2048]{2,1,0:T(8,128)(2,1)S(1)} %all-to-all-done.6) | copy-start | bytes 9437188
  285.1 16.8 %all-to-all-start.7 = ((bf16[8,384,128]{2,1,0:T(8,128)(2,1)}), bf16[8,384,128]{2,1,0:T(8,128)(2,1)}, u32[]{:S(2)}, u32[]{:S(2)}) async-start(bf16[8,384,128]{2,1,0:T(8,128)(2,1)} %get-tuple-element.92), calls=%async_computation.7 | async-start | bytes 1572864 | tf_op jit(solution)/shard_map/all_to_all | solution.py:225
  293.7 14.0 %copy-start.25 = (bf16[128,2048]{1,0:T(8,128)(2,1)S(1)}, bf16[128,2048]{1,0:T(8,128)(2,1)}, u32[]{:S(2)}) copy-start(bf16[128,2048]{1,0:T(8,128)(2,1)} %get-tuple-element.89) | copy-start | bytes 1572868
  293.7 14.4 %copy-start.16 = (bf16[128,2048]{1,0:T(8,128)(2,1)S(1)}, bf16[128,2048]{1,0:T(8,128)(2,1)}, u32[]{:S(2)}) copy-start(bf16[128,2048]{1,0:T(8,128)(2,1)} %get-tuple-element.87) | copy-start | bytes 1572868
  293.7 14.4 %collective-permute-start.14 = (bf16[128,2048]{1,0:T(8,128)(2,1)}, bf16[128,2048]{1,0:T(8,128)(2,1)S(1)}, u32[]{:S(2)}, u32[]{:S(2)}) collective-permute-start(bf16[128,2048]{1,0:T(8,128)(2,1)} %get-tuple-element.88), channel_id=1, source_target_pairs={{0,8},{8,0},{1,9},{9,1},{2,10},{10,2},{3,11},{11,3},{4,12},{12,4},... | collective-permute-start | bytes 1572872 | tf_op jit(solution)/shard_map/ppermute | solution.py:655
  304.1 16.1 %all-to-all-start.8 = ((bf16[8,384,128]{2,1,0:T(8,128)(2,1)}), bf16[8,384,128]{2,1,0:T(8,128)(2,1)S(1)}, u32[]{:S(2)}, u32[]{:S(2)}) async-start(bf16[8,384,128]{2,1,0:T(8,128)(2,1)} %shard_map.188), calls=%async_computation.8 | async-start | bytes 1572864 | tf_op jit(solution)/shard_map/all_to_all | solution.py:225
  307.7 24.4 %collective-permute-start.16 = (bf16[128,2048]{1,0:T(8,128)(2,1)S(1)}, bf16[128,2048]{1,0:T(8,128)(2,1)S(1)}, u32[]{:S(2)}, u32[]{:S(2)}) collective-permute-start(bf16[128,2048]{1,0:T(8,128)(2,1)S(1)} %copy-done.25), channel_id=1, source_target_pairs={{0,8},{8,0},{1,9},{9,1},{2,10},{10,2},{3,11},{11,3},{4,12},{12,4},... | collective-permute-start | bytes 1572872 | tf_op jit(solution)/shard_map/ppermute | solution.py:655
  308.2 26.1 %collective-permute-start.15 = (bf16[128,2048]{1,0:T(8,128)(2,1)S(1)}, bf16[128,2048]{1,0:T(8,128)(2,1)S(1)}, u32[]{:S(2)}, u32[]{:S(2)}) collective-permute-start(bf16[128,2048]{1,0:T(8,128)(2,1)S(1)} %add_convert_fusion), channel_id=1, source_target_pairs={{0,16},{16,0},{1,17},{17,1},{2,18},{18,2},{3,19},{19,3},{4,20},{20... | collective-permute-start | bytes 1572872 | tf_op jit(solution)/shard_map/ppermute | solution.py:655
  320.2 0.9 copy-start.6
  332.0 2.3 copy-start.13
  334.3 0.8 copy-start.14
  (4 other events, 2.9 us)

commit v4 on v3

--- a/solution.py
+++ b/solution.py
@@ -19,7 +19,7 @@
 ALL = ("far", "near", "ctx")
 F32 = jnp.float32
 BF16 = jnp.bfloat16
-LIMIT = 60 << 20
+LIMIT = 62 << 20
 
 
 def mm(a, b):
@@ -114,22 +114,6 @@
     return pl.BlockSpec(memory_space=pltpu.SMEM)
 
 
-def route(plane, blocks, experts, rows, cap):
-    tokens, n = blocks[0].shape[0], len(blocks)
-    return call(
-        functools.partial(route_kernel, cap, TOPK),
-        (
-            jax.ShapeDtypeStruct((rows, n * tokens), BF16),
-            jax.ShapeDtypeStruct((n * tokens, experts), F32),
-        ),
-        (1,),
-        [smem()] + [pl.BlockSpec((tokens, 128), lambda i: (0, D // 128))] * n,
-        (whole((rows, n * tokens)), whole((n * tokens, experts))),
-        flops=2 * n * rows * tokens * experts,
-        moved=2 * n * rows * tokens,
-    )(plane, *blocks)
-
-
 def gather_kernel(masked, pick_ref, chosen_ref, *refs):
     *block_refs, send_ref, stack_ref = refs
     tokens = block_refs[0].shape[0]
@@ -160,6 +144,32 @@
         flops=2 * rows * pick.shape[1] * D,
         moved=2 * rows * D,
     )(pick, chosen, *blocks)
+
+
+def route_gather_kernel(cap, top, plane_ref, *refs):
+    *block_refs, pick_ref, chosen_ref, send_ref, stack_ref = refs
+    ids_refs = [ref.at[:, D : D + 128] for ref in block_refs]
+    route_kernel(cap, top, plane_ref, *ids_refs, pick_ref, chosen_ref)
+    gather_kernel(True, pick_ref, chosen_ref, *block_refs, send_ref, stack_ref)
+
+
+def route_gather(plane, blocks, experts, rows, cap):
+    tokens, n = blocks[0].shape[0], len(blocks)
+    width = D + lanes_of(experts)
+    return call(
+        functools.partial(route_gather_kernel, cap, TOPK),
+        (
+            jax.ShapeDtypeStruct((rows, n * tokens), BF16),
+            jax.ShapeDtypeStruct((n * tokens, experts), F32),
+            jax.ShapeDtypeStruct((rows, width), BF16),
+        ),
+        (1,),
+        [smem()] + [whole(blocks[0].shape)] * n,
+        (whole((rows, n * tokens)), whole((n * tokens, experts)), whole((rows, width))),
+        scratch=[pltpu.VMEM((n * tokens, D), BF16)],
+        flops=2 * n * rows * tokens * D,
+        moved=2 * rows * D,
+    )(plane, *blocks)
 
 
 def partial_kernel(pick_ref, back_ref, *out_refs):
@@ -738,8 +748,8 @@
     earlier = to_heads(sums).reshape(H, DH, DH)
     z, att, sig = attention_forward(q, k, v, prior, earlier, gain, router_weight, ids)
     z_blocks = replicate(z)
-    pick, chosen = route(plane, after(dy_blocks, z), experts, rows, cap)
-    dy_rows = exchange(gather(pick, chosen, dy_blocks, True))
+    pick, chosen, dy_send = route_gather(plane, after(dy_blocks, z), experts, rows, cap)
+    dy_rows = exchange(dy_send)
     z_rows = exchange(gather(pick, chosen, z_blocks, False))
 
     dh_plain = expert_down_back(dy_rows, down_mat)

time: 341 us -> 337 us (0.988)
    pallas_call x2 -> x1, Pallas kernels: 11 us -> 5.29 us  [gather(): call(functools.partial(gather_kernel, masked), jax.ShapeDtypeStruct((rows...]
    unnamed x54 -> x52, local copies, waits for them, and re-layouts: 11.7 us -> 8.91 us
  transfers between devices with their start and end apart: 26 -> 26, of which waited for: 18 -> 17; matrix products, arithmetic and copies ran while one was open for 1% -> 1% of each run, Pallas kernels for 23% -> 23%
where the time goes in v4:
time: 337 us; the launch traced here: 336 us
  waiting for transfers between devices  159 us (47%)
  Pallas kernels  104 us (31%)
  starting transfers between devices  57.3 us (17%)
  local copies, waits for them, and re-layouts  8.91 us (3%)
  other arithmetic  4.55 us (1%)
    ppermute x17, waiting for transfers between devices, swap(): lax.ppermute(block, axis, [(i, i ^ by) for i in range(lax.axis_size(axis))])  102 us
    all_to_all x5, waiting for transfers between devices, exchange(): lax.all_to_all(shaped, 'ctx', split_axis=0, concat_axis=0, tiled=True)  30.7 us
    all_to_all x4, waiting for transfers between devices, to_heads(): return lax.all_to_all(block, 'ctx', split_axis=0, concat_axis=0, tiled=True)  26.8 us
    all_to_all x5, starting transfers between devices, exchange(): lax.all_to_all(shaped, 'ctx', split_axis=0, concat_axis=0, tiled=True)  21.7 us
    ppermute x17, starting transfers between devices, swap(): lax.ppermute(block, axis, [(i, i ^ by) for i in range(lax.axis_size(axis))])  20.9 us
    all_to_all x4, starting transfers between devices, to_heads(): return lax.all_to_all(block, 'ctx', split_axis=0, concat_axis=0, tiled=True)  14.7 us
    pallas_call x1, Pallas kernels, expert_forward(): call(expert_kernel, (inner, inner, inner, column, pair), (hidden // tile,...  12.3 us
    pallas_call x1, Pallas kernels, expert_weights(): call(weights_kernel, (jax.ShapeDtypeStruct((D, hidden), BF16), jax.ShapeD...  11.8 us
  transfers between devices with their start and end apart: 26, of which 17 were waited for; matrix products, arithmetic and copies ran while one was open for 1% of the time, Pallas kernels for 23%

profile of v4, /device:TPU:0, one launch (start us, length us, event | category | flops | bytes accessed | tf_op | source)
XLA Modules:
  0.0 335.5 jit_solution(15381037222522478332)
XLA Ops:
  2.6 4.1 %collective-permute-start = (bf16[128,2176]{1,0:T(8,128)(2,1)S(1)}, bf16[128,2176]{1,0:T(8,128)(2,1)S(1)}, u32[]{:S(2)}, u32[]{:S(2)}) collective-permute-start(bf16[128,2176]{1,0:T(8,128)(2,1)S(1)} %fusion.1.refs_0_), channel_id=1, source_target_pairs={{0,16},{16,0},{1,17},{17,1},{2,18},{18,2},{3,19},{19,3},{4,20},{20... | collective-permute-start | bytes 1671176 | tf_op jit(solution)/shard_map/ppermute | solution.py:665
  6.7 2.3 shard_map.170
  9.0 3.7 %all-to-all-start = ((bf16[8,256,128]{2,1,0:T(8,128)(2,1)}), bf16[8,256,128]{2,1,0:T(8,128)(2,1)S(1)}, u32[]{:S(2)}, u32[]{:S(2)}) async-start(bf16[8,256,128]{2,1,0:T(8,128)(2,1)} %bitcast.56), calls=%async_computation | async-start | bytes 1048576 | tf_op jit(solution)/shard_map/all_to_all | solution.py:235
  14.3 8.2 %all-to-all-done.in_ref = bf16[8,256,128]{2,1,0:T(8,128)(2,1)S(1)} async-done(((bf16[8,256,128]{2,1,0:T(8,128)(2,1)}), bf16[8,256,128]{2,1,0:T(8,128)(2,1)S(1)}, u32[]{:S(2)}, u32[]{:S(2)}) %all-to-all-start) | async-done | bytes 524320 | tf_op jit(solution)/shard_map/all_to_all | solution.py:235
  25.2 6.2 %collective-permute-done.refs_1_ = bf16[128,2176]{1,0:T(8,128)(2,1)S(1)} collective-permute-done((bf16[128,2176]{1,0:T(8,128)(2,1)S(1)}, bf16[128,2176]{1,0:T(8,128)(2,1)S(1)}, u32[]{:S(2)}, u32[]{:S(2)}) %collective-permute-start) | collective-permute-done | bytes 557088 | tf_op jit(solution)/shard_map/ppermute | solution.py:665
  32.0 3.7 %all-to-all-start.1 = ((bf16[8,256,128]{2,1,0:T(8,128)(2,1)}), bf16[8,256,128]{2,1,0:T(8,128)(2,1)S(1)}, u32[]{:S(2)}, u32[]{:S(2)}) async-start(bf16[8,256,128]{2,1,0:T(8,128)(2,1)} %shard_map.171), calls=%async_computation.1 | async-start | bytes 1048576 | tf_op jit(solution)/shard_map/all_to_all | solution.py:235
  36.8 8.7 %all-to-all-done.1 = bf16[8,256,128]{2,1,0:T(8,128)(2,1)S(1)} async-done(((bf16[8,256,128]{2,1,0:T(8,128)(2,1)}), bf16[8,256,128]{2,1,0:T(8,128)(2,1)S(1)}, u32[]{:S(2)}, u32[]{:S(2)}) %all-to-all-start.1) | async-done | bytes 524320 | tf_op jit(solution)/shard_map/all_to_all | solution.py:235
  46.3 5.3 %shard_map.172 = (bf16[128,2048]{1,0:T(8,128)(2,1)}, f32[128,2048]{1,0:T(8,128)}, f32[128,32]{1,0:T(8,128)}) custom-call(bf16[128,2048]{1,0:T(8,128)(2,1)} %bitcast.44, bf16[128,2048]{1,0:T(8,128)(2,1)} %bitcast.37, bf16[128,2048]{1,0:T(8,128)(2,1)} %bitcast.41, f32[16,128,128]{2,1,0:T(8,128)} %bitcast.49, bf16[16,128,128]{2,1,0:T(8,128)(2,1)} %bitcast.47, ...), custom_call_target="tpu_custom_call" | custom-call | flops 268435456 | bytes 4194304 | tf_op jit(solution)/shard_map/pallas_call | solution.py:286
  51.6 6.0 %shard_map.173 = (bf16[768,512]{1,0:T(8,128)(2,1)}, f32[512,32]{1,0:T(8,128)}, bf16[768,2176]{1,0:T(8,128)(2,1)}) custom-call(s32[1,1]{1,0:T(1,128)} %bitcast.8.plane_ref, bf16[128,2176]{1,0:T(8,128)(2,1)} %copy-done.7, bf16[128,2176]{1,0:T(8,128)(2,1)} %copy-done.22, bf16[128,2176]{1,0:T(8,128)(2,1)} %collective-permute-done.1.refs_2_, ...), custom_call_target="tpu_custom_call" | custom-call | flops 1610612736 | bytes 3145728 | tf_op jit(solution)/shard_map/pallas_call | solution.py:159
  57.6 4.6 %all-to-all-start.3 = ((bf16[8,96,2176]{2,1,0:T(8,128)(2,1)}), bf16[8,96,2176]{2,1,0:T(8,128)(2,1)}, u32[]{:S(2)}, u32[]{:S(2)}) async-start(bf16[8,96,2176]{2,1,0:T(8,128)(2,1)} %bitcast.51), calls=%async_computation.3 | async-start | bytes 6684672 | tf_op jit(solution)/shard_map/all_to_all | solution.py:656
  62.3 3.5 %collective-permute-start.3 = (bf16[128,2048]{1,0:T(8,128)(2,1)S(1)}, bf16[128,2048]{1,0:T(8,128)(2,1)S(1)}, u32[]{:S(2)}, u32[]{:S(2)}) collective-permute-start(bf16[128,2048]{1,0:T(8,128)(2,1)S(1)} %copy-done), channel_id=1, source_target_pairs={{0,16},{16,0},{1,17},{17,1},{2,18},{18,2},{3,19},{19,3},{4,20},{20... | collective-permute-start | bytes 1572872 | tf_op jit(solution)/shard_map/ppermute | solution.py:665
  65.8 23.7 %collective-permute-done.3.refs_1_ = bf16[128,2048]{1,0:T(8,128)(2,1)S(1)} collective-permute-done((bf16[128,2048]{1,0:T(8,128)(2,1)S(1)}, bf16[128,2048]{1,0:T(8,128)(2,1)S(1)}, u32[]{:S(2)}, u32[]{:S(2)}) %collective-permute-start.3) | collective-permute-done | bytes 524320 | tf_op jit(solution)/shard_map/ppermute | solution.py:665
  90.7 12.5 %collective-permute-done.5.refs_3_ = bf16[128,2048]{1,0:T(8,128)(2,1)S(1)} collective-permute-done((bf16[128,2048]{1,0:T(8,128)(2,1)S(1)}, bf16[128,2048]{1,0:T(8,128)(2,1)S(1)}, u32[]{:S(2)}, u32[]{:S(2)}) %collective-permute-start.5) | collective-permute-done | bytes 524320 | tf_op jit(solution)/shard_map/ppermute | solution.py:665
  104.0 5.3 %shard_map.174 = bf16[768,2048]{1,0:T(8,128)(2,1)} custom-call(bf16[768,512]{1,0:T(8,128)(2,1)} %get-tuple-element.61.pick_ref.refs_2_.refs_4_, f32[512,32]{1,0:T(8,128)} %get-tuple-element.62.chosen_ref, bf16[128,2048]{1,0:T(8,128)(2,1)} %get-tuple-element.55.refs_0_.z_ref, bf16[128,2048]{1,0:T(8,128)(2,1)} %copy-done.12, bf16[128,2048]{1,0:T(8,128)(2,1)} %copy-done.15, ...), custom_call_target="tpu_custom_call" | custom-call | flops 1610612736 | bytes 3145728 | tf_op jit(solution)/shard_map/pallas_call | solution.py:137
  109.3 4.5 %all-to-all-start.2 = ((bf16[8,96,2048]{2,1,0:T(8,128)(2,1)}), bf16[8,96,2048]{2,1,0:T(8,128)(2,1)}, u32[]{:S(2)}, u32[]{:S(2)}) async-start(bf16[8,96,2048]{2,1,0:T(8,128)(2,1)} %bitcast.35), calls=%async_computation.2 | async-start | bytes 6291456 | tf_op jit(solution)/shard_map/all_to_all | solution.py:656
  114.4 6.6 %shard_map.175.dh_ref = f32[768,768]{1,0:T(8,128)} custom-call(bf16[768,2176]{1,0:T(8,128)(2,1)} %bitcast.15.dy_ref.mask_ref, bf16[768,2048]{1,0:T(8,128)(2,1)} %bitcast.68), custom_call_target="tpu_custom_call" | custom-call | flops 2415919104 | bytes 6291456 | tf_op jit(solution)/shard_map/pallas_call | solution.py:509
  121.0 30.7 %all-to-all-done.2 = bf16[8,96,2048]{2,1,0:T(8,128)(2,1)} async-done(((bf16[8,96,2048]{2,1,0:T(8,128)(2,1)}), bf16[8,96,2048]{2,1,0:T(8,128)(2,1)}, u32[]{:S(2)}, u32[]{:S(2)}) %all-to-all-start.2) | async-done | bytes 3145760 | tf_op jit(solution)/shard_map/all_to_all | solution.py:656
  151.7 12.3 %shard_map.176 = (bf16[768,768]{1,0:T(8,128)(2,1)}, bf16[768,768]{1,0:T(8,128)(2,1)}, bf16[768,768]{1,0:T(8,128)(2,1)}, f32[768,1]{1,0:T(8,128)}, bf16[768,128]{1,0:T(8,128)(2,1)}) custom-call(s32[1,2]{1,0:T(1,128)} %add_bitcast_fusion.me_ref, bf16[768,2048]{1,0:T(8,128)(2,1)} %bitcast.13.z_ref, bf16[768,2176]{1,0:T(8,128)(2,1)} %bitcast.15.dy_ref.mask_ref, ...), custom_call_target="tpu_custom_call" | custom-call | flops 4831838208 | bytes 9437184 | tf_op jit(solution)/shard_map/pallas_call | solution.py:569
  164.0 3.4 %all-to-all-start.4 = ((bf16[8,96,128]{2,1,0:T(8,128)(2,1)}), bf16[8,96,128]{2,1,0:T(8,128)(2,1)S(1)}, u32[]{:S(2)}, u32[]{:S(2)}) async-start(bf16[8,96,128]{2,1,0:T(8,128)(2,1)} %bitcast.61), calls=%async_computation.4 | async-start | bytes 393216 | tf_op jit(solution)/shard_map/all_to_all | solution.py:656
  167.4 9.1 %shard_map.177 = bf16[768,2048]{1,0:T(8,128)(2,1)} custom-call(bf16[768,768]{1,0:T(8,128)(2,1)} %get-tuple-element.67.dgp_ref, bf16[768,768]{1,0:T(8,128)(2,1)} %get-tuple-element.68.dup_ref, bf16[2048,768]{1,0:T(8,128)(2,1)} %bitcast.65, bf16[2048,768]{1,0:T(8,128)(2,1)} %bitcast.67, f32[768,1]{1,0:T(8,128)} %get-tuple-element.69.weight_ref), custom_call_target="tpu_custom_call" | custom-call | flops 4831838208 | bytes 9437184 | tf_op jit(solution)/shard_map/pallas_call | solution.py:597
  177.2 4.6 %all-to-all-start.5 = ((bf16[8,96,2048]{2,1,0:T(8,128)(2,1)}), bf16[8,96,2048]{2,1,0:T(8,128)(2,1)}, u32[]{:S(2)}, u32[]{:S(2)}) async-start(bf16[8,96,2048]{2,1,0:T(8,128)(2,1)} %bitcast.52), calls=%async_computation.5 | async-start | bytes 6291456 | tf_op jit(solution)/shard_map/all_to_all | solution.py:656
  181.9 2.1 shard_map.178
  186.2 2.2 collective-permute-start.8
  189.5 2.7 collective-permute-done.8.refs_6_
  192.7 4.3 %shard_map.179 = (bf16[3,128,32]{2,1,0:T(8,128)(2,1)}, f32[32,2048]{1,0:T(8,128)}) custom-call(bf16[128,2048]{1,0:T(8,128)(2,1)} %get-tuple-element.55.refs_0_.z_ref, bf16[768,128]{1,0:T(8,128)(2,1)} %bitcast.58, bf16[768,512]{1,0:T(8,128)(2,1)} %get-tuple-element.61.pick_ref.refs_2_.refs_4_, f32[128,32]{1,0:T(8,128)} %get-tuple-element.66.refs_3_, ...), custom_call_target="tpu_custom_call" | custom-call | flops 50331648 | bytes 524288 | tf_op jit(solution)/shard_map/pallas_call | solution.py:336
  197.1 6.4 %shard_map.180 = bf16[768,2048]{1,0:T(8,128)(2,1)} custom-call(bf16[768,768]{1,0:T(8,128)(2,1)} %get-tuple-element.75.hid_ref, bf16[768,2048]{1,0:T(8,128)(2,1)} %bitcast.69, f32[768,1]{1,0:T(8,128)} %get-tuple-element.69.weight_ref), custom_call_target="tpu_custom_call" | custom-call | flops 2415919104 | bytes 6291456 | tf_op jit(solution)/shard_map/pallas_call | solution.py:614
  203.5 6.7 %collective-permute-done.9 = f32[32,2048]{1,0:T(8,128)S(1)} collective-permute-done((f32[32,2048]{1,0:T(8,128)}, f32[32,2048]{1,0:T(8,128)S(1)}, u32[]{:S(2)}, u32[]{:S(2)}) %collective-permute-start.9) | collective-permute-done | bytes 262176 | tf_op jit(solution)/shard_map/ppermute | solution.py:665
  210.3 11.8 %shard_map.181 = (bf16[2048,768]{1,0:T(8,128)(2,1)}, bf16[2048,768]{1,0:T(8,128)(2,1)}, bf16[768,2048]{1,0:T(8,128)(2,1)}) custom-call(bf16[768,2048]{1,0:T(8,128)(2,1)} %bitcast.13.z_ref, bf16[768,2176]{1,0:T(8,128)(2,1)} %bitcast.15.dy_ref.mask_ref, bf16[768,768]{1,0:T(8,128)(2,1)} %get-tuple-element.75.hid_ref, ...), custom_call_target="tpu_custom_call" | custom-call | flops 7247757312 | bytes 15728640 | tf_op jit(solution)/shard_map/pallas_call | solution.py:638
  222.9 4.4 %shard_map.182 = (bf16[128,2048]{1,0:T(8,128)(2,1)}, bf16[128,2048]{1,0:T(8,128)(2,1)}, bf16[128,2048]{1,0:T(8,128)(2,1)}) custom-call(bf16[768,512]{1,0:T(8,128)(2,1)} %get-tuple-element.61.pick_ref.refs_2_.refs_4_, bf16[768,2048]{1,0:T(8,128)(2,1)} %bitcast.22.back_ref.refs_3_), custom_call_target="tpu_custom_call" | custom-call | flops 1207959552 | bytes 3145728 | tf_op jit(solution)/shard_map/pallas_call | solution.py:187
  227.3 4.6 %all-to-all-start.6 = ((bf16[8,96,2048]{2,1,0:T(8,128)(2,1)}), bf16[8,96,2048]{2,1,0:T(8,128)(2,1)}, u32[]{:S(2)}, u32[]{:S(2)}) async-start(bf16[8,96,2048]{2,1,0:T(8,128)(2,1)} %bitcast.53), calls=%async_computation.6 | async-start | bytes 6291456 | tf_op jit(solution)/shard_map/all_to_all | solution.py:656
  231.9 2.1 collective-permute-start.11
  234.0 12.6 %collective-permute-done.11 = bf16[128,2048]{1,0:T(8,128)(2,1)S(1)} collective-permute-done((bf16[128,2048]{1,0:T(8,128)(2,1)S(1)}, bf16[128,2048]{1,0:T(8,128)(2,1)S(1)}, u32[]{:S(2)}, u32[]{:S(2)}) %collective-permute-start.11) | collective-permute-done | bytes 524320 | tf_op jit(solution)/shard_map/ppermute | solution.py:665
  246.8 2.3 collective-permute-start.12
  249.1 17.6 %collective-permute-done.13.refs_10_ = bf16[128,2048]{1,0:T(8,128)(2,1)S(1)} collective-permute-done((bf16[128,2048]{1,0:T(8,128)(2,1)S(1)}, bf16[128,2048]{1,0:T(8,128)(2,1)S(1)}, u32[]{:S(2)}, u32[]{:S(2)}) %collective-permute-start.13) | collective-permute-done | bytes 524320 | tf_op jit(solution)/shard_map/ppermute | solution.py:665
  266.6 5.8 %collective-permute-done.12.refs_9_ = bf16[128,2048]{1,0:T(8,128)(2,1)S(1)} collective-permute-done((bf16[128,2048]{1,0:T(8,128)(2,1)S(1)}, bf16[128,2048]{1,0:T(8,128)(2,1)S(1)}, u32[]{:S(2)}, u32[]{:S(2)}) %collective-permute-start.12) | collective-permute-done | bytes 524320 | tf_op jit(solution)/shard_map/ppermute | solution.py:665
  273.2 6.1 %shard_map.183 = (bf16[128,2048]{1,0:T(8,128)(2,1)}, bf16[8,384,128]{2,1,0:T(8,128)(2,1)}) custom-call(bf16[128,2048]{1,0:T(8,128)(2,1)} %bitcast.45, f32[128,2048]{1,0:T(8,128)} %get-tuple-element.86.refs_1_, bf16[128,2048]{1,0:T(8,128)(2,1)} %bitcast.55, bf16[768,2048]{1,0:T(8,128)(2,1)} %bitcast.22.back_ref.refs_3_, ...), custom_call_target="tpu_custom_call" | custom-call | flops 520093696 | bytes 7340032 | tf_op jit(solution)/shard_map/pallas_call | solution.py:387
  279.3 3.7 %all-to-all-start.7 = ((bf16[8,384,128]{2,1,0:T(8,128)(2,1)}), bf16[8,384,128]{2,1,0:T(8,128)(2,1)S(1)}, u32[]{:S(2)}, u32[]{:S(2)}) async-start(bf16[8,384,128]{2,1,0:T(8,128)(2,1)} %get-tuple-element.94), calls=%async_computation.7 | async-start | bytes 1572864 | tf_op jit(solution)/shard_map/all_to_all | solution.py:235
  283.0 4.4 %shard_map.184 = (bf16[128,2048]{1,0:T(8,128)(2,1)}, bf16[128,2048]{1,0:T(8,128)(2,1)}, bf16[128,2048]{1,0:T(8,128)(2,1)}) custom-call(bf16[768,512]{1,0:T(8,128)(2,1)} %get-tuple-element.61.pick_ref.refs_2_.refs_4_, bf16[768,2048]{1,0:T(8,128)(2,1)} %bitcast.24.back_ref), custom_call_target="tpu_custom_call" | custom-call | flops 1207959552 | bytes 3145728 | tf_op jit(solution)/shard_map/pallas_call | solution.py:187
  287.4 8.2 %all-to-all-done.7.in_ref = bf16[8,384,128]{2,1,0:T(8,128)(2,1)S(1)} async-done(((bf16[8,384,128]{2,1,0:T(8,128)(2,1)}), bf16[8,384,128]{2,1,0:T(8,128)(2,1)S(1)}, u32[]{:S(2)}, u32[]{:S(2)}) %all-to-all-start.7) | async-done | bytes 786464 | tf_op jit(solution)/shard_map/all_to_all | solution.py:235
  296.5 2.2 shard_map.187
  298.6 3.5 %all-to-all-start.8 = ((bf16[8,384,128]{2,1,0:T(8,128)(2,1)}), bf16[8,384,128]{2,1,0:T(8,128)(2,1)S(1)}, u32[]{:S(2)}, u32[]{:S(2)}) async-start(bf16[8,384,128]{2,1,0:T(8,128)(2,1)} %shard_map.187), calls=%async_computation.8 | async-start | bytes 1572864 | tf_op jit(solution)/shard_map/all_to_all | solution.py:235
  302.3 2.0 add_convert_fusion
  304.3 2.2 collective-permute-start.15
  306.4 6.6 %shard_map.186 = (bf16[128,2048]{1,0:T(8,128)(2,1)}, f32[128,2048]{1,0:T(8,128)}, f32[128,2048]{1,0:T(8,128)}) custom-call(bf16[128,2048]{1,0:T(8,128)(2,1)} %bitcast.46, bf16[128,2048]{1,0:T(8,128)(2,1)} %bitcast.38, bf16[128,2048]{1,0:T(8,128)(2,1)} %bitcast.42, bf16[128,2048]{1,0:T(8,128)(2,1)} %get-tuple-element.92.datt_ref, f32[16,128,128]{2,1,0:T(8,128)} %bitcast.50, ...), custom_call_target="tpu_custom_call" | custom-call | flops 469762048 | bytes 5767168 | tf_op jit(solution)/shard_map/pallas_call | solution.py:429
  315.6 3.3 shard_map.188
  318.9 6.0 %collective-permute-done.16.refs_1_ = bf16[128,2048]{1,0:T(8,128)(2,1)S(1)} collective-permute-done((bf16[128,2048]{1,0:T(8,128)(2,1)}, bf16[128,2048]{1,0:T(8,128)(2,1)S(1)}, u32[]{:S(2)}, u32[]{:S(2)}) %collective-permute-start.16) | collective-permute-done | bytes 524320 | tf_op jit(solution)/shard_map/ppermute | solution.py:665
  324.9 5.9 %collective-permute-done.15.refs_0_ = bf16[128,2048]{1,0:T(8,128)(2,1)S(1)} collective-permute-done((bf16[128,2048]{1,0:T(8,128)(2,1)}, bf16[128,2048]{1,0:T(8,128)(2,1)S(1)}, u32[]{:S(2)}, u32[]{:S(2)}) %collective-permute-start.15) | collective-permute-done | bytes 524320 | tf_op jit(solution)/shard_map/ppermute | solution.py:665
  331.6 3.9 %shard_map.185 = bf16[128,2048]{1,0:T(8,128)(2,1)} custom-call(bf16[128,2048]{1,0:T(8,128)(2,1)} %get-tuple-element.55.refs_0_.z_ref, bf16[768,512]{1,0:T(8,128)(2,1)} %get-tuple-element.61.pick_ref.refs_2_.refs_4_, bf16[768,2048]{1,0:T(8,128)(2,1)} %bitcast.24.back_ref, bf16[128,2048]{1,0:T(8,128)(2,1)} %copy-done.9, bf16[128,2048]{1,0:T(8,128)(2,1)} %copy-done.8), custom_call_target="tpu_custom_call" | custom-call | flops 402653184 | bytes 3145728 | tf_op jit(solution)/shard_map/pallas_call | solution.py:491
  (82 shorter events, 22.0 us)
Async XLA Ops:
  0.6 35.1 %copy-start.18 = (bf16[2048,32]{0,1:T(8,128)(2,1)S(1)}, bf16[2048,32]{0,1:T(8,128)(2,1)}, u32[]{:S(2)}) copy-start(bf16[2048,32]{0,1:T(8,128)(2,1)} %param.16) | copy-start | bytes 393220
  1.5 35.3 %copy-start.6 = (s32[1,128,4]{2,1,0:T(8,128)}, s32[1,128,4]{2,1,0:T(8,128)S(1)}, u32[]{:S(2)}) copy-start(s32[1,128,4]{2,1,0:T(8,128)S(1)} %copy.19) | copy-start | bytes 6148
  2.6 49.0 %copy-start.7 = (bf16[128,2176]{1,0:T(8,128)(2,1)}, bf16[128,2176]{1,0:T(8,128)(2,1)S(1)}, u32[]{:S(2)}) copy-start(bf16[128,2176]{1,0:T(8,128)(2,1)S(1)} %fusion.1.refs_0_) | copy-start | bytes 1671172
  2.6 28.8 %collective-permute-start = (bf16[128,2176]{1,0:T(8,128)(2,1)S(1)}, bf16[128,2176]{1,0:T(8,128)(2,1)S(1)}, u32[]{:S(2)}, u32[]{:S(2)}) collective-permute-start(bf16[128,2176]{1,0:T(8,128)(2,1)S(1)} %fusion.1.refs_0_), channel_id=1, source_target_pairs={{0,16},{16,0},{1,17},{17,1},{2,18},{18,2},{3,19},{19,3},{4,20},{20... | collective-permute-start | bytes 1671176 | tf_op jit(solution)/shard_map/ppermute | solution.py:665
  9.0 13.5 %all-to-all-start = ((bf16[8,256,128]{2,1,0:T(8,128)(2,1)}), bf16[8,256,128]{2,1,0:T(8,128)(2,1)S(1)}, u32[]{:S(2)}, u32[]{:S(2)}) async-start(bf16[8,256,128]{2,1,0:T(8,128)(2,1)} %bitcast.56), calls=%async_computation | async-start | bytes 1048576 | tf_op jit(solution)/shard_map/all_to_all | solution.py:235
  12.7 38.9 %collective-permute-start.1 = (bf16[128,2176]{1,0:T(8,128)(2,1)S(1)}, bf16[128,2176]{1,0:T(8,128)(2,1)}, u32[]{:S(2)}, u32[]{:S(2)}) collective-permute-start(bf16[128,2176]{1,0:T(8,128)(2,1)S(1)} %fusion.1.refs_0_), channel_id=1, source_target_pairs={{0,8},{8,0},{1,9},{9,1},{2,10},{10,2},{3,11},{11,3},{4,12},{12,4},... | collective-permute-start | bytes 1671176 | tf_op jit(solution)/shard_map/ppermute | solution.py:665
  22.5 0.8 copy-start.4
  31.4 20.2 %copy-start.22 = (bf16[128,2176]{1,0:T(8,128)(2,1)}, bf16[128,2176]{1,0:T(8,128)(2,1)S(1)}, u32[]{:S(2)}) copy-start(bf16[128,2176]{1,0:T(8,128)(2,1)S(1)} %collective-permute-done.refs_1_) | copy-start | bytes 1671172
  31.4 20.2 %collective-permute-start.2 = (bf16[128,2176]{1,0:T(8,128)(2,1)S(1)}, bf16[128,2176]{1,0:T(8,128)(2,1)}, u32[]{:S(2)}, u32[]{:S(2)}) collective-permute-start(bf16[128,2176]{1,0:T(8,128)(2,1)S(1)} %collective-permute-done.refs_1_), channel_id=1, source_target_pairs={{0,8},{8,0},{1,9},{9,1},{2,10},{10,2},{3,11},{11,3},{4,12},{12,4},... | collective-permute-start | bytes 1671176 | tf_op jit(solution)/shard_map/ppermute | solution.py:665
  32.0 13.5 %all-to-all-start.1 = ((bf16[8,256,128]{2,1,0:T(8,128)(2,1)}), bf16[8,256,128]{2,1,0:T(8,128)(2,1)S(1)}, u32[]{:S(2)}, u32[]{:S(2)}) async-start(bf16[8,256,128]{2,1,0:T(8,128)(2,1)} %shard_map.171), calls=%async_computation.1 | async-start | bytes 1048576 | tf_op jit(solution)/shard_map/all_to_all | solution.py:235
  45.5 0.8 copy-start.1
  57.6 4.6 %copy-start = (bf16[128,2048]{1,0:T(8,128)(2,1)S(1)}, bf16[128,2048]{1,0:T(8,128)(2,1)}, u32[]{:S(2)}) copy-start(bf16[128,2048]{1,0:T(8,128)(2,1)} %get-tuple-element.55.refs_0_.z_ref) | copy-start | bytes 1572868
  57.6 51.7 %all-to-all-start.3 = ((bf16[8,96,2176]{2,1,0:T(8,128)(2,1)}), bf16[8,96,2176]{2,1,0:T(8,128)(2,1)}, u32[]{:S(2)}, u32[]{:S(2)}) async-start(bf16[8,96,2176]{2,1,0:T(8,128)(2,1)} %bitcast.51), calls=%async_computation.3 | async-start | bytes 6684672 | tf_op jit(solution)/shard_map/all_to_all | solution.py:656
  62.3 27.2 %collective-permute-start.3 = (bf16[128,2048]{1,0:T(8,128)(2,1)S(1)}, bf16[128,2048]{1,0:T(8,128)(2,1)S(1)}, u32[]{:S(2)}, u32[]{:S(2)}) collective-permute-start(bf16[128,2048]{1,0:T(8,128)(2,1)S(1)} %copy-done), channel_id=1, source_target_pairs={{0,16},{16,0},{1,17},{17,1},{2,18},{18,2},{3,19},{19,3},{4,20},{20... | collective-permute-start | bytes 1572872 | tf_op jit(solution)/shard_map/ppermute | solution.py:665
  65.8 24.9 %collective-permute-start.4 = (bf16[128,2048]{1,0:T(8,128)(2,1)S(1)}, bf16[128,2048]{1,0:T(8,128)(2,1)S(1)}, u32[]{:S(2)}, u32[]{:S(2)}) collective-permute-start(bf16[128,2048]{1,0:T(8,128)(2,1)S(1)} %copy-done), channel_id=1, source_target_pairs={{0,8},{8,0},{1,9},{9,1},{2,10},{10,2},{3,11},{11,3},{4,12},{12,4},... | collective-permute-start | bytes 1572872 | tf_op jit(solution)/shard_map/ppermute | solution.py:665
  89.5 13.7 %copy-start.12 = (bf16[128,2048]{1,0:T(8,128)(2,1)}, bf16[128,2048]{1,0:T(8,128)(2,1)S(1)}, u32[]{:S(2)}) copy-start(bf16[128,2048]{1,0:T(8,128)(2,1)S(1)} %collective-permute-done.3.refs_1_) | copy-start | bytes 1572868
  89.5 13.7 %collective-permute-start.5 = (bf16[128,2048]{1,0:T(8,128)(2,1)S(1)}, bf16[128,2048]{1,0:T(8,128)(2,1)S(1)}, u32[]{:S(2)}, u32[]{:S(2)}) collective-permute-start(bf16[128,2048]{1,0:T(8,128)(2,1)S(1)} %collective-permute-done.3.refs_1_), channel_id=1, source_target_pairs={{0,8},{8,0},{1,9},{9,1},{2,10},{10,2},{3,11},{11,3},{4,12},{12,4},... | collective-permute-start | bytes 1572872 | tf_op jit(solution)/shard_map/ppermute | solution.py:665
  90.7 12.5 %copy-start.15 = (bf16[128,2048]{1,0:T(8,128)(2,1)}, bf16[128,2048]{1,0:T(8,128)(2,1)S(1)}, u32[]{:S(2)}) copy-start(bf16[128,2048]{1,0:T(8,128)(2,1)S(1)} %collective-permute-done.4.refs_2_) | copy-start | bytes 1572868
  103.2 0.8 copy-start.16
  109.3 42.3 %all-to-all-start.2 = ((bf16[8,96,2048]{2,1,0:T(8,128)(2,1)}), bf16[8,96,2048]{2,1,0:T(8,128)(2,1)}, u32[]{:S(2)}, u32[]{:S(2)}) async-start(bf16[8,96,2048]{2,1,0:T(8,128)(2,1)} %bitcast.35), calls=%async_computation.2 | async-start | bytes 6291456 | tf_op jit(solution)/shard_map/all_to_all | solution.py:656
  164.0 12.6 %all-to-all-start.4 = ((bf16[8,96,128]{2,1,0:T(8,128)(2,1)}), bf16[8,96,128]{2,1,0:T(8,128)(2,1)S(1)}, u32[]{:S(2)}, u32[]{:S(2)}) async-start(bf16[8,96,128]{2,1,0:T(8,128)(2,1)} %bitcast.61), calls=%async_computation.4 | async-start | bytes 393216 | tf_op jit(solution)/shard_map/all_to_all | solution.py:656
  177.2 45.7 %all-to-all-start.5 = ((bf16[8,96,2048]{2,1,0:T(8,128)(2,1)}), bf16[8,96,2048]{2,1,0:T(8,128)(2,1)}, u32[]{:S(2)}, u32[]{:S(2)}) async-start(bf16[8,96,2048]{2,1,0:T(8,128)(2,1)} %bitcast.52), calls=%async_computation.5 | async-start | bytes 6291456 | tf_op jit(solution)/shard_map/all_to_all | solution.py:656
  184.0 5.4 %collective-permute-start.6 = (bf16[128,128]{1,0:T(8,128)(2,1)}, bf16[128,128]{1,0:T(8,128)(2,1)S(1)}, u32[]{:S(2)}, u32[]{:S(2)}) collective-permute-start(bf16[128,128]{1,0:T(8,128)(2,1)} %get-tuple-element.71), channel_id=1, source_target_pairs={{0,16},{8,24},{16,0},{24,8},{1,17},{9,25},{17,1},{25,9},{2,18},{10... | collective-permute-start | bytes 98312 | tf_op jit(solution)/shard_map/ppermute | solution.py:665
  184.5 5.0 %collective-permute-start.7 = (bf16[128,128]{1,0:T(8,128)(2,1)}, bf16[128,128]{1,0:T(8,128)(2,1)S(1)}, u32[]{:S(2)}, u32[]{:S(2)}) collective-permute-start(bf16[128,128]{1,0:T(8,128)(2,1)} %get-tuple-element.72), channel_id=1, source_target_pairs={{0,8},{8,0},{16,24},{24,16},{1,9},{9,1},{17,25},{25,17},{2,10},{10... | collective-permute-start | bytes 98312 | tf_op jit(solution)/shard_map/ppermute | solution.py:665
  186.2 5.9 %collective-permute-start.8 = (bf16[128,128]{1,0:T(8,128)(2,1)}, bf16[128,128]{1,0:T(8,128)(2,1)S(1)}, u32[]{:S(2)}, u32[]{:S(2)}) collective-permute-start(bf16[128,128]{1,0:T(8,128)(2,1)} %get-tuple-element.73), channel_id=1, source_target_pairs={{0,24},{8,16},{16,8},{24,0},{1,25},{9,17},{17,9},{25,1},{2,26},{10... | collective-permute-start | bytes 98312 | tf_op jit(solution)/shard_map/ppermute | solution.py:665
  189.4 2.7 copy-start.19
  189.5 2.7 copy-start.20
  197.1 13.1 %collective-permute-start.9 = (f32[32,2048]{1,0:T(8,128)}, f32[32,2048]{1,0:T(8,128)S(1)}, u32[]{:S(2)}, u32[]{:S(2)}) collective-permute-start(f32[32,2048]{1,0:T(8,128)} %get-tuple-element.76), channel_id=1, source_target_pairs={{0,16},{16,0},{1,17},{17,1},{2,18},{18,2},{3,19},{19,3},{4,20},{20... | collective-permute-start | bytes 786440 | tf_op jit(solution)/shard_map/ppermute | solution.py:665
  197.1 13.1 %copy-start.17 = (f32[32,2048]{1,0:T(8,128)S(1)}, f32[32,2048]{1,0:T(8,128)}, u32[]{:S(2)}) copy-start(f32[32,2048]{1,0:T(8,128)} %get-tuple-element.76) | copy-start | bytes 786436
  210.2 11.9 %collective-permute-start.10 = (f32[32,2048]{1,0:T(8,128)S(1)}, f32[32,2048]{1,0:T(8,128)S(1)}, u32[]{:S(2)}, u32[]{:S(2)}) collective-permute-start(f32[32,2048]{1,0:T(8,128)S(1)} %add.26), channel_id=1, source_target_pairs={{0,8},{8,0},{1,9},{9,1},{2,10},{10,2},{3,11},{11,3},{4,12},{12,4},... | collective-permute-start | bytes 786440 | tf_op jit(solution)/shard_map/ppermute | solution.py:665
  227.3 4.6 %copy-start.24 = (bf16[128,2048]{1,0:T(8,128)(2,1)S(1)}, bf16[128,2048]{1,0:T(8,128)(2,1)}, u32[]{:S(2)}) copy-start(bf16[128,2048]{1,0:T(8,128)(2,1)} %get-tuple-element.84) | copy-start | bytes 1572868
  227.3 6.7 %copy-start.23 = (bf16[128,2048]{1,0:T(8,128)(2,1)S(1)}, bf16[128,2048]{1,0:T(8,128)(2,1)}, u32[]{:S(2)}) copy-start(bf16[128,2048]{1,0:T(8,128)(2,1)} %get-tuple-element.83) | copy-start | bytes 1572868
  227.3 19.4 %copy-start.13 = (bf16[128,2048]{1,0:T(8,128)(2,1)S(1)}, bf16[128,2048]{1,0:T(8,128)(2,1)}, u32[]{:S(2)}) copy-start(bf16[128,2048]{1,0:T(8,128)(2,1)} %get-tuple-element.82) | copy-start | bytes 1572868
  227.3 52.0 %all-to-all-start.6 = ((bf16[8,96,2048]{2,1,0:T(8,128)(2,1)}), bf16[8,96,2048]{2,1,0:T(8,128)(2,1)}, u32[]{:S(2)}, u32[]{:S(2)}) async-start(bf16[8,96,2048]{2,1,0:T(8,128)(2,1)} %bitcast.53), calls=%async_computation.6 | async-start | bytes 6291456 | tf_op jit(solution)/shard_map/all_to_all | solution.py:656
  231.9 14.8 %collective-permute-start.11 = (bf16[128,2048]{1,0:T(8,128)(2,1)S(1)}, bf16[128,2048]{1,0:T(8,128)(2,1)S(1)}, u32[]{:S(2)}, u32[]{:S(2)}) collective-permute-start(bf16[128,2048]{1,0:T(8,128)(2,1)S(1)} %copy-done.24), channel_id=1, source_target_pairs={{0,8},{8,0},{1,9},{9,1},{2,10},{10,2},{3,11},{11,3},{4,12},{12,4},... | collective-permute-start | bytes 1572872 | tf_op jit(solution)/shard_map/ppermute | solution.py:665
  234.0 32.7 %collective-permute-start.13 = (bf16[128,2048]{1,0:T(8,128)(2,1)S(1)}, bf16[128,2048]{1,0:T(8,128)(2,1)S(1)}, u32[]{:S(2)}, u32[]{:S(2)}) collective-permute-start(bf16[128,2048]{1,0:T(8,128)(2,1)S(1)} %copy-done.23), channel_id=1, source_target_pairs={{0,8},{8,0},{1,9},{9,1},{2,10},{10,2},{3,11},{11,3},{4,12},{12,4},... | collective-permute-start | bytes 1572872 | tf_op jit(solution)/shard_map/ppermute | solution.py:665
  246.8 25.6 %collective-permute-start.12 = (bf16[128,2048]{1,0:T(8,128)(2,1)S(1)}, bf16[128,2048]{1,0:T(8,128)(2,1)S(1)}, u32[]{:S(2)}, u32[]{:S(2)}) collective-permute-start(bf16[128,2048]{1,0:T(8,128)(2,1)S(1)} %add_convert_fusion.1), channel_id=1, source_target_pairs={{0,16},{16,0},{1,17},{17,1},{2,18},{18,2},{3,19},{19,3},{4,20},{20... | collective-permute-start | bytes 1572872 | tf_op jit(solution)/shard_map/ppermute | solution.py:665
  266.6 5.8 %copy-start.10 = (bf16[128,2048]{1,0:T(8,128)(2,1)}, bf16[128,2048]{1,0:T(8,128)(2,1)S(1)}, u32[]{:S(2)}) copy-start(bf16[128,2048]{1,0:T(8,128)(2,1)S(1)} %collective-permute-done.13.refs_10_) | copy-start | bytes 1572868
  279.3 16.3 %all-to-all-start.7 = ((bf16[8,384,128]{2,1,0:T(8,128)(2,1)}), bf16[8,384,128]{2,1,0:T(8,128)(2,1)S(1)}, u32[]{:S(2)}, u32[]{:S(2)}) async-start(bf16[8,384,128]{2,1,0:T(8,128)(2,1)} %get-tuple-element.94), calls=%async_computation.7 | async-start | bytes 1572864 | tf_op jit(solution)/shard_map/all_to_all | solution.py:235
  287.4 14.9 %copy-start.11 = (bf16[128,2048]{1,0:T(8,128)(2,1)S(1)}, bf16[128,2048]{1,0:T(8,128)(2,1)}, u32[]{:S(2)}) copy-start(bf16[128,2048]{1,0:T(8,128)(2,1)} %get-tuple-element.89) | copy-start | bytes 1572868
  287.4 14.9 %collective-permute-start.14 = (bf16[128,2048]{1,0:T(8,128)(2,1)}, bf16[128,2048]{1,0:T(8,128)(2,1)}, u32[]{:S(2)}, u32[]{:S(2)}) collective-permute-start(bf16[128,2048]{1,0:T(8,128)(2,1)} %get-tuple-element.90), channel_id=1, source_target_pairs={{0,8},{8,0},{1,9},{9,1},{2,10},{10,2},{3,11},{11,3},{4,12},{12,4},... | collective-permute-start | bytes 1572872 | tf_op jit(solution)/shard_map/ppermute | solution.py:665
  295.6 0.9 copy-start.2
  298.6 16.1 %all-to-all-start.8 = ((bf16[8,384,128]{2,1,0:T(8,128)(2,1)}), bf16[8,384,128]{2,1,0:T(8,128)(2,1)S(1)}, u32[]{:S(2)}, u32[]{:S(2)}) async-start(bf16[8,384,128]{2,1,0:T(8,128)(2,1)} %shard_map.187), calls=%async_computation.8 | async-start | bytes 1572864 | tf_op jit(solution)/shard_map/all_to_all | solution.py:235
  302.2 22.7 %collective-permute-start.16 = (bf16[128,2048]{1,0:T(8,128)(2,1)}, bf16[128,2048]{1,0:T(8,128)(2,1)S(1)}, u32[]{:S(2)}, u32[]{:S(2)}) collective-permute-start(bf16[128,2048]{1,0:T(8,128)(2,1)} %get-tuple-element.91), channel_id=1, source_target_pairs={{0,8},{8,0},{1,9},{9,1},{2,10},{10,2},{3,11},{11,3},{4,12},{12,4},... | collective-permute-start | bytes 1572872 | tf_op jit(solution)/shard_map/ppermute | solution.py:665
  304.3 26.5 %collective-permute-start.15 = (bf16[128,2048]{1,0:T(8,128)(2,1)}, bf16[128,2048]{1,0:T(8,128)(2,1)S(1)}, u32[]{:S(2)}, u32[]{:S(2)}) collective-permute-start(bf16[128,2048]{1,0:T(8,128)(2,1)} %add_convert_fusion), channel_id=1, source_target_pairs={{0,16},{16,0},{1,17},{17,1},{2,18},{18,2},{3,19},{19,3},{4,20},{20... | collective-permute-start | bytes 1572872 | tf_op jit(solution)/shard_map/ppermute | solution.py:665
  314.7 0.9 copy-start.3
  324.9 5.9 %copy-start.8 = (bf16[128,2048]{1,0:T(8,128)(2,1)}, bf16[128,2048]{1,0:T(8,128)(2,1)S(1)}, u32[]{:S(2)}) copy-start(bf16[128,2048]{1,0:T(8,128)(2,1)S(1)} %collective-permute-done.16.refs_1_) | copy-start | bytes 1572868
  330.8 0.8 copy-start.9
  (3 other events, 2.1 us)

commit v5 on v4

--- a/solution.py
+++ b/solution.py
@@ -483,14 +483,14 @@
     total = z_ref[...].astype(F32) + mm_tn(pick_ref[:, :tokens], back_ref[...])
     for ref in more_refs:
         total += ref[...].astype(F32)
-    out_ref[...] = total.astype(BF16)
+    out_ref[...] = total
 
 
 def layer_output(z, pick, back, more):
     tokens, rows = z.shape[0], pick.shape[0]
     return call(
         output_kernel,
-        jax.ShapeDtypeStruct((tokens, D), BF16),
+        jax.ShapeDtypeStruct((tokens, D), F32),
         (D // HEADS,),
         [columns(tokens), whole(pick.shape), columns(rows)] + [columns(tokens)] * len(more),
         columns(tokens),
@@ -783,7 +783,8 @@
     later = to_heads(running_sum(there, True))
     grad_k, grad_v, grad_router = attention_late(k, v, later, gk, gv, experts)
     grad_router = grad_router.T
-    output = layer_output(z, pick, eo_back, eo_more)
+    own = layer_output(z, pick, after(eo_back, gq), [])
+    output = sum((x.astype(F32) for x in eo_more), own).astype(BF16)
     return (
         output[None],
         gq[None],

time: 337 us -> 335 us (level)
    unnamed x52 -> x48, local copies, waits for them, and re-layouts: 8.91 us -> 8.88 us
  transfers between devices with their start and end apart: 26 -> 26, of which waited for: 17 -> 17; matrix products, arithmetic and copies ran while one was open for 1% -> 1% of each run, Pallas kernels for 23% -> 24%
where the time goes in v5:
time: 335 us; the launch traced here: 333 us
  waiting for transfers between devices  156 us (47%)
  Pallas kernels  104 us (31%)
  starting transfers between devices  57.4 us (17%)
  local copies, waits for them, and re-layouts  8.88 us (3%)
  other arithmetic  6.25 us (2%)
    ppermute x17, waiting for transfers between devices, swap(): lax.ppermute(block, axis, [(i, i ^ by) for i in range(lax.axis_size(axis))])  98.6 us
    all_to_all x5, waiting for transfers between devices, exchange(): lax.all_to_all(shaped, 'ctx', split_axis=0, concat_axis=0, tiled=True)  30.7 us
    all_to_all x4, waiting for transfers between devices, to_heads(): return lax.all_to_all(block, 'ctx', split_axis=0, concat_axis=0, tiled=True)  26.6 us
    all_to_all x5, starting transfers between devices, exchange(): lax.all_to_all(shaped, 'ctx', split_axis=0, concat_axis=0, tiled=True)  21.7 us
    ppermute x17, starting transfers between devices, swap(): lax.ppermute(block, axis, [(i, i ^ by) for i in range(lax.axis_size(axis))])  21 us
    all_to_all x4, starting transfers between devices, to_heads(): return lax.all_to_all(block, 'ctx', split_axis=0, concat_axis=0, tiled=True)  14.7 us
    pallas_call x1, Pallas kernels, expert_forward(): call(expert_kernel, (inner, inner, inner, column, pair), (hidden // tile,...  12.3 us
    pallas_call x1, Pallas kernels, expert_weights(): call(weights_kernel, (jax.ShapeDtypeStruct((D, hidden), BF16), jax.ShapeD...  11.8 us
  transfers between devices with their start and end apart: 26, of which 17 were waited for; matrix products, arithmetic and copies ran while one was open for 1% of the time, Pallas kernels for 24%

profile of v5, /device:TPU:0, one launch (start us, length us, event | category | flops | bytes accessed | tf_op | source)
XLA Modules:
  0.0 333.2 jit_solution(5623001171237596944)
XLA Ops:
  2.6 4.1 %collective-permute-start = (bf16[128,2176]{1,0:T(8,128)(2,1)S(1)}, bf16[128,2176]{1,0:T(8,128)(2,1)S(1)}, u32[]{:S(2)}, u32[]{:S(2)}) collective-permute-start(bf16[128,2176]{1,0:T(8,128)(2,1)S(1)} %fusion.1.refs_0_), channel_id=1, source_target_pairs={{0,16},{16,0},{1,17},{17,1},{2,18},{18,2},{3,19},{19,3},{4,20},{20... | collective-permute-start | bytes 1671176 | tf_op jit(solution)/shard_map/ppermute | solution.py:665
  6.7 2.3 shard_map.170
  9.0 3.7 %all-to-all-start = ((bf16[8,256,128]{2,1,0:T(8,128)(2,1)}), bf16[8,256,128]{2,1,0:T(8,128)(2,1)S(1)}, u32[]{:S(2)}, u32[]{:S(2)}) async-start(bf16[8,256,128]{2,1,0:T(8,128)(2,1)} %bitcast.57), calls=%async_computation | async-start | bytes 1048576 | tf_op jit(solution)/shard_map/all_to_all | solution.py:235
  14.3 8.2 %all-to-all-done.in_ref = bf16[8,256,128]{2,1,0:T(8,128)(2,1)S(1)} async-done(((bf16[8,256,128]{2,1,0:T(8,128)(2,1)}), bf16[8,256,128]{2,1,0:T(8,128)(2,1)S(1)}, u32[]{:S(2)}, u32[]{:S(2)}) %all-to-all-start) | async-done | bytes 524320 | tf_op jit(solution)/shard_map/all_to_all | solution.py:235
  25.2 6.2 %collective-permute-done.refs_1_ = bf16[128,2176]{1,0:T(8,128)(2,1)S(1)} collective-permute-done((bf16[128,2176]{1,0:T(8,128)(2,1)S(1)}, bf16[128,2176]{1,0:T(8,128)(2,1)S(1)}, u32[]{:S(2)}, u32[]{:S(2)}) %collective-permute-start) | collective-permute-done | bytes 557088 | tf_op jit(solution)/shard_map/ppermute | solution.py:665
  32.0 3.7 %all-to-all-start.1 = ((bf16[8,256,128]{2,1,0:T(8,128)(2,1)}), bf16[8,256,128]{2,1,0:T(8,128)(2,1)S(1)}, u32[]{:S(2)}, u32[]{:S(2)}) async-start(bf16[8,256,128]{2,1,0:T(8,128)(2,1)} %shard_map.171), calls=%async_computation.1 | async-start | bytes 1048576 | tf_op jit(solution)/shard_map/all_to_all | solution.py:235
  36.8 8.7 %all-to-all-done.1 = bf16[8,256,128]{2,1,0:T(8,128)(2,1)S(1)} async-done(((bf16[8,256,128]{2,1,0:T(8,128)(2,1)}), bf16[8,256,128]{2,1,0:T(8,128)(2,1)S(1)}, u32[]{:S(2)}, u32[]{:S(2)}) %all-to-all-start.1) | async-done | bytes 524320 | tf_op jit(solution)/shard_map/all_to_all | solution.py:235
  46.3 5.3 %shard_map.172 = (bf16[128,2048]{1,0:T(8,128)(2,1)}, f32[128,2048]{1,0:T(8,128)}, f32[128,32]{1,0:T(8,128)}) custom-call(bf16[128,2048]{1,0:T(8,128)(2,1)} %bitcast.45, bf16[128,2048]{1,0:T(8,128)(2,1)} %bitcast.38, bf16[128,2048]{1,0:T(8,128)(2,1)} %bitcast.42, f32[16,128,128]{2,1,0:T(8,128)} %bitcast.50, bf16[16,128,128]{2,1,0:T(8,128)(2,1)} %bitcast.48, ...), custom_call_target="tpu_custom_call" | custom-call | flops 268435456 | bytes 4194304 | tf_op jit(solution)/shard_map/pallas_call | solution.py:286
  51.6 6.0 %shard_map.173 = (bf16[768,512]{1,0:T(8,128)(2,1)}, f32[512,32]{1,0:T(8,128)}, bf16[768,2176]{1,0:T(8,128)(2,1)}) custom-call(s32[1,1]{1,0:T(1,128)} %bitcast.8.plane_ref, bf16[128,2176]{1,0:T(8,128)(2,1)} %copy-done.7, bf16[128,2176]{1,0:T(8,128)(2,1)} %copy-done.20, bf16[128,2176]{1,0:T(8,128)(2,1)} %collective-permute-done.1.refs_2_, ...), custom_call_target="tpu_custom_call" | custom-call | flops 1610612736 | bytes 3145728 | tf_op jit(solution)/shard_map/pallas_call | solution.py:159
  57.6 4.6 %all-to-all-start.3 = ((bf16[8,96,2176]{2,1,0:T(8,128)(2,1)}), bf16[8,96,2176]{2,1,0:T(8,128)(2,1)}, u32[]{:S(2)}, u32[]{:S(2)}) async-start(bf16[8,96,2176]{2,1,0:T(8,128)(2,1)} %bitcast.52), calls=%async_computation.3 | async-start | bytes 6684672 | tf_op jit(solution)/shard_map/all_to_all | solution.py:656
  62.3 3.5 %collective-permute-start.3 = (bf16[128,2048]{1,0:T(8,128)(2,1)S(1)}, bf16[128,2048]{1,0:T(8,128)(2,1)S(1)}, u32[]{:S(2)}, u32[]{:S(2)}) collective-permute-start(bf16[128,2048]{1,0:T(8,128)(2,1)S(1)} %copy-done.1), channel_id=1, source_target_pairs={{0,16},{16,0},{1,17},{17,1},{2,18},{18,2},{3,19},{19,3},{4,20},{20... | collective-permute-start | bytes 1572872 | tf_op jit(solution)/shard_map/ppermute | solution.py:665
  65.8 23.7 %collective-permute-done.3.refs_1_ = bf16[128,2048]{1,0:T(8,128)(2,1)S(1)} collective-permute-done((bf16[128,2048]{1,0:T(8,128)(2,1)S(1)}, bf16[128,2048]{1,0:T(8,128)(2,1)S(1)}, u32[]{:S(2)}, u32[]{:S(2)}) %collective-permute-start.3) | collective-permute-done | bytes 524320 | tf_op jit(solution)/shard_map/ppermute | solution.py:665
  90.7 12.5 %collective-permute-done.5.refs_3_ = bf16[128,2048]{1,0:T(8,128)(2,1)S(1)} collective-permute-done((bf16[128,2048]{1,0:T(8,128)(2,1)S(1)}, bf16[128,2048]{1,0:T(8,128)(2,1)S(1)}, u32[]{:S(2)}, u32[]{:S(2)}) %collective-permute-start.5) | collective-permute-done | bytes 524320 | tf_op jit(solution)/shard_map/ppermute | solution.py:665
  104.0 5.3 %shard_map.174 = bf16[768,2048]{1,0:T(8,128)(2,1)} custom-call(bf16[768,512]{1,0:T(8,128)(2,1)} %get-tuple-element.62.pick_ref.refs_2_.refs_4_, f32[512,32]{1,0:T(8,128)} %get-tuple-element.63.chosen_ref, bf16[128,2048]{1,0:T(8,128)(2,1)} %get-tuple-element.56.refs_0_.z_ref, bf16[128,2048]{1,0:T(8,128)(2,1)} %copy-done.10, bf16[128,2048]{1,0:T(8,128)(2,1)} %copy-done.13, ...), custom_call_target="tpu_custom_call" | custom-call | flops 1610612736 | bytes 3145728 | tf_op jit(solution)/shard_map/pallas_call | solution.py:137
  109.3 4.5 %all-to-all-start.2 = ((bf16[8,96,2048]{2,1,0:T(8,128)(2,1)}), bf16[8,96,2048]{2,1,0:T(8,128)(2,1)}, u32[]{:S(2)}, u32[]{:S(2)}) async-start(bf16[8,96,2048]{2,1,0:T(8,128)(2,1)} %bitcast.36), calls=%async_computation.2 | async-start | bytes 6291456 | tf_op jit(solution)/shard_map/all_to_all | solution.py:656
  114.4 6.6 %shard_map.175.dh_ref = f32[768,768]{1,0:T(8,128)} custom-call(bf16[768,2176]{1,0:T(8,128)(2,1)} %bitcast.15.dy_ref.mask_ref, bf16[768,2048]{1,0:T(8,128)(2,1)} %bitcast.68), custom_call_target="tpu_custom_call" | custom-call | flops 2415919104 | bytes 6291456 | tf_op jit(solution)/shard_map/pallas_call | solution.py:509
  121.1 30.7 %all-to-all-done.2 = bf16[8,96,2048]{2,1,0:T(8,128)(2,1)} async-done(((bf16[8,96,2048]{2,1,0:T(8,128)(2,1)}), bf16[8,96,2048]{2,1,0:T(8,128)(2,1)}, u32[]{:S(2)}, u32[]{:S(2)}) %all-to-all-start.2) | async-done | bytes 3145760 | tf_op jit(solution)/shard_map/all_to_all | solution.py:656
  151.7 12.3 %shard_map.176 = (bf16[768,768]{1,0:T(8,128)(2,1)}, bf16[768,768]{1,0:T(8,128)(2,1)}, bf16[768,768]{1,0:T(8,128)(2,1)}, f32[768,1]{1,0:T(8,128)}, bf16[768,128]{1,0:T(8,128)(2,1)}) custom-call(s32[1,2]{1,0:T(1,128)} %add_bitcast_fusion.me_ref, bf16[768,2048]{1,0:T(8,128)(2,1)} %bitcast.13.z_ref, bf16[768,2176]{1,0:T(8,128)(2,1)} %bitcast.15.dy_ref.mask_ref, ...), custom_call_target="tpu_custom_call" | custom-call | flops 4831838208 | bytes 9437184 | tf_op jit(solution)/shard_map/pallas_call | solution.py:569
  164.0 3.4 %all-to-all-start.4 = ((bf16[8,96,128]{2,1,0:T(8,128)(2,1)}), bf16[8,96,128]{2,1,0:T(8,128)(2,1)S(1)}, u32[]{:S(2)}, u32[]{:S(2)}) async-start(bf16[8,96,128]{2,1,0:T(8,128)(2,1)} %bitcast.61), calls=%async_computation.4 | async-start | bytes 393216 | tf_op jit(solution)/shard_map/all_to_all | solution.py:656
  167.4 9.1 %shard_map.177 = bf16[768,2048]{1,0:T(8,128)(2,1)} custom-call(bf16[768,768]{1,0:T(8,128)(2,1)} %get-tuple-element.68.dgp_ref, bf16[768,768]{1,0:T(8,128)(2,1)} %get-tuple-element.69.dup_ref, bf16[2048,768]{1,0:T(8,128)(2,1)} %bitcast.65, bf16[2048,768]{1,0:T(8,128)(2,1)} %bitcast.67, f32[768,1]{1,0:T(8,128)} %get-tuple-element.70.weight_ref), custom_call_target="tpu_custom_call" | custom-call | flops 4831838208 | bytes 9437184 | tf_op jit(solution)/shard_map/pallas_call | solution.py:597
  177.3 4.6 %all-to-all-start.5 = ((bf16[8,96,2048]{2,1,0:T(8,128)(2,1)}), bf16[8,96,2048]{2,1,0:T(8,128)(2,1)}, u32[]{:S(2)}, u32[]{:S(2)}) async-start(bf16[8,96,2048]{2,1,0:T(8,128)(2,1)} %bitcast.53), calls=%async_computation.5 | async-start | bytes 6291456 | tf_op jit(solution)/shard_map/all_to_all | solution.py:656
  181.9 2.1 shard_map.178
  186.2 2.2 collective-permute-start.8
  189.5 2.7 collective-permute-done.8.refs_6_
  192.8 4.3 %shard_map.179 = (bf16[3,128,32]{2,1,0:T(8,128)(2,1)}, f32[32,2048]{1,0:T(8,128)}) custom-call(bf16[128,2048]{1,0:T(8,128)(2,1)} %get-tuple-element.56.refs_0_.z_ref, bf16[768,128]{1,0:T(8,128)(2,1)} %bitcast.59, bf16[768,512]{1,0:T(8,128)(2,1)} %get-tuple-element.62.pick_ref.refs_2_.refs_4_, f32[128,32]{1,0:T(8,128)} %get-tuple-element.67.refs_3_, ...), custom_call_target="tpu_custom_call" | custom-call | flops 50331648 | bytes 524288 | tf_op jit(solution)/shard_map/pallas_call | solution.py:336
  197.1 6.4 %shard_map.180 = bf16[768,2048]{1,0:T(8,128)(2,1)} custom-call(bf16[768,768]{1,0:T(8,128)(2,1)} %get-tuple-element.76.hid_ref, bf16[768,2048]{1,0:T(8,128)(2,1)} %bitcast.69, f32[768,1]{1,0:T(8,128)} %get-tuple-element.70.weight_ref), custom_call_target="tpu_custom_call" | custom-call | flops 2415919104 | bytes 6291456 | tf_op jit(solution)/shard_map/pallas_call | solution.py:614
  203.5 6.7 %collective-permute-done.9 = f32[32,2048]{1,0:T(8,128)S(1)} collective-permute-done((f32[32,2048]{1,0:T(8,128)}, f32[32,2048]{1,0:T(8,128)S(1)}, u32[]{:S(2)}, u32[]{:S(2)}) %collective-permute-start.9) | collective-permute-done | bytes 262176 | tf_op jit(solution)/shard_map/ppermute | solution.py:665
  210.4 11.8 %shard_map.181 = (bf16[2048,768]{1,0:T(8,128)(2,1)}, bf16[2048,768]{1,0:T(8,128)(2,1)}, bf16[768,2048]{1,0:T(8,128)(2,1)}) custom-call(bf16[768,2048]{1,0:T(8,128)(2,1)} %bitcast.13.z_ref, bf16[768,2176]{1,0:T(8,128)(2,1)} %bitcast.15.dy_ref.mask_ref, bf16[768,768]{1,0:T(8,128)(2,1)} %get-tuple-element.76.hid_ref, ...), custom_call_target="tpu_custom_call" | custom-call | flops 7247757312 | bytes 15728640 | tf_op jit(solution)/shard_map/pallas_call | solution.py:638
  222.9 4.4 %shard_map.182 = (bf16[128,2048]{1,0:T(8,128)(2,1)}, bf16[128,2048]{1,0:T(8,128)(2,1)}, bf16[128,2048]{1,0:T(8,128)(2,1)}) custom-call(bf16[768,512]{1,0:T(8,128)(2,1)} %get-tuple-element.62.pick_ref.refs_2_.refs_4_, bf16[768,2048]{1,0:T(8,128)(2,1)} %bitcast.22.back_ref.refs_3_), custom_call_target="tpu_custom_call" | custom-call | flops 1207959552 | bytes 3145728 | tf_op jit(solution)/shard_map/pallas_call | solution.py:187
  227.3 4.6 %all-to-all-start.6 = ((bf16[8,96,2048]{2,1,0:T(8,128)(2,1)}), bf16[8,96,2048]{2,1,0:T(8,128)(2,1)}, u32[]{:S(2)}, u32[]{:S(2)}) async-start(bf16[8,96,2048]{2,1,0:T(8,128)(2,1)} %bitcast.54), calls=%async_computation.6 | async-start | bytes 6291456 | tf_op jit(solution)/shard_map/all_to_all | solution.py:656
  231.9 2.1 collective-permute-start.11
  234.1 12.6 %collective-permute-done.11 = bf16[128,2048]{1,0:T(8,128)(2,1)S(1)} collective-permute-done((bf16[128,2048]{1,0:T(8,128)(2,1)S(1)}, bf16[128,2048]{1,0:T(8,128)(2,1)S(1)}, u32[]{:S(2)}, u32[]{:S(2)}) %collective-permute-start.11) | collective-permute-done | bytes 524320 | tf_op jit(solution)/shard_map/ppermute | solution.py:665
  246.9 2.2 collective-permute-start.12
  249.1 17.6 %collective-permute-done.13.refs_10_ = bf16[128,2048]{1,0:T(8,128)(2,1)S(1)} collective-permute-done((bf16[128,2048]{1,0:T(8,128)(2,1)S(1)}, bf16[128,2048]{1,0:T(8,128)(2,1)S(1)}, u32[]{:S(2)}, u32[]{:S(2)}) %collective-permute-start.13) | collective-permute-done | bytes 524320 | tf_op jit(solution)/shard_map/ppermute | solution.py:665
  266.7 5.8 %collective-permute-done.12.refs_9_ = bf16[128,2048]{1,0:T(8,128)(2,1)S(1)} collective-permute-done((bf16[128,2048]{1,0:T(8,128)(2,1)S(1)}, bf16[128,2048]{1,0:T(8,128)(2,1)S(1)}, u32[]{:S(2)}, u32[]{:S(2)}) %collective-permute-start.12) | collective-permute-done | bytes 524320 | tf_op jit(solution)/shard_map/ppermute | solution.py:665
  273.3 6.0 %shard_map.183 = (bf16[128,2048]{1,0:T(8,128)(2,1)}, bf16[8,384,128]{2,1,0:T(8,128)(2,1)}) custom-call(bf16[128,2048]{1,0:T(8,128)(2,1)} %bitcast.46, f32[128,2048]{1,0:T(8,128)} %get-tuple-element.87.refs_1_, bf16[128,2048]{1,0:T(8,128)(2,1)} %bitcast.56, bf16[768,2048]{1,0:T(8,128)(2,1)} %bitcast.22.back_ref.refs_3_, ...), custom_call_target="tpu_custom_call" | custom-call | flops 520093696 | bytes 7340032 | tf_op jit(solution)/shard_map/pallas_call | solution.py:387
  279.3 3.7 %all-to-all-start.7 = ((bf16[8,384,128]{2,1,0:T(8,128)(2,1)}), bf16[8,384,128]{2,1,0:T(8,128)(2,1)S(1)}, u32[]{:S(2)}, u32[]{:S(2)}) async-start(bf16[8,384,128]{2,1,0:T(8,128)(2,1)} %get-tuple-element.96), calls=%async_computation.7 | async-start | bytes 1572864 | tf_op jit(solution)/shard_map/all_to_all | solution.py:235
  283.0 4.4 %shard_map.184 = (bf16[128,2048]{1,0:T(8,128)(2,1)}, bf16[128,2048]{1,0:T(8,128)(2,1)}, bf16[128,2048]{1,0:T(8,128)(2,1)}) custom-call(bf16[768,512]{1,0:T(8,128)(2,1)} %get-tuple-element.62.pick_ref.refs_2_.refs_4_, bf16[768,2048]{1,0:T(8,128)(2,1)} %bitcast.24.back_ref), custom_call_target="tpu_custom_call" | custom-call | flops 1207959552 | bytes 3145728 | tf_op jit(solution)/shard_map/pallas_call | solution.py:187
  287.4 8.2 %all-to-all-done.7.in_ref = bf16[8,384,128]{2,1,0:T(8,128)(2,1)S(1)} async-done(((bf16[8,384,128]{2,1,0:T(8,128)(2,1)}), bf16[8,384,128]{2,1,0:T(8,128)(2,1)S(1)}, u32[]{:S(2)}, u32[]{:S(2)}) %all-to-all-start.7) | async-done | bytes 786464 | tf_op jit(solution)/shard_map/all_to_all | solution.py:235
  296.5 2.1 shard_map.187
  298.6 3.5 %all-to-all-start.8 = ((bf16[8,384,128]{2,1,0:T(8,128)(2,1)}), bf16[8,384,128]{2,1,0:T(8,128)(2,1)S(1)}, u32[]{:S(2)}, u32[]{:S(2)}) async-start(bf16[8,384,128]{2,1,0:T(8,128)(2,1)} %shard_map.187), calls=%async_computation.8 | async-start | bytes 1572864 | tf_op jit(solution)/shard_map/all_to_all | solution.py:235
  304.4 2.2 collective-permute-start.15
  306.6 6.6 %shard_map.185 = (bf16[128,2048]{1,0:T(8,128)(2,1)}, f32[128,2048]{1,0:T(8,128)}, f32[128,2048]{1,0:T(8,128)}) custom-call(bf16[128,2048]{1,0:T(8,128)(2,1)} %bitcast.47, bf16[128,2048]{1,0:T(8,128)(2,1)} %bitcast.39, bf16[128,2048]{1,0:T(8,128)(2,1)} %bitcast.43, bf16[128,2048]{1,0:T(8,128)(2,1)} %get-tuple-element.93.datt_ref, f32[16,128,128]{2,1,0:T(8,128)} %bitcast.51, ...), custom_call_target="tpu_custom_call" | custom-call | flops 469762048 | bytes 5767168 | tf_op jit(solution)/shard_map/pallas_call | solution.py:429
  315.6 3.3 shard_map.188
  318.9 3.5 %shard_map.186 = f32[128,2048]{1,0:T(8,128)} custom-call(bf16[128,2048]{1,0:T(8,128)(2,1)} %get-tuple-element.56.refs_0_.z_ref, bf16[768,512]{1,0:T(8,128)(2,1)} %get-tuple-element.62.pick_ref.refs_2_.refs_4_, bf16[768,2048]{1,0:T(8,128)(2,1)} %bitcast.24.back_ref), custom_call_target="tpu_custom_call" | custom-call | flops 402653184 | bytes 3145728 | tf_op jit(solution)/shard_map/pallas_call | solution.py:491
  322.4 2.5 collective-permute-done.16
  324.9 6.0 %collective-permute-done.15 = bf16[128,2048]{1,0:T(8,128)(2,1)} collective-permute-done((bf16[128,2048]{1,0:T(8,128)(2,1)S(1)}, bf16[128,2048]{1,0:T(8,128)(2,1)}, u32[]{:S(2)}, u32[]{:S(2)}) %collective-permute-start.15) | collective-permute-done | bytes 524320 | tf_op jit(solution)/shard_map/ppermute | solution.py:665
  330.9 2.3 fusion.2
  (79 shorter events, 23.1 us)
Async XLA Ops:
  0.6 35.1 %copy-start.16 = (bf16[2048,32]{0,1:T(8,128)(2,1)S(1)}, bf16[2048,32]{0,1:T(8,128)(2,1)}, u32[]{:S(2)}) copy-start(bf16[2048,32]{0,1:T(8,128)(2,1)} %param.16) | copy-start | bytes 393220
  1.5 35.3 %copy-start.6 = (s32[1,128,4]{2,1,0:T(8,128)}, s32[1,128,4]{2,1,0:T(8,128)S(1)}, u32[]{:S(2)}) copy-start(s32[1,128,4]{2,1,0:T(8,128)S(1)} %copy.19) | copy-start | bytes 6148
  2.6 49.0 %copy-start.7 = (bf16[128,2176]{1,0:T(8,128)(2,1)}, bf16[128,2176]{1,0:T(8,128)(2,1)S(1)}, u32[]{:S(2)}) copy-start(bf16[128,2176]{1,0:T(8,128)(2,1)S(1)} %fusion.1.refs_0_) | copy-start | bytes 1671172
  2.6 28.8 %collective-permute-start = (bf16[128,2176]{1,0:T(8,128)(2,1)S(1)}, bf16[128,2176]{1,0:T(8,128)(2,1)S(1)}, u32[]{:S(2)}, u32[]{:S(2)}) collective-permute-start(bf16[128,2176]{1,0:T(8,128)(2,1)S(1)} %fusion.1.refs_0_), channel_id=1, source_target_pairs={{0,16},{16,0},{1,17},{17,1},{2,18},{18,2},{3,19},{19,3},{4,20},{20... | collective-permute-start | bytes 1671176 | tf_op jit(solution)/shard_map/ppermute | solution.py:665
  9.0 13.5 %all-to-all-start = ((bf16[8,256,128]{2,1,0:T(8,128)(2,1)}), bf16[8,256,128]{2,1,0:T(8,128)(2,1)S(1)}, u32[]{:S(2)}, u32[]{:S(2)}) async-start(bf16[8,256,128]{2,1,0:T(8,128)(2,1)} %bitcast.57), calls=%async_computation | async-start | bytes 1048576 | tf_op jit(solution)/shard_map/all_to_all | solution.py:235
  12.7 38.9 %collective-permute-start.1 = (bf16[128,2176]{1,0:T(8,128)(2,1)S(1)}, bf16[128,2176]{1,0:T(8,128)(2,1)}, u32[]{:S(2)}, u32[]{:S(2)}) collective-permute-start(bf16[128,2176]{1,0:T(8,128)(2,1)S(1)} %fusion.1.refs_0_), channel_id=1, source_target_pairs={{0,8},{8,0},{1,9},{9,1},{2,10},{10,2},{3,11},{11,3},{4,12},{12,4},... | collective-permute-start | bytes 1671176 | tf_op jit(solution)/shard_map/ppermute | solution.py:665
  22.5 0.8 copy-start.4
  31.4 20.3 %copy-start.20 = (bf16[128,2176]{1,0:T(8,128)(2,1)}, bf16[128,2176]{1,0:T(8,128)(2,1)S(1)}, u32[]{:S(2)}) copy-start(bf16[128,2176]{1,0:T(8,128)(2,1)S(1)} %collective-permute-done.refs_1_) | copy-start | bytes 1671172
  31.4 20.2 %collective-permute-start.2 = (bf16[128,2176]{1,0:T(8,128)(2,1)S(1)}, bf16[128,2176]{1,0:T(8,128)(2,1)}, u32[]{:S(2)}, u32[]{:S(2)}) collective-permute-start(bf16[128,2176]{1,0:T(8,128)(2,1)S(1)} %collective-permute-done.refs_1_), channel_id=1, source_target_pairs={{0,8},{8,0},{1,9},{9,1},{2,10},{10,2},{3,11},{11,3},{4,12},{12,4},... | collective-permute-start | bytes 1671176 | tf_op jit(solution)/shard_map/ppermute | solution.py:665
  32.0 13.5 %all-to-all-start.1 = ((bf16[8,256,128]{2,1,0:T(8,128)(2,1)}), bf16[8,256,128]{2,1,0:T(8,128)(2,1)S(1)}, u32[]{:S(2)}, u32[]{:S(2)}) async-start(bf16[8,256,128]{2,1,0:T(8,128)(2,1)} %shard_map.171), calls=%async_computation.1 | async-start | bytes 1048576 | tf_op jit(solution)/shard_map/all_to_all | solution.py:235
  45.5 0.8 copy-start
  57.6 4.6 %copy-start.1 = (bf16[128,2048]{1,0:T(8,128)(2,1)S(1)}, bf16[128,2048]{1,0:T(8,128)(2,1)}, u32[]{:S(2)}) copy-start(bf16[128,2048]{1,0:T(8,128)(2,1)} %get-tuple-element.56.refs_0_.z_ref) | copy-start | bytes 1572868
  57.6 51.7 %all-to-all-start.3 = ((bf16[8,96,2176]{2,1,0:T(8,128)(2,1)}), bf16[8,96,2176]{2,1,0:T(8,128)(2,1)}, u32[]{:S(2)}, u32[]{:S(2)}) async-start(bf16[8,96,2176]{2,1,0:T(8,128)(2,1)} %bitcast.52), calls=%async_computation.3 | async-start | bytes 6684672 | tf_op jit(solution)/shard_map/all_to_all | solution.py:656
  62.3 27.2 %collective-permute-start.3 = (bf16[128,2048]{1,0:T(8,128)(2,1)S(1)}, bf16[128,2048]{1,0:T(8,128)(2,1)S(1)}, u32[]{:S(2)}, u32[]{:S(2)}) collective-permute-start(bf16[128,2048]{1,0:T(8,128)(2,1)S(1)} %copy-done.1), channel_id=1, source_target_pairs={{0,16},{16,0},{1,17},{17,1},{2,18},{18,2},{3,19},{19,3},{4,20},{20... | collective-permute-start | bytes 1572872 | tf_op jit(solution)/shard_map/ppermute | solution.py:665
  65.8 24.9 %collective-permute-start.4 = (bf16[128,2048]{1,0:T(8,128)(2,1)S(1)}, bf16[128,2048]{1,0:T(8,128)(2,1)S(1)}, u32[]{:S(2)}, u32[]{:S(2)}) collective-permute-start(bf16[128,2048]{1,0:T(8,128)(2,1)S(1)} %copy-done.1), channel_id=1, source_target_pairs={{0,8},{8,0},{1,9},{9,1},{2,10},{10,2},{3,11},{11,3},{4,12},{12,4},... | collective-permute-start | bytes 1572872 | tf_op jit(solution)/shard_map/ppermute | solution.py:665
  89.5 13.7 %copy-start.10 = (bf16[128,2048]{1,0:T(8,128)(2,1)}, bf16[128,2048]{1,0:T(8,128)(2,1)S(1)}, u32[]{:S(2)}) copy-start(bf16[128,2048]{1,0:T(8,128)(2,1)S(1)} %collective-permute-done.3.refs_1_) | copy-start | bytes 1572868
  89.5 13.7 %collective-permute-start.5 = (bf16[128,2048]{1,0:T(8,128)(2,1)S(1)}, bf16[128,2048]{1,0:T(8,128)(2,1)S(1)}, u32[]{:S(2)}, u32[]{:S(2)}) collective-permute-start(bf16[128,2048]{1,0:T(8,128)(2,1)S(1)} %collective-permute-done.3.refs_1_), channel_id=1, source_target_pairs={{0,8},{8,0},{1,9},{9,1},{2,10},{10,2},{3,11},{11,3},{4,12},{12,4},... | collective-permute-start | bytes 1572872 | tf_op jit(solution)/shard_map/ppermute | solution.py:665
  90.7 12.5 %copy-start.13 = (bf16[128,2048]{1,0:T(8,128)(2,1)}, bf16[128,2048]{1,0:T(8,128)(2,1)S(1)}, u32[]{:S(2)}) copy-start(bf16[128,2048]{1,0:T(8,128)(2,1)S(1)} %collective-permute-done.4.refs_2_) | copy-start | bytes 1572868
  103.2 0.8 copy-start.14
  109.3 42.4 %all-to-all-start.2 = ((bf16[8,96,2048]{2,1,0:T(8,128)(2,1)}), bf16[8,96,2048]{2,1,0:T(8,128)(2,1)}, u32[]{:S(2)}, u32[]{:S(2)}) async-start(bf16[8,96,2048]{2,1,0:T(8,128)(2,1)} %bitcast.36), calls=%async_computation.2 | async-start | bytes 6291456 | tf_op jit(solution)/shard_map/all_to_all | solution.py:656
  164.0 12.6 %all-to-all-start.4 = ((bf16[8,96,128]{2,1,0:T(8,128)(2,1)}), bf16[8,96,128]{2,1,0:T(8,128)(2,1)S(1)}, u32[]{:S(2)}, u32[]{:S(2)}) async-start(bf16[8,96,128]{2,1,0:T(8,128)(2,1)} %bitcast.61), calls=%async_computation.4 | async-start | bytes 393216 | tf_op jit(solution)/shard_map/all_to_all | solution.py:656
  176.6 0.7 copy-start.5
  177.3 45.7 %all-to-all-start.5 = ((bf16[8,96,2048]{2,1,0:T(8,128)(2,1)}), bf16[8,96,2048]{2,1,0:T(8,128)(2,1)}, u32[]{:S(2)}, u32[]{:S(2)}) async-start(bf16[8,96,2048]{2,1,0:T(8,128)(2,1)} %bitcast.53), calls=%async_computation.5 | async-start | bytes 6291456 | tf_op jit(solution)/shard_map/all_to_all | solution.py:656
  184.1 5.4 %collective-permute-start.6 = (bf16[128,128]{1,0:T(8,128)(2,1)}, bf16[128,128]{1,0:T(8,128)(2,1)S(1)}, u32[]{:S(2)}, u32[]{:S(2)}) collective-permute-start(bf16[128,128]{1,0:T(8,128)(2,1)} %get-tuple-element.72), channel_id=1, source_target_pairs={{0,16},{8,24},{16,0},{24,8},{1,17},{9,25},{17,1},{25,9},{2,18},{10... | collective-permute-start | bytes 98312 | tf_op jit(solution)/shard_map/ppermute | solution.py:665
  184.5 5.0 %collective-permute-start.7 = (bf16[128,128]{1,0:T(8,128)(2,1)}, bf16[128,128]{1,0:T(8,128)(2,1)S(1)}, u32[]{:S(2)}, u32[]{:S(2)}) collective-permute-start(bf16[128,128]{1,0:T(8,128)(2,1)} %get-tuple-element.73), channel_id=1, source_target_pairs={{0,8},{8,0},{16,24},{24,16},{1,9},{9,1},{17,25},{25,17},{2,10},{10... | collective-permute-start | bytes 98312 | tf_op jit(solution)/shard_map/ppermute | solution.py:665
  186.2 5.9 %collective-permute-start.8 = (bf16[128,128]{1,0:T(8,128)(2,1)}, bf16[128,128]{1,0:T(8,128)(2,1)S(1)}, u32[]{:S(2)}, u32[]{:S(2)}) collective-permute-start(bf16[128,128]{1,0:T(8,128)(2,1)} %get-tuple-element.74), channel_id=1, source_target_pairs={{0,24},{8,16},{16,8},{24,0},{1,25},{9,17},{17,9},{25,1},{2,26},{10... | collective-permute-start | bytes 98312 | tf_op jit(solution)/shard_map/ppermute | solution.py:665
  189.5 2.7 copy-start.17
  189.5 2.7 copy-start.18
  197.1 13.2 %collective-permute-start.9 = (f32[32,2048]{1,0:T(8,128)}, f32[32,2048]{1,0:T(8,128)S(1)}, u32[]{:S(2)}, u32[]{:S(2)}) collective-permute-start(f32[32,2048]{1,0:T(8,128)} %get-tuple-element.77), channel_id=1, source_target_pairs={{0,16},{16,0},{1,17},{17,1},{2,18},{18,2},{3,19},{19,3},{4,20},{20... | collective-permute-start | bytes 786440 | tf_op jit(solution)/shard_map/ppermute | solution.py:665
  197.1 13.2 %copy-start.15 = (f32[32,2048]{1,0:T(8,128)S(1)}, f32[32,2048]{1,0:T(8,128)}, u32[]{:S(2)}) copy-start(f32[32,2048]{1,0:T(8,128)} %get-tuple-element.77) | copy-start | bytes 786436
  210.3 11.9 %collective-permute-start.10 = (f32[32,2048]{1,0:T(8,128)S(1)}, f32[32,2048]{1,0:T(8,128)S(1)}, u32[]{:S(2)}, u32[]{:S(2)}) collective-permute-start(f32[32,2048]{1,0:T(8,128)S(1)} %add.32), channel_id=1, source_target_pairs={{0,8},{8,0},{1,9},{9,1},{2,10},{10,2},{3,11},{11,3},{4,12},{12,4},... | collective-permute-start | bytes 786440 | tf_op jit(solution)/shard_map/ppermute | solution.py:665
  227.3 4.6 %copy-start.22 = (bf16[128,2048]{1,0:T(8,128)(2,1)S(1)}, bf16[128,2048]{1,0:T(8,128)(2,1)}, u32[]{:S(2)}) copy-start(bf16[128,2048]{1,0:T(8,128)(2,1)} %get-tuple-element.85) | copy-start | bytes 1572868
  227.3 6.7 %copy-start.21 = (bf16[128,2048]{1,0:T(8,128)(2,1)S(1)}, bf16[128,2048]{1,0:T(8,128)(2,1)}, u32[]{:S(2)}) copy-start(bf16[128,2048]{1,0:T(8,128)(2,1)} %get-tuple-element.84) | copy-start | bytes 1572868
  227.3 19.4 %copy-start.11 = (bf16[128,2048]{1,0:T(8,128)(2,1)S(1)}, bf16[128,2048]{1,0:T(8,128)(2,1)}, u32[]{:S(2)}) copy-start(bf16[128,2048]{1,0:T(8,128)(2,1)} %get-tuple-element.83) | copy-start | bytes 1572868
  227.3 52.0 %all-to-all-start.6 = ((bf16[8,96,2048]{2,1,0:T(8,128)(2,1)}), bf16[8,96,2048]{2,1,0:T(8,128)(2,1)}, u32[]{:S(2)}, u32[]{:S(2)}) async-start(bf16[8,96,2048]{2,1,0:T(8,128)(2,1)} %bitcast.54), calls=%async_computation.6 | async-start | bytes 6291456 | tf_op jit(solution)/shard_map/all_to_all | solution.py:656
  231.9 14.8 %collective-permute-start.11 = (bf16[128,2048]{1,0:T(8,128)(2,1)S(1)}, bf16[128,2048]{1,0:T(8,128)(2,1)S(1)}, u32[]{:S(2)}, u32[]{:S(2)}) collective-permute-start(bf16[128,2048]{1,0:T(8,128)(2,1)S(1)} %copy-done.22), channel_id=1, source_target_pairs={{0,8},{8,0},{1,9},{9,1},{2,10},{10,2},{3,11},{11,3},{4,12},{12,4},... | collective-permute-start | bytes 1572872 | tf_op jit(solution)/shard_map/ppermute | solution.py:665
  234.0 32.6 %collective-permute-start.13 = (bf16[128,2048]{1,0:T(8,128)(2,1)S(1)}, bf16[128,2048]{1,0:T(8,128)(2,1)S(1)}, u32[]{:S(2)}, u32[]{:S(2)}) collective-permute-start(bf16[128,2048]{1,0:T(8,128)(2,1)S(1)} %copy-done.21), channel_id=1, source_target_pairs={{0,8},{8,0},{1,9},{9,1},{2,10},{10,2},{3,11},{11,3},{4,12},{12,4},... | collective-permute-start | bytes 1572872 | tf_op jit(solution)/shard_map/ppermute | solution.py:665
  246.9 25.6 %collective-permute-start.12 = (bf16[128,2048]{1,0:T(8,128)(2,1)S(1)}, bf16[128,2048]{1,0:T(8,128)(2,1)S(1)}, u32[]{:S(2)}, u32[]{:S(2)}) collective-permute-start(bf16[128,2048]{1,0:T(8,128)(2,1)S(1)} %add_convert_fusion.2), channel_id=1, source_target_pairs={{0,16},{16,0},{1,17},{17,1},{2,18},{18,2},{3,19},{19,3},{4,20},{20... | collective-permute-start | bytes 1572872 | tf_op jit(solution)/shard_map/ppermute | solution.py:665
  266.7 5.8 %copy-start.8 = (bf16[128,2048]{1,0:T(8,128)(2,1)}, bf16[128,2048]{1,0:T(8,128)(2,1)S(1)}, u32[]{:S(2)}) copy-start(bf16[128,2048]{1,0:T(8,128)(2,1)S(1)} %collective-permute-done.13.refs_10_) | copy-start | bytes 1572868
  272.5 0.8 copy-start.12
  279.3 16.3 %all-to-all-start.7 = ((bf16[8,384,128]{2,1,0:T(8,128)(2,1)}), bf16[8,384,128]{2,1,0:T(8,128)(2,1)S(1)}, u32[]{:S(2)}, u32[]{:S(2)}) async-start(bf16[8,384,128]{2,1,0:T(8,128)(2,1)} %get-tuple-element.96), calls=%async_computation.7 | async-start | bytes 1572864 | tf_op jit(solution)/shard_map/all_to_all | solution.py:235
  287.4 14.9 %collective-permute-start.14 = (bf16[128,2048]{1,0:T(8,128)(2,1)}, bf16[128,2048]{1,0:T(8,128)(2,1)S(1)}, u32[]{:S(2)}, u32[]{:S(2)}) collective-permute-start(bf16[128,2048]{1,0:T(8,128)(2,1)} %get-tuple-element.92), channel_id=1, source_target_pairs={{0,8},{8,0},{1,9},{9,1},{2,10},{10,2},{3,11},{11,3},{4,12},{12,4},... | collective-permute-start | bytes 1572872 | tf_op jit(solution)/shard_map/ppermute | solution.py:665
  295.6 0.9 copy-start.2
  298.6 16.1 %all-to-all-start.8 = ((bf16[8,384,128]{2,1,0:T(8,128)(2,1)}), bf16[8,384,128]{2,1,0:T(8,128)(2,1)S(1)}, u32[]{:S(2)}, u32[]{:S(2)}) async-start(bf16[8,384,128]{2,1,0:T(8,128)(2,1)} %shard_map.187), calls=%async_computation.8 | async-start | bytes 1572864 | tf_op jit(solution)/shard_map/all_to_all | solution.py:235
  302.2 22.7 %collective-permute-start.16 = (bf16[128,2048]{1,0:T(8,128)(2,1)}, bf16[128,2048]{1,0:T(8,128)(2,1)S(1)}, u32[]{:S(2)}, u32[]{:S(2)}) collective-permute-start(bf16[128,2048]{1,0:T(8,128)(2,1)} %get-tuple-element.91), channel_id=1, source_target_pairs={{0,8},{8,0},{1,9},{9,1},{2,10},{10,2},{3,11},{11,3},{4,12},{12,4},... | collective-permute-start | bytes 1572872 | tf_op jit(solution)/shard_map/ppermute | solution.py:665
  302.3 0.8 copy-start.9
  304.4 26.5 %collective-permute-start.15 = (bf16[128,2048]{1,0:T(8,128)(2,1)S(1)}, bf16[128,2048]{1,0:T(8,128)(2,1)}, u32[]{:S(2)}, u32[]{:S(2)}) collective-permute-start(bf16[128,2048]{1,0:T(8,128)(2,1)S(1)} %add_convert_fusion.1), channel_id=1, source_target_pairs={{0,16},{16,0},{1,17},{17,1},{2,18},{18,2},{3,19},{19,3},{4,20},{20... | collective-permute-start | bytes 1572872 | tf_op jit(solution)/shard_map/ppermute | solution.py:665
  314.7 0.9 copy-start.3
  (1 other events, 0.6 us)
